TPU v7x, 512 devices: a whole 4x4x16 slice. The times are simulated.
512 devices in a mesh: row: 32 (over z, core), col: 16 (over x, y).
Axes of the slice: x: 4, y: 4, z: 16, core: 2. Of those that a mesh axis runs over, the one named last changes fastest.
Arguments:
- records: float32 [9, 4096], P(None, 'row'), may hold values from -0.3 to 703, as said below
- pattern: int32 [32, 32], replicated, may hold values from 0 to 1, as said below
- iterate: float32 [4096, 4096], P('row', 'col'), may hold values from -0.5 to 0.5, as said below
Outputs:
- margin: float32 [4096, 4096], P('row', 'col')
- updated: float32 [4096, 4096], P('row', 'col')
Inputs may be any that keep to these rules, and one draw needn't show every extreme that they name: `pattern`: symmetric 0 or 1 entries; the diagonal and the first off-diagonals are 1. `records`: exponents and coefficients are positive. `iterate`: symmetric.
All inputs are finite; a program needn't handle non-finite values.
Results may differ from a plain program's by a relative error of at most 0.0003.
Values sent between devices are 32-bit elements; how exact they have to be, the bound alone decides.
No kernel may reach another device: no remote copies, remote signals or barrier semaphores. Data moves between devices by JAX's collectives and lax.ppermute only.
A program may use at most 64 MiB of HBM per device.

v0:
```python
import jax
import jax.numpy as jnp
from jax import lax
from jax.sharding import PartitionSpec as P

BLOCK = 128
PRIMS = 3


def expand(blocks, size):
    row_blocks, col_blocks = blocks.shape
    grown = jnp.broadcast_to(blocks[:, None, :, None], (row_blocks, size, col_blocks, size))
    return grown.reshape(row_blocks * size, col_blocks * size).astype(jnp.float32)


def pair_margin(left, right):
    distance = (left[0][:, None] - right[0][None, :]) ** 2
    distance = distance + (left[1][:, None] - right[1][None, :]) ** 2
    distance = distance + (left[2][:, None] - right[2][None, :]) ** 2
    accumulated = jnp.zeros(distance.shape, jnp.float32)
    for p in range(PRIMS):
        for q in range(PRIMS):
            exponent_a = left[3 + p][:, None]
            exponent_b = right[3 + q][None, :]
            summed = exponent_a + exponent_b
            prefactor = (2.0 * jnp.sqrt(exponent_a * exponent_b) / summed) ** 1.5
            weight_ab = left[3 + PRIMS + p][:, None] * right[3 + PRIMS + q][None, :]
            accumulated = accumulated + weight_ab * prefactor * jnp.exp(
                -(exponent_a * exponent_b / summed) * distance
            )
    return accumulated


def self_norm(recs):
    accumulated = jnp.zeros(recs.shape[1], jnp.float32)
    for p in range(PRIMS):
        for q in range(PRIMS):
            exponent_a = recs[3 + p]
            exponent_b = recs[3 + q]
            prefactor = (2.0 * jnp.sqrt(exponent_a * exponent_b) / (exponent_a + exponent_b)) ** 1.5
            accumulated = accumulated + recs[3 + PRIMS + p] * recs[3 + PRIMS + q] * prefactor
    return accumulated


def matmul(left, right):
    return jnp.dot(left, right, precision=lax.Precision.HIGHEST, preferred_element_type=jnp.float32)


def accumulate(left, piece):
    return matmul(left, piece)


def body(records, pattern, iterate):
    row_idx = lax.axis_index("row")
    col_idx = lax.axis_index("col")
    row_count, col_count = iterate.shape
    row_blocks = row_count // BLOCK
    col_blocks = col_count // BLOCK
    everyone = lax.all_gather(records, "row", axis=1, tiled=True)
    col_records = lax.dynamic_slice_in_dim(everyone, col_idx * col_count, col_count, 1)
    row_norms = self_norm(records)
    col_norms = self_norm(col_records)
    tile_blocks = lax.dynamic_slice(
        pattern, (row_idx * row_blocks, col_idx * col_blocks), (row_blocks, col_blocks)
    )
    tile_mask = expand(tile_blocks, BLOCK)
    margin = tile_mask * (
        pair_margin(records, col_records) / jnp.sqrt(row_norms[:, None] * col_norms[None, :])
    )
    masked = tile_mask * iterate
    margin_row = lax.all_gather(margin, "col", axis=1, tiled=True)
    iterate_row = lax.all_gather(masked, "col", axis=1, tiled=True)
    iterate_col = lax.all_gather(masked, "row", axis=0, tiled=True)
    product_one = tile_mask * matmul(margin_row, iterate_col)
    product_two = tile_mask * accumulate(
        iterate_row, lax.all_gather(product_one, "row", axis=0, tiled=True)
    )
    second_row = lax.all_gather(product_two, "col", axis=1, tiled=True)
    product_three = matmul(second_row, iterate_col)
    updated = tile_mask * (1.5 * masked - 0.5 * product_three)
    return (margin, updated)


def solution(mesh):
    in_specs = (P(None, "row"), P(), P("row", "col"))
    out_specs = (P("row", "col"), P("row", "col"))
    return jax.shard_map(body, mesh=mesh, in_specs=in_specs, out_specs=out_specs, check_vma=False)
```

profile of v0, /device:TPU:1, one launch (start us, length us, event | category | flops | bytes accessed | tf_op | source)
XLA Modules:
  0.0 397.5 jit_solution(15753159277731944957)
XLA Ops:
  7.2 0.0 copy-start
  7.2 0.0 all-gather.8.cloned.1.call-start
  7.2 0.9 multiply_add_fusion.1
  8.1 1.0 slice_bitcast_fusion.8
  9.1 38.5 %all_gather.18 = f32[9,4096]{1,0:T(8,128)S(1)} all-gather(f32[9,128]{1,0:T(8,128)} %param.3), channel_id=1, replica_groups=mesh['row'=32,'col'=16] {'row'}, dimensions={1}, use_global_device_ids=true | all-gather | bytes 152064 | tf_op jit(solution)/shard_map/all_gather | solution.py:59
  47.6 0.8 convert_bitcast_fusion
  48.4 0.1 broadcast_bitcast_fusion
  48.5 0.1 constant_dynamic-slice_fusion
  48.6 2.1 fusion.74
  50.8 0.0 all-gather.8.cloned.1.call-update
  50.8 0.0 all-gather.10.cloned.1.call-start
  50.8 0.0 copy-done
  50.8 0.7 broadcast_multiply_fusion
  51.5 0.0 all-gather.10.cloned.1.call-update
  51.5 0.0 all-gather.6.cloned.1.call-start
  51.6 0.7 all-gather.6.cloned.1.call-update
  52.3 0.0 all-gather.12.cloned.1.call-start
  52.3 55.1 %all-gather.8.cloned.1.call-done = f32[128,4096]{1,0:T(8,128)} async-done(((f32[128,256]{1,0:T(8,128)}), f32[128,4096]{1,0:T(8,128)}) %all-gather.8.cloned.1.call-update) | async-done | bytes 2097168 | tf_op jit(solution)/shard_map/all_gather | solution.py:71
  107.4 77.3 %all-gather.10.cloned.1.call-done = f32[4096,256]{1,0:T(8,128)} async-done(((f32[128,256]{1,0:T(8,128)}), f32[4096,256]{1,0:T(8,128)}) %all-gather.10.cloned.1.call-update) | async-done | bytes 4194320 | tf_op jit(solution)/shard_map/all_gather | solution.py:73
  184.7 5.6 %convolution_multiply_fusion.2 = f32[128,256]{1,0:T(8,128)} fusion(f32[128,4096]{1,0:T(8,128)} %all-gather.8.cloned.1.call-done, f32[4096,256]{1,0:T(8,128)} %all-gather.10.cloned.1.call-done, f32[256]{0:T(256)S(1)} %broadcast_bitcast_fusion), kind=kOutput, calls=%fused_computation.4 | convolution fusion | flops 1610645504 | bytes 6423552 | tf_op jit(solution)/shard_map/dot_general | solution.py:46
  190.3 0.0 all-gather.12.cloned.1.call-update
  190.3 0.0 all-gather.14.cloned.1.call-start
  190.3 55.3 %all-gather.6.cloned.1.call-done = f32[128,4096]{1,0:T(8,128)} async-done(((f32[128,256]{1,0:T(8,128)}), f32[128,4096]{1,0:T(8,128)}) %all-gather.6.cloned.1.call-update) | async-done | bytes 2097168 | tf_op jit(solution)/shard_map/all_gather | solution.py:72
  245.7 76.6 %all-gather.12.cloned.1.call-done = f32[4096,256]{1,0:T(8,128)} async-done(((f32[128,256]{1,0:T(8,128)}), f32[4096,256]{1,0:T(8,128)}) %all-gather.12.cloned.1.call-update) | async-done | bytes 4194320 | tf_op jit(solution)/shard_map/all_gather | solution.py:76
  322.3 5.6 %convolution_multiply_fusion.1 = f32[128,256]{1,0:T(8,128)} fusion(f32[128,4096]{1,0:T(8,128)} %all-gather.6.cloned.1.call-done, f32[4096,256]{1,0:T(8,128)} %all-gather.12.cloned.1.call-done, f32[256]{0:T(256)S(1)} %broadcast_bitcast_fusion), kind=kOutput, calls=%fused_computation.3 | convolution fusion | flops 1610645504 | bytes 6423552 | tf_op jit(solution)/shard_map/dot_general | solution.py:46
  327.8 0.0 all-gather.14.cloned.1.call-update
  327.9 57.5 %all-gather.14.cloned.1.call-done = f32[128,4096]{1,0:T(8,128)} async-done(((f32[128,256]{1,0:T(8,128)}), f32[128,4096]{1,0:T(8,128)}) %all-gather.14.cloned.1.call-update) | async-done | bytes 2097168 | tf_op jit(solution)/shard_map/all_gather | solution.py:78
  385.4 5.6 %fusion.1 = f32[128,256]{1,0:T(8,128)} fusion(f32[128,4096]{1,0:T(8,128)} %all-gather.14.cloned.1.call-done, f32[4096,256]{1,0:T(8,128)} %all-gather.10.cloned.1.call-done, f32[256]{0:T(256)S(1)} %broadcast_bitcast_fusion, f32[128,256]{1,0:T(8,128)S(1)} %copy-done), kind=kOutput, calls=%fused_computation.2 | convolution fusion | flops 1610776576 | bytes 6554624 | tf_op jit(solution)/shard_map/dot_general | solution.py:46
Async XLA Ops:
  7.2 43.7 %copy-start = (f32[128,256]{1,0:T(8,128)S(1)}, f32[128,256]{1,0:T(8,128)}, u32[]{:S(2)}) copy-start(f32[128,256]{1,0:T(8,128)} %param.5) | copy-start | bytes 393220
  7.2 100.2 %all-gather.8.cloned.1.call-start = ((), (), s32[]{:S(2)}) async-start(), calls=%async_computation.1 | async-start | bytes 2228224 | tf_op jit(solution)/shard_map/all_gather | solution.py:71
  50.8 133.9 %all-gather.10.cloned.1.call-start = ((), (), s32[]{:S(2)}) async-start(), calls=%async_computation.2 | async-start | bytes 4325376 | tf_op jit(solution)/shard_map/all_gather | solution.py:73
  51.5 194.1 %all-gather.6.cloned.1.call-start = ((), (), s32[]{:S(2)}) async-start(), calls=%async_computation | async-start | bytes 2228224 | tf_op jit(solution)/shard_map/all_gather | solution.py:72
  52.3 270.0 %all-gather.12.cloned.1.call-start = ((), (), s32[]{:S(2)}) async-start(), calls=%async_computation.3 | async-start | bytes 4325376 | tf_op jit(solution)/shard_map/all_gather | solution.py:76
  190.3 195.1 %all-gather.14.cloned.1.call-start = ((), (), s32[]{:S(2)}) async-start(), calls=%async_computation.4 | async-start | bytes 2228224 | tf_op jit(solution)/shard_map/all_gather | solution.py:78
Sparse Core Ops, SparseCore 0:
  50.9 56.4 all-gather.7
  110.1 74.5 all-gather.9
  188.2 57.3 all-gather.5
  247.6 74.5 all-gather.11
  328.0 57.3 all-gather.13
where the time goes:
time: 398 us
  waiting for transfers between devices  323 us (81%)
  blocking collectives  38.5 us (10%)
  matrix products  16.7 us (4%)
  between operations  13.8 us (3%)
  other arithmetic  4.61 us (1%)
    all_gather x1, waiting for transfers between devices, body(): iterate_col = lax.all_gather(masked, 'row', axis=0, tiled=True)  77.3 us
    all_gather x1, waiting for transfers between devices, body(): lax.all_gather(product_one, 'row', axis=0, tiled=True)  76.6 us
    all_gather x1, waiting for transfers between devices, body(): second_row = lax.all_gather(product_two, 'col', axis=1, tiled=True)  57.5 us
    all_gather x1, waiting for transfers between devices, body(): iterate_row = lax.all_gather(masked, 'col', axis=1, tiled=True)  55.3 us
    all_gather x1, waiting for transfers between devices, body(): margin_row = lax.all_gather(margin, 'col', axis=1, tiled=True)  55.1 us
    all_gather x1, blocking collectives, body(): everyone = lax.all_gather(records, 'row', axis=1, tiled=True)  38.5 us
    dot_general x3, matrix products, matmul(): jnp.dot(left, right, precision=lax.Precision.HIGHEST, preferred_element_t...  16.7 us
  transfers between devices with their start and end apart: 5, of which 5 were waited for; matrix products, arithmetic and copies ran while one was open for 2% of the time, Pallas kernels for 0%

commit v1 on v0

v1 whole, which is shorter than its diff:
```python
import jax
import jax.numpy as jnp
from jax import lax
from jax.experimental import pallas as pl
from jax.experimental.pallas import tpu as pltpu
from jax.sharding import PartitionSpec as P

BLOCK = 128
PRIMS = 3
NB = 32
FIELDS = 3 + 3 * PRIMS
CHUNK = 32
VMEM = pltpu.VMEM
SMEM = pltpu.SMEM


def split(value):
    high = value.astype(jnp.bfloat16)
    low = (value - high.astype(jnp.float32)).astype(jnp.bfloat16)
    return high, low


def product(left, right, right_dim):
    left_high, left_low = split(left)
    right_high, right_low = split(right)
    dims = (((1,), (right_dim,)), ((), ()))

    def dot(a, b):
        return lax.dot_general(a, b, dims, preferred_element_type=jnp.float32)

    return dot(left_high, right_high) + (dot(left_high, right_low) + dot(left_low, right_high))


def half_tile(fields_ref, left_ref, tile_ref, half, block):
    right = [fields_ref[f, pl.ds(block, 1), :] for f in range(FIELDS)]

    def chunk(step, carry):
        rows = pl.ds(pl.multiple_of(step * CHUNK, CHUNK), CHUNK)
        left = [left_ref[half, f, rows, :] for f in range(FIELDS)]
        distance = (left[0] - right[0]) ** 2
        distance = distance + (left[1] - right[1]) ** 2
        distance = distance + (left[2] - right[2]) ** 2
        total = jnp.zeros_like(distance)
        for p in range(PRIMS):
            inner = jnp.zeros_like(distance)
            for q in range(PRIMS):
                inverse_root = lax.rsqrt(left[3 + p] + right[3 + q])
                root_rate = (left[6 + p] * inverse_root) * right[6 + q]
                ratio = jnp.maximum(root_rate * inverse_root, 1e-37)
                decay = jnp.exp(-(root_rate * root_rate) * distance)
                inner = inner + right[9 + q] * ((ratio * ratio * lax.rsqrt(ratio)) * decay)
            total = total + left[9 + p] * inner
        tile_ref[rows, :] = total
        return carry

    lax.fori_loop(0, BLOCK // CHUNK, chunk, 0)


def first_kernel(place, pattern, records, iterate_row, margin, product_one, fields, left, tile, acc):
    row, col = place[0], place[1]
    exponents = [records[:, 3 + p, :] for p in range(PRIMS)]
    coefficients = [records[:, 3 + PRIMS + p, :] for p in range(PRIMS)]
    roots = [jnp.sqrt(e) for e in exponents]
    norm = jnp.zeros_like(exponents[0])
    for p in range(PRIMS):
        for q in range(PRIMS):
            ratio = 2.0 * roots[p] * roots[q] / (exponents[p] + exponents[q])
            norm = norm + coefficients[p] * coefficients[q] * (ratio * jnp.sqrt(ratio))
    scale = (2.0**0.75) * lax.rsqrt(norm)
    for f in range(3):
        fields[f] = records[:, f, :]
    for p in range(PRIMS):
        fields[3 + p] = exponents[p]
        fields[6 + p] = roots[p]
        fields[9 + p] = coefficients[p] * scale
    for half in range(2):
        for f in range(FIELDS):
            own = jnp.broadcast_to(fields[f, pl.ds(2 * col + half, 1), :], (BLOCK, BLOCK))
            left[half, f] = own.T
        margin_live = pattern[row, 2 * col + half] != 0
        lanes = slice(half * BLOCK, (half + 1) * BLOCK)

        @pl.when(margin_live)
        def _():
            half_tile(fields, left, tile, half, row)
            margin[:, lanes] = tile[...].T

        @pl.when(jnp.logical_not(margin_live))
        def _():
            margin[:, lanes] = jnp.zeros((BLOCK, BLOCK), jnp.float32)

    acc[...] = jnp.zeros_like(acc)

    def step(index, carry):
        half, block = index // NB, index % NB
        own = 2 * col + half
        live = pattern[own, block] * pattern[block, row] * pattern[row, own]

        @pl.when(live != 0)
        def _():
            half_tile(fields, left, tile, half, block)
            lanes = pl.ds(pl.multiple_of((block % 2) * BLOCK, BLOCK), BLOCK)
            acc[half] += product(iterate_row[block // 2, :, lanes], tile[...], 1)

        return carry

    lax.fori_loop(0, 2 * NB, step, 0)
    product_one[:, :BLOCK] = acc[0]
    product_one[:, BLOCK:] = acc[1]


def second_kernel(place, pattern, one_row, iterate_col, slices, acc):
    row, col = place[0], place[1]
    acc[...] = jnp.zeros_like(acc)

    def step(index, carry):
        half, block = index // NB, index % NB
        own = 2 * col + half
        live = pattern[row, block] * pattern[block, own] * pattern[row, own]

        @pl.when(live != 0)
        def _():
            lanes = pl.ds(pl.multiple_of((block % 2) * BLOCK, BLOCK), BLOCK)
            rows = pl.ds(pl.multiple_of(block * BLOCK, BLOCK), BLOCK)
            own_lanes = pl.ds(pl.multiple_of(half * BLOCK, BLOCK), BLOCK)
            acc[half] += product(one_row[block // 2, :, lanes], iterate_col[rows, own_lanes], 0)

        return carry

    lax.fori_loop(0, 2 * NB, step, 0)
    for half in range(2):
        slices[:, half] = acc[half].T.reshape(BLOCK // 8, 8, BLOCK)


def third_kernel(place, pattern, two_row, iterate_col, iterate, updated, acc):
    row, col = place[0], place[1]
    acc[...] = jnp.zeros_like(acc)

    def step(index, carry):
        half, block = index // NB, index % NB
        own = 2 * col + half
        live = pattern[row, block] * pattern[block, own] * pattern[row, own]

        @pl.when(live != 0)
        def _():
            rows = pl.ds(pl.multiple_of(block * BLOCK, BLOCK), BLOCK)
            own_lanes = pl.ds(pl.multiple_of(half * BLOCK, BLOCK), BLOCK)
            piece = two_row[:, block].reshape(BLOCK, BLOCK)
            acc[half] += product(piece, iterate_col[rows, own_lanes], 0)

        return carry

    lax.fori_loop(0, 2 * NB, step, 0)
    for half in range(2):
        lanes = slice(half * BLOCK, (half + 1) * BLOCK)
        mask = (pattern[row, 2 * col + half] != 0).astype(jnp.float32)
        updated[:, lanes] = mask * (1.5 * iterate[:, lanes] - 0.5 * acc[half])


def spread(value, axis, count):
    return lax.all_to_all(jnp.broadcast_to(value[None], (count,) + value.shape), axis, 0, 0, tiled=True)


def call(kernel, out_shapes, scratch, *operands):
    whole = pl.BlockSpec(memory_space=VMEM)
    scalars = pl.BlockSpec(memory_space=SMEM)
    return pl.pallas_call(
        kernel,
        out_shape=out_shapes,
        in_specs=[scalars, scalars] + [whole] * (len(operands) - 2),
        out_specs=jax.tree.map(lambda _: whole, out_shapes),
        scratch_shapes=scratch,
    )(*operands)


def body(records, pattern, iterate):
    place = jnp.stack([lax.axis_index("row"), lax.axis_index("col")]).astype(jnp.int32)
    tile = jax.ShapeDtypeStruct((BLOCK, 2 * BLOCK), jnp.float32)
    acc = VMEM((2, BLOCK, BLOCK), jnp.float32)
    iterate_col = lax.all_gather(iterate, "row", axis=0, tiled=True)
    everyone = spread(records, "row", 32)
    iterate_row = spread(iterate, "col", 16)
    margin, product_one = call(
        first_kernel,
        (tile, tile),
        [
            VMEM((FIELDS, NB, BLOCK), jnp.float32),
            VMEM((2, FIELDS, BLOCK, BLOCK), jnp.float32),
            VMEM((BLOCK, BLOCK), jnp.float32),
            acc,
        ],
        place,
        pattern,
        everyone,
        iterate_row,
    )
    one_row = spread(product_one, "col", 16)
    slices = call(
        second_kernel,
        jax.ShapeDtypeStruct((16, 2, 8, BLOCK), jnp.float32),
        [acc],
        place,
        pattern,
        one_row,
        iterate_col,
    )
    slices = lax.all_to_all(slices, "col", 0, 0, tiled=True).reshape(NB, 8, BLOCK)
    slices = lax.all_to_all(slices, "row", 0, 0, tiled=True)
    two_row = spread(slices, "col", 16)
    updated = call(third_kernel, tile, [acc], place, pattern, two_row, iterate_col, iterate)
    return (margin, updated)


def solution(mesh):
    in_specs = (P(None, "row"), P(), P("row", "col"))
    out_specs = (P("row", "col"), P("row", "col"))
    return jax.shard_map(body, mesh=mesh, in_specs=in_specs, out_specs=out_specs, check_vma=False)
```

time: 398 us -> 228 us (0.57)
  waiting for transfers between devices: 323 us -> 27.4 us
  blocking collectives: 38.5 us -> 139 us
  Pallas kernels: 0 us -> 37.1 us
  matrix products: 16.7 us -> 0 us
  starting transfers between devices: 0.2 us -> 6.78 us
  local copies, waits for them, and re-layouts: 1.06 us -> 5.75 us
    all_gather x5 -> x1, waiting for transfers between devices: 322 us -> 0.01 us  [body(): iterate_col = lax.all_gather(iterate, 'row', axis=0, tiled=True)]
    all_to_all x0 -> x5, blocking collectives: none -> 139 us  [the longest x3 96.5 us: spread(): lax.all_to_all(jnp.broadcast_to(value[None], (count,) + value.shape), axi...]
    all_gather x1 -> x0, blocking collectives: 38.5 us -> none  [body(): everyone = lax.all_gather(records, 'row', axis=1, tiled=True)]
    pallas_call x0 -> x3, Pallas kernels: none -> 37.1 us  [call(): pl.pallas_call(kernel, out_shape=out_shapes, in_specs=[scalars, scalars]...]
    all_to_all x0 -> x1, waiting for transfers between devices: none -> 26.7 us  [spread(): lax.all_to_all(jnp.broadcast_to(value[None], (count,) + value.shape), axi...]
    dot_general x3 -> x0, matrix products: 16.7 us -> none  [matmul(): jnp.dot(left, right, precision=lax.Precision.HIGHEST, preferred_element_t...]
    all_to_all x0 -> x1, starting transfers between devices: none -> 6.74 us  [spread(): lax.all_to_all(jnp.broadcast_to(value[None], (count,) + value.shape), axi...]
    broadcast_in_dim x0 -> x4, local copies, waits for them, and re-layouts: none -> 4.44 us  [spread(): jnp.broadcast_to(value[None], (count,) + value.shape)]
  transfers between devices with their start and end apart: 5 -> 2, of which waited for: 5 -> 1; matrix products, arithmetic and copies ran while one was open for 2% -> 2% of each run, Pallas kernels for 0% -> 9%
where the time goes in v1:
time: 228 us; the launch traced here: 230 us
  blocking collectives  139 us (61%)
  Pallas kernels  37.1 us (16%)
  waiting for transfers between devices  27.4 us (12%)
  between operations  14.1 us (6%)
  starting transfers between devices  6.78 us (3%)
  local copies, waits for them, and re-layouts  5.75 us (3%)
    all_to_all x3, blocking collectives, spread(): lax.all_to_all(jnp.broadcast_to(value[None], (count,) + value.shape), axi...  96.5 us
    pallas_call x3, Pallas kernels, call(): pl.pallas_call(kernel, out_shape=out_shapes, in_specs=[scalars, scalars]...  37.1 us
    all_to_all x1, blocking collectives, body(): slices = lax.all_to_all(slices, 'row', 0, 0, tiled=True)  32.2 us
    all_to_all x1, waiting for transfers between devices, spread(): lax.all_to_all(jnp.broadcast_to(value[None], (count,) + value.shape), axi...  26.7 us
    all_to_all x1, blocking collectives, body(): lax.all_to_all(slices, 'col', 0, 0, tiled=True).reshape(NB, 8, BLOCK)  10.1 us
    all_to_all x1, starting transfers between devices, spread(): lax.all_to_all(jnp.broadcast_to(value[None], (count,) + value.shape), axi...  6.74 us
  transfers between devices with their start and end apart: 2, of which 1 were waited for; matrix products, arithmetic and copies ran while one was open for 2% of the time, Pallas kernels for 9%

profile of v1, /device:TPU:1, one launch (start us, length us, event | category | flops | bytes accessed | tf_op | source)
XLA Modules:
  0.0 230.5 jit_solution(3586008972002340954)
XLA Ops:
  7.2 0.0 all-gather.2.cloned.1.call-start
  7.2 0.7 all-gather.2.cloned.1.call-update
  7.9 0.7 broadcast_in_dim.8
  8.6 39.5 %all_to_all.30.records = f32[32,9,128]{2,1,0:T(8,128)} all-to-all(f32[32,9,128]{2,1,0:T(8,128)S(1)} %broadcast_in_dim.8), channel_id=1, replica_groups=mesh['row'=32,'col'=16] {'row'}, dimensions={0} | all-to-all | bytes 294912 | tf_op jit(solution)/shard_map/all_to_all | solution.py:161
  48.1 2.4 %broadcast_in_dim.9 = f32[16,128,256]{2,1,0:T(8,128)} broadcast(f32[128,256]{1,0:T(8,128)} %iterate.1), dimensions={1,2} | broadcast | bytes 2228224 | tf_op jit(solution)/shard_map/broadcast_in_dim | solution.py:161
  50.5 6.7 %all-to-all-start.1 = ((f32[16,128,256]{2,1,0:T(8,128)}), f32[16,128,256]{2,1,0:T(8,128)S(1)}, u32[]{:S(2)}, u32[]{:S(2)}) async-start(f32[16,128,256]{2,1,0:T(8,128)} %broadcast_in_dim.9), calls=%async_computation.1 | async-start | bytes 4194304 | tf_op jit(solution)/shard_map/all_to_all | solution.py:161
  57.3 0.7 pad_add_fusion.place
  57.9 26.7 %all-to-all-done.1.iterate_row = f32[16,128,256]{2,1,0:T(8,128)S(1)} async-done(((f32[16,128,256]{2,1,0:T(8,128)}), f32[16,128,256]{2,1,0:T(8,128)S(1)}, u32[]{:S(2)}, u32[]{:S(2)}) %all-to-all-start.1) | async-done | bytes 2097184 | tf_op jit(solution)/shard_map/all_to_all | solution.py:161
  84.6 0.0 copy-start
  84.6 1.3 copy-done
  85.9 19.7 %shard_map.50 = (f32[128,256]{1,0:T(8,128)}, f32[128,256]{1,0:T(8,128)}) custom-call(s32[2]{0:T(128)} %pad_add_fusion.place, s32[32,32]{1,0:T(8,128)} %pattern.5, f32[32,9,128]{2,1,0:T(8,128)} %all_to_all.30.records, f32[16,128,256]{2,1,0:T(8,128)} %copy-done), custom_call_target="tpu_custom_call" | custom-call | tf_op jit(solution)/shard_map/pallas_call | solution.py:167
  105.6 1.1 broadcast_in_dim.10
  106.7 27.6 %all_to_all.31.one_row = f32[16,128,256]{2,1,0:T(8,128)} all-to-all(f32[16,128,256]{2,1,0:T(8,128)S(1)} %broadcast_in_dim.10), channel_id=1, replica_groups=mesh['row'=32,'col'=16] {'col'}, dimensions={0} | all-to-all | bytes 4194304 | tf_op jit(solution)/shard_map/all_to_all | solution.py:161
  134.3 0.0 all-gather.2.cloned.1.call-done.iterate_col
  134.3 8.7 %shard_map.51 = f32[16,2,8,128]{3,2,1,0:T(8,128)} custom-call(s32[2]{0:T(128)} %pad_add_fusion.place, s32[32,32]{1,0:T(8,128)} %pattern.5, f32[16,128,256]{2,1,0:T(8,128)} %all_to_all.31.one_row, f32[4096,256]{1,0:T(8,128)} %all-gather.2.cloned.1.call-done.iterate_col), custom_call_target="tpu_custom_call" | custom-call | tf_op jit(solution)/shard_map/pallas_call | solution.py:167
  143.1 10.1 %all_to_all.32 = f32[16,2,8,128]{3,2,1,0:T(8,128)S(1)} all-to-all(f32[16,2,8,128]{3,2,1,0:T(8,128)} %shard_map.51), channel_id=1, replica_groups=mesh['row'=32,'col'=16] {'col'}, dimensions={0} | all-to-all | bytes 262144 | tf_op jit(solution)/shard_map/all_to_all | solution.py:207
  153.2 32.2 %all_to_all.33 = f32[32,8,128]{2,1,0:T(8,128)S(1)} all-to-all(f32[32,8,128]{2,1,0:T(8,128)S(1)} %bitcast.3), channel_id=1, replica_groups=mesh['row'=32,'col'=16] {'row'}, dimensions={0} | all-to-all | bytes 262144 | tf_op jit(solution)/shard_map/all_to_all | solution.py:208
  185.3 0.2 broadcast_in_dim.11
  185.5 29.4 %all_to_all.34.two_row = f32[16,32,8,128]{3,2,1,0:T(8,128)} all-to-all(f32[16,32,8,128]{3,2,1,0:T(8,128)S(1)} %broadcast_in_dim.11), channel_id=1, replica_groups=mesh['row'=32,'col'=16] {'col'}, dimensions={0} | all-to-all | bytes 4194304 | tf_op jit(solution)/shard_map/all_to_all | solution.py:161
  215.0 8.7 %shard_map.52 = f32[128,256]{1,0:T(8,128)} custom-call(s32[2]{0:T(128)} %pad_add_fusion.place, s32[32,32]{1,0:T(8,128)} %pattern.5, f32[16,32,8,128]{3,2,1,0:T(8,128)} %all_to_all.34.two_row, f32[4096,256]{1,0:T(8,128)} %all-gather.2.cloned.1.call-done.iterate_col, f32[128,256]{1,0:T(8,128)} %iterate.1), custom_call_target="tpu_custom_call" | custom-call | tf_op jit(solution)/shard_map/pallas_call | solution.py:167
Async XLA Ops:
  7.2 127.2 %all-gather.2.cloned.1.call-start = ((), (), s32[]{:S(2)}) async-start(), calls=%async_computation.6 | async-start | bytes 4325376 | tf_op jit(solution)/shard_map/all_gather | solution.py:180
  50.5 34.1 %all-to-all-start.1 = ((f32[16,128,256]{2,1,0:T(8,128)}), f32[16,128,256]{2,1,0:T(8,128)S(1)}, u32[]{:S(2)}, u32[]{:S(2)}) async-start(f32[16,128,256]{2,1,0:T(8,128)} %broadcast_in_dim.9), calls=%async_computation.1 | async-start | bytes 4194304 | tf_op jit(solution)/shard_map/all_to_all | solution.py:161
  84.6 1.3 copy-start
Sparse Core Ops, SparseCore 0:
  10.1 82.7 all-gather.1

commit v2 on v1

v2 whole, which is shorter than its diff:
```python
import jax
import jax.numpy as jnp
from jax import lax
from jax.experimental import pallas as pl
from jax.experimental.pallas import tpu as pltpu
from jax.sharding import PartitionSpec as P


BLOCK = 128
PRIMS = 3
NB = 32
FIELDS = 3 + 3 * PRIMS
CHUNK = 32
LOG2E = 1.4426950408889634
VMEM = pltpu.VMEM
SMEM = pltpu.SMEM


def split(value):
    high = value.astype(jnp.bfloat16)
    low = (value - high.astype(jnp.float32)).astype(jnp.bfloat16)
    return high, low


def product(left, right, right_dim):
    left_high, left_low = split(left)
    right_high, right_low = split(right)
    dims = (((1,), (right_dim,)), ((), ()))

    def dot(a, b):
        return lax.dot_general(a, b, dims, preferred_element_type=jnp.float32)

    return dot(left_high, right_high) + (dot(left_high, right_low) + dot(left_low, right_high))


def half_tile(fields_ref, left_ref, tile_ref, half, block):
    right = [fields_ref[f, pl.ds(block, 1), :] for f in range(FIELDS)]

    def chunk(step, carry):
        rows = pl.ds(pl.multiple_of(step * CHUNK, CHUNK), CHUNK)
        left = [left_ref[half, f, rows, :] for f in range(FIELDS)]
        distance = (left[0] - right[0]) ** 2
        distance = distance + (left[1] - right[1]) ** 2
        distance = (distance + (left[2] - right[2]) ** 2) * -LOG2E
        total = jnp.zeros_like(distance)
        for p in range(PRIMS):
            inner = jnp.zeros_like(distance)
            for q in range(PRIMS):
                summed = left[3 + p] + right[3 + q]
                root = (left[6 + p] * lax.rsqrt(summed)) * right[6 + q]
                ratio = root * root
                decay = jnp.exp2(((ratio * summed) * ratio) * distance)
                inner = inner + right[9 + q] * ((ratio * root) * decay)
            total = total + left[9 + p] * inner
        tile_ref[rows, :] = total
        return carry

    lax.fori_loop(0, BLOCK // CHUNK, chunk, 0)


def spread_own(fields, left, col):
    for half in range(2):
        for f in range(FIELDS):
            own = jnp.broadcast_to(fields[f, pl.ds(2 * col + half, 1), :], (BLOCK, BLOCK))
            left[half, f] = own.T


def margin_kernel(place, pattern, records, fields, margin, left, tile):
    row, col = place[0], place[1]
    exponents = [records[:, 3 + p, :] for p in range(PRIMS)]
    coefficients = [records[:, 3 + PRIMS + p, :] for p in range(PRIMS)]
    roots = [jnp.sqrt(e) for e in exponents]
    norm = jnp.zeros_like(exponents[0])
    for p in range(PRIMS):
        for q in range(PRIMS):
            ratio = 2.0 * roots[p] * roots[q] / (exponents[p] + exponents[q])
            norm = norm + coefficients[p] * coefficients[q] * (ratio * jnp.sqrt(ratio))
    scale = (2.0**0.75) * lax.rsqrt(norm)
    for f in range(3):
        fields[f] = records[:, f, :]
    for p in range(PRIMS):
        fields[3 + p] = exponents[p]
        fields[6 + p] = jnp.sqrt(roots[p])
        fields[9 + p] = coefficients[p] * scale
    spread_own(fields, left, col)
    for half in range(2):
        margin_live = pattern[row, 2 * col + half] != 0
        lanes = slice(half * BLOCK, (half + 1) * BLOCK)

        @pl.when(margin_live)
        def _():
            half_tile(fields, left, tile, half, row)
            margin[:, lanes] = tile[...].T

        @pl.when(jnp.logical_not(margin_live))
        def _():
            margin[:, lanes] = jnp.zeros((BLOCK, BLOCK), jnp.float32)


def first_kernel(place, pattern, fields, iterate_row, product_one, left, tile, acc):
    row, col = place[0], place[1]
    spread_own(fields, left, col)
    acc[...] = jnp.zeros_like(acc)

    def step(index, carry):
        half, block = index // NB, index % NB
        own = 2 * col + half
        needed = pattern[own, block] * pattern[block, row] * pattern[row, own]

        @pl.when(needed != 0)
        def _():
            half_tile(fields, left, tile, half, block)
            lanes = pl.ds(pl.multiple_of((block % 2) * BLOCK, BLOCK), BLOCK)
            acc[half] += product(iterate_row[block // 2, :, lanes], tile[...], 1)

        return carry

    lax.fori_loop(0, 2 * NB, step, 0)
    product_one[:, :BLOCK] = acc[0]
    product_one[:, BLOCK:] = acc[1]


def prepare_kernel(place, pattern, iterate_col, high, low):
    col = place[1]

    def step(block, carry):
        rows = pl.ds(pl.multiple_of(block * BLOCK, BLOCK), BLOCK)
        for half in range(2):
            lanes = slice(half * BLOCK, (half + 1) * BLOCK)
            mask = (pattern[block, 2 * col + half] != 0).astype(jnp.float32)
            high[rows, lanes], low[rows, lanes] = split(mask * iterate_col[rows, lanes])
        return carry

    lax.fori_loop(0, NB, step, 0)


def contract(pieces, high, low):
    total = jnp.zeros((BLOCK, 2 * BLOCK), jnp.float32)
    for k, piece in enumerate(pieces):
        rows = slice(2 * BLOCK * k, 2 * BLOCK * (k + 1))
        piece_high, piece_low = split(piece)
        total = total + jnp.dot(piece_high, high[rows], preferred_element_type=jnp.float32)
        total = total + jnp.dot(piece_high, low[rows], preferred_element_type=jnp.float32)
        total = total + jnp.dot(piece_low, high[rows], preferred_element_type=jnp.float32)
    return total


def live(pattern, row, column):
    return (pattern[row, column] != 0).astype(jnp.float32)


def second_kernel(place, pattern, one_row, high, low, slices):
    row, col = place[0], place[1]
    total = contract([one_row[k] for k in range(16)], high, low)
    for half in range(2):
        own = total[:, half * BLOCK : (half + 1) * BLOCK]
        own = (live(pattern, row, 2 * col + half) * own).T
        slices[:, half] = own.reshape(BLOCK // 8, 8, BLOCK)


def third_kernel(place, pattern, two_row, high, low, iterate, updated):
    row, col = place[0], place[1]
    pieces = []
    for k in range(16):
        pair = [two_row[:, 2 * k + h].reshape(BLOCK, BLOCK) for h in range(2)]
        pieces.append(jnp.concatenate(pair, axis=1))
    total = contract(pieces, high, low)
    for half in range(2):
        lanes = slice(half * BLOCK, (half + 1) * BLOCK)
        mask = live(pattern, row, 2 * col + half)
        updated[:, lanes] = mask * (1.5 * iterate[:, lanes] - 0.5 * total[:, lanes])


def spread(value, axis, count):
    return lax.all_to_all(jnp.broadcast_to(value[None], (count,) + value.shape), axis, 0, 0, tiled=True)


def call(kernel, out_shapes, scratch, *operands):
    whole = pl.BlockSpec(memory_space=VMEM)
    scalars = pl.BlockSpec(memory_space=SMEM)
    return pl.pallas_call(
        kernel,
        out_shape=out_shapes,
        in_specs=[scalars, scalars] + [whole] * (len(operands) - 2),
        out_specs=jax.tree.map(lambda _: whole, out_shapes),
        scratch_shapes=scratch,
    )(*operands)


def stages(records, pattern, iterate):
    place = jnp.stack([lax.axis_index("row"), lax.axis_index("col")]).astype(jnp.int32)
    tile = jax.ShapeDtypeStruct((BLOCK, 2 * BLOCK), jnp.float32)
    panel = jax.ShapeDtypeStruct((NB * BLOCK, 2 * BLOCK), jnp.bfloat16)
    iterate_col = lax.all_gather(iterate, "row", axis=0, tiled=True)
    everyone = lax.all_gather(records, "row", axis=0)
    iterate_row = spread(iterate, "col", 16)
    left = VMEM((2, FIELDS, BLOCK, BLOCK), jnp.float32)
    square = VMEM((BLOCK, BLOCK), jnp.float32)
    acc = VMEM((2, BLOCK, BLOCK), jnp.float32)
    table = jax.ShapeDtypeStruct((FIELDS, NB, BLOCK), jnp.float32)
    fields, margin = call(margin_kernel, (table, tile), [left, square], place, pattern, everyone)
    product_one = call(first_kernel, tile, [left, square, acc], place, pattern, fields, iterate_row)
    one_row = spread(product_one, "col", 16)
    high, low = call(prepare_kernel, (panel, panel), [], place, pattern, iterate_col)
    slices = jax.ShapeDtypeStruct((16, 2, 8, BLOCK), jnp.float32)
    slices = call(second_kernel, slices, [], place, pattern, one_row, high, low)
    slices = lax.all_to_all(slices, "col", 0, 0, tiled=True).reshape(NB, 8, BLOCK)
    slices = lax.all_to_all(slices, "row", 0, 0, tiled=True)
    two_row = spread(slices, "col", 16)
    updated = call(third_kernel, tile, [], place, pattern, two_row, high, low, iterate)
    return (margin, updated)


def solution(mesh):
    in_specs = (P(None, "row"), P(), P("row", "col"))
    out_specs = (P("row", "col"), P("row", "col"))
    return jax.shard_map(stages, mesh=mesh, in_specs=in_specs, out_specs=out_specs, check_vma=False)
```

time: 228 us -> 204 us (0.89); the launches traced: 230 us -> 203 us
  blocking collectives: 139 us -> 109 us
  starting transfers between devices: 6.78 us -> 12.5 us
  waiting for transfers between devices: 27.4 us -> 24.4 us
  Pallas kernels: 37.1 us -> 34.2 us
    all_to_all x3 -> x1, blocking collectives: 96.5 us -> 29.4 us  [spread(): lax.all_to_all(jnp.broadcast_to(value[None], (count,) + value.shape), axi...]
    all_gather x0 -> x1, blocking collectives: none -> 40.5 us  [stages(): everyone = lax.all_gather(records, 'row', axis=0)]
    all_to_all x1 -> x2, starting transfers between devices: 6.74 us -> 12.5 us  [spread(): lax.all_to_all(jnp.broadcast_to(value[None], (count,) + value.shape), axi...]
    all_to_all x1 -> x2, waiting for transfers between devices: 26.7 us -> 21.4 us  [spread(): lax.all_to_all(jnp.broadcast_to(value[None], (count,) + value.shape), axi...]
    all_to_all x2, blocking collectives: 42.3 us -> 39.3 us  [the longest x1 27.2 us: stages(): slices = lax.all_to_all(slices, 'row', 0, 0, tiled=True)]
    pallas_call x3 -> x5, Pallas kernels: 37.1 us -> 34.2 us  [call(): pl.pallas_call(kernel, out_shape=out_shapes, in_specs=[scalars, scalars]...]
    broadcast_in_dim x4 -> x3, local copies, waits for them, and re-layouts: 4.44 us -> 5.1 us  [spread(): jnp.broadcast_to(value[None], (count,) + value.shape)]
  transfers between devices with their start and end apart: 2 -> 3, of which waited for: 1 -> 2; matrix products, arithmetic and copies ran while one was open for 2% -> 3% of each run, Pallas kernels for 9% -> 12%
where the time goes in v2:
time: 204 us; the launch traced here: 203 us
  blocking collectives  109 us (53%)
  Pallas kernels  34.2 us (17%)
  waiting for transfers between devices  24.4 us (12%)
  between operations  14.1 us (7%)
  starting transfers between devices  12.5 us (6%)
  local copies, waits for them, and re-layouts  7.76 us (4%)
    all_gather x1, blocking collectives, stages(): everyone = lax.all_gather(records, 'row', axis=0)  40.5 us
    pallas_call x5, Pallas kernels, call(): pl.pallas_call(kernel, out_shape=out_shapes, in_specs=[scalars, scalars]...  34.2 us
    all_to_all x1, blocking collectives, spread(): lax.all_to_all(jnp.broadcast_to(value[None], (count,) + value.shape), axi...  29.4 us
    all_to_all x1, blocking collectives, stages(): slices = lax.all_to_all(slices, 'row', 0, 0, tiled=True)  27.2 us
    all_to_all x2, waiting for transfers between devices, spread(): lax.all_to_all(jnp.broadcast_to(value[None], (count,) + value.shape), axi...  21.4 us
    all_to_all x2, starting transfers between devices, spread(): lax.all_to_all(jnp.broadcast_to(value[None], (count,) + value.shape), axi...  12.5 us
    all_to_all x1, blocking collectives, stages(): lax.all_to_all(slices, 'col', 0, 0, tiled=True).reshape(NB, 8, BLOCK)  12.1 us
    broadcast_in_dim x3, local copies, waits for them, and re-layouts, spread(): jnp.broadcast_to(value[None], (count,) + value.shape)  5.1 us
  transfers between devices with their start and end apart: 3, of which 2 were waited for; matrix products, arithmetic and copies ran while one was open for 3% of the time, Pallas kernels for 12%

profile of v2, /device:TPU:1, one launch (start us, length us, event | category | flops | bytes accessed | tf_op | source)
XLA Modules:
  0.0 202.6 jit_solution(5499983646785334691)
XLA Ops:
  7.2 0.0 all-gather.4.cloned.1.call-start
  7.2 0.7 all-gather.4.cloned.1.call-update
  7.9 2.4 %broadcast_in_dim.6 = f32[16,128,256]{2,1,0:T(8,128)} broadcast(f32[128,256]{1,0:T(8,128)} %iterate.1), dimensions={1,2} | broadcast | bytes 2228224 | tf_op jit(solution)/shard_map/broadcast_in_dim | solution.py:175
  10.3 0.0 copy-start.2
  10.3 7.7 %all-to-all-start = ((f32[16,128,256]{2,1,0:T(8,128)}), f32[16,128,256]{2,1,0:T(8,128)S(1)}, u32[]{:S(2)}, u32[]{:S(2)}) async-start(f32[16,128,256]{2,1,0:T(8,128)} %broadcast_in_dim.6), calls=%async_computation | async-start | bytes 4194304 | tf_op jit(solution)/shard_map/all_to_all | solution.py:175
  18.1 0.0 copy-done.2
  18.1 40.5 %all-gather.1.records = f32[32,9,128]{2,1,0:T(8,128)} all-gather(f32[1,9,128]{2,1,0:T(8,128)S(1)} %bitcast.5), channel_id=2, replica_groups=mesh['row'=32,'col'=16] {'row'}, dimensions={0}, use_global_device_ids=true | all-gather | bytes 152064 | tf_op jit(solution)/shard_map/all_gather | solution.py:195
  58.5 0.6 pad_add_fusion.place
  59.1 4.1 %shard_map.50 = (f32[12,32,128]{2,1,0:T(8,128)}, f32[128,256]{1,0:T(8,128)}) custom-call(s32[2]{0:T(128)} %pad_add_fusion.place, s32[32,32]{1,0:T(8,128)} %pattern.9, f32[32,9,128]{2,1,0:T(8,128)} %all-gather.1.records), custom_call_target="tpu_custom_call" | custom-call | tf_op jit(solution)/shard_map/pallas_call | solution.py:181
  63.1 0.0 all-to-all-done.iterate_row
  63.1 0.0 copy-start.1
  63.1 1.3 copy-done.1
  64.5 15.6 %shard_map.51 = f32[128,256]{1,0:T(8,128)} custom-call(s32[2]{0:T(128)} %pad_add_fusion.place, s32[32,32]{1,0:T(8,128)} %pattern.9, f32[12,32,128]{2,1,0:T(8,128)} %get-tuple-element.7.fields, f32[16,128,256]{2,1,0:T(8,128)} %copy-done.1), custom_call_target="tpu_custom_call" | custom-call | tf_op jit(solution)/shard_map/pallas_call | solution.py:181
  80.0 2.5 %broadcast_in_dim.7 = f32[16,128,256]{2,1,0:T(8,128)} broadcast(f32[128,256]{1,0:T(8,128)} %shard_map.51), dimensions={1,2} | broadcast | bytes 2228224 | tf_op jit(solution)/shard_map/broadcast_in_dim | solution.py:175
  82.5 4.8 %all-to-all-start.1 = ((f32[16,128,256]{2,1,0:T(8,128)}), f32[16,128,256]{2,1,0:T(8,128)S(1)}, u32[]{:S(2)}, u32[]{:S(2)}) async-start(f32[16,128,256]{2,1,0:T(8,128)} %broadcast_in_dim.7), calls=%async_computation.1 | async-start | bytes 4194304 | tf_op jit(solution)/shard_map/all_to_all | solution.py:175
  87.3 2.2 %all-gather.4.cloned.1.call-done.iterate_col = f32[4096,256]{1,0:T(8,128)} async-done(((f32[128,256]{1,0:T(8,128)}), f32[4096,256]{1,0:T(8,128)}) %all-gather.4.cloned.1.call-update) | async-done | bytes 4194320 | tf_op jit(solution)/shard_map/all_gather | solution.py:194
  89.5 5.4 %shard_map.52 = (bf16[4096,256]{1,0:T(8,128)(2,1)}, bf16[4096,256]{1,0:T(8,128)(2,1)}) custom-call(s32[2]{0:T(128)} %pad_add_fusion.place, s32[32,32]{1,0:T(8,128)} %pattern.9, f32[4096,256]{1,0:T(8,128)} %all-gather.4.cloned.1.call-done.iterate_col), custom_call_target="tpu_custom_call" | custom-call | tf_op jit(solution)/shard_map/pallas_call | solution.py:181
  95.0 21.4 %all-to-all-done.1.one_row = f32[16,128,256]{2,1,0:T(8,128)S(1)} async-done(((f32[16,128,256]{2,1,0:T(8,128)}), f32[16,128,256]{2,1,0:T(8,128)S(1)}, u32[]{:S(2)}, u32[]{:S(2)}) %all-to-all-start.1) | async-done | bytes 2097184 | tf_op jit(solution)/shard_map/all_to_all | solution.py:175
  116.4 0.0 copy-start
  116.4 1.3 copy-done
  117.7 4.6 %shard_map.53 = f32[16,2,8,128]{3,2,1,0:T(8,128)} custom-call(s32[2]{0:T(128)} %pad_add_fusion.place, s32[32,32]{1,0:T(8,128)} %pattern.9, f32[16,128,256]{2,1,0:T(8,128)} %copy-done, bf16[4096,256]{1,0:T(8,128)(2,1)} %get-tuple-element.8.high, bf16[4096,256]{1,0:T(8,128)(2,1)} %get-tuple-element.9.low), custom_call_target="tpu_custom_call" | custom-call | tf_op jit(solution)/shard_map/pallas_call | solution.py:181
  122.3 12.1 %all_to_all.25 = f32[16,2,8,128]{3,2,1,0:T(8,128)S(1)} all-to-all(f32[16,2,8,128]{3,2,1,0:T(8,128)} %shard_map.53), channel_id=1, replica_groups=mesh['row'=32,'col'=16] {'col'}, dimensions={0} | all-to-all | bytes 262144 | tf_op jit(solution)/shard_map/all_to_all | solution.py:207
  134.4 27.2 %all_to_all.26 = f32[32,8,128]{2,1,0:T(8,128)S(1)} all-to-all(f32[32,8,128]{2,1,0:T(8,128)S(1)} %bitcast.4), channel_id=1, replica_groups=mesh['row'=32,'col'=16] {'row'}, dimensions={0} | all-to-all | bytes 262144 | tf_op jit(solution)/shard_map/all_to_all | solution.py:208
  161.6 0.2 broadcast_in_dim.8
  161.8 29.4 %all_to_all.27.two_row = f32[16,32,8,128]{3,2,1,0:T(8,128)} all-to-all(f32[16,32,8,128]{3,2,1,0:T(8,128)S(1)} %broadcast_in_dim.8), channel_id=1, replica_groups=mesh['row'=32,'col'=16] {'col'}, dimensions={0} | all-to-all | bytes 4194304 | tf_op jit(solution)/shard_map/all_to_all | solution.py:175
  191.3 4.5 %shard_map.54 = f32[128,256]{1,0:T(8,128)} custom-call(s32[2]{0:T(128)} %pad_add_fusion.place, s32[32,32]{1,0:T(8,128)} %pattern.9, f32[16,32,8,128]{3,2,1,0:T(8,128)} %all_to_all.27.two_row, bf16[4096,256]{1,0:T(8,128)(2,1)} %get-tuple-element.8.high, bf16[4096,256]{1,0:T(8,128)(2,1)} %get-tuple-element.9.low, f32[128,256]{1,0:T(8,128)} %iterate.1), custom_call_target="tpu_custom_call" | custom-call | tf_op jit(solution)/shard_map/pallas_call | solution.py:181
Async XLA Ops:
  7.2 82.4 %all-gather.4.cloned.1.call-start = ((), (), s32[]{:S(2)}) async-start(), calls=%async_computation.5 | async-start | bytes 4325376 | tf_op jit(solution)/shard_map/all_gather | solution.py:194
  10.3 7.7 %copy-start.2 = (f32[9,128]{1,0:T(8,128)S(1)}, f32[9,128]{1,0:T(8,128)}, u32[]{:S(2)}) copy-start(f32[9,128]{1,0:T(8,128)} %param.3) | copy-start | bytes 13828
  10.3 52.8 %all-to-all-start = ((f32[16,128,256]{2,1,0:T(8,128)}), f32[16,128,256]{2,1,0:T(8,128)S(1)}, u32[]{:S(2)}, u32[]{:S(2)}) async-start(f32[16,128,256]{2,1,0:T(8,128)} %broadcast_in_dim.6), calls=%async_computation | async-start | bytes 4194304 | tf_op jit(solution)/shard_map/all_to_all | solution.py:175
  63.1 1.3 copy-start.1
  82.5 33.9 %all-to-all-start.1 = ((f32[16,128,256]{2,1,0:T(8,128)}), f32[16,128,256]{2,1,0:T(8,128)S(1)}, u32[]{:S(2)}, u32[]{:S(2)}) async-start(f32[16,128,256]{2,1,0:T(8,128)} %broadcast_in_dim.7), calls=%async_computation.1 | async-start | bytes 4194304 | tf_op jit(solution)/shard_map/all_to_all | solution.py:175
  116.4 1.3 copy-start
Sparse Core Ops, SparseCore 0:
  10.1 79.3 all-gather.3

commit v3 on v2

--- a/solution.py
+++ b/solution.py
@@ -116,8 +116,14 @@
         return carry
 
     lax.fori_loop(0, 2 * NB, step, 0)
-    product_one[:, :BLOCK] = acc[0]
-    product_one[:, BLOCK:] = acc[1]
+    for copy in range(16):
+        product_one[copy, :, :BLOCK] = acc[0]
+        product_one[copy, :, BLOCK:] = acc[1]
+
+
+def replicate_kernel(place, pattern, value, copies):
+    for copy in range(copies.shape[0]):
+        copies[copy] = value[...]
 
 
 def prepare_kernel(place, pattern, iterate_col, high, low):
@@ -171,43 +177,53 @@
         updated[:, lanes] = mask * (1.5 * iterate[:, lanes] - 0.5 * total[:, lanes])
 
 
-def spread(value, axis, count):
-    return lax.all_to_all(jnp.broadcast_to(value[None], (count,) + value.shape), axis, 0, 0, tiled=True)
-
-
-def call(kernel, out_shapes, scratch, *operands):
+def exchange(pieces, axis):
+    return lax.all_to_all(pieces, axis, 0, 0, tiled=True)
+
+
+def call(kernel, out_shapes, scratch, *operands, on_chip=()):
     whole = pl.BlockSpec(memory_space=VMEM)
     scalars = pl.BlockSpec(memory_space=SMEM)
+    operands = list(operands)
+    for k in on_chip:
+        operands[k] = pltpu.with_memory_space_constraint(operands[k], VMEM)
     return pl.pallas_call(
         kernel,
         out_shape=out_shapes,
         in_specs=[scalars, scalars] + [whole] * (len(operands) - 2),
         out_specs=jax.tree.map(lambda _: whole, out_shapes),
         scratch_shapes=scratch,
+        compiler_params=pltpu.CompilerParams(vmem_limit_bytes=24 * 2**20),
     )(*operands)
 
 
 def stages(records, pattern, iterate):
     place = jnp.stack([lax.axis_index("row"), lax.axis_index("col")]).astype(jnp.int32)
     tile = jax.ShapeDtypeStruct((BLOCK, 2 * BLOCK), jnp.float32)
-    panel = jax.ShapeDtypeStruct((NB * BLOCK, 2 * BLOCK), jnp.bfloat16)
+    panel = VMEM((NB * BLOCK, 2 * BLOCK), jnp.bfloat16)
+    tiles = jax.ShapeDtypeStruct((16, BLOCK, 2 * BLOCK), jnp.float32)
     iterate_col = lax.all_gather(iterate, "row", axis=0, tiled=True)
     everyone = lax.all_gather(records, "row", axis=0)
-    iterate_row = spread(iterate, "col", 16)
+    iterate_row = exchange(jnp.broadcast_to(iterate[None], tiles.shape), "col")
     left = VMEM((2, FIELDS, BLOCK, BLOCK), jnp.float32)
     square = VMEM((BLOCK, BLOCK), jnp.float32)
     acc = VMEM((2, BLOCK, BLOCK), jnp.float32)
     table = jax.ShapeDtypeStruct((FIELDS, NB, BLOCK), jnp.float32)
     fields, margin = call(margin_kernel, (table, tile), [left, square], place, pattern, everyone)
-    product_one = call(first_kernel, tile, [left, square, acc], place, pattern, fields, iterate_row)
-    one_row = spread(product_one, "col", 16)
+    product_one = call(
+        first_kernel, tiles, [left, square, acc], place, pattern, fields, iterate_row, on_chip=(3,)
+    )
+    one_row = exchange(product_one, "col")
     high, low = call(prepare_kernel, (panel, panel), [], place, pattern, iterate_col)
-    slices = jax.ShapeDtypeStruct((16, 2, 8, BLOCK), jnp.float32)
-    slices = call(second_kernel, slices, [], place, pattern, one_row, high, low)
-    slices = lax.all_to_all(slices, "col", 0, 0, tiled=True).reshape(NB, 8, BLOCK)
-    slices = lax.all_to_all(slices, "row", 0, 0, tiled=True)
-    two_row = spread(slices, "col", 16)
-    updated = call(third_kernel, tile, [], place, pattern, two_row, high, low, iterate)
+    slices = VMEM((16, 2, 8, BLOCK), jnp.float32)
+    slices = call(second_kernel, slices, [], place, pattern, one_row, high, low, on_chip=(2, 3, 4))
+    slices = exchange(slices, "col").reshape(NB, 8, BLOCK)
+    slices = exchange(slices, "row")
+    slices = call(
+        replicate_kernel, VMEM((16, NB, 8, BLOCK), jnp.float32), [], place, pattern, slices, on_chip=(2,)
+    )
+    two_row = exchange(slices, "col")
+    updated = call(third_kernel, tile, [], place, pattern, two_row, high, low, iterate, on_chip=(2, 3, 4))
     return (margin, updated)
 
 

time: 204 us -> 194 us (0.951)
  Pallas kernels: 34.2 us -> 26.2 us
    pallas_call x5 -> x6, Pallas kernels: 34.2 us -> 26.2 us  [call(): pl.pallas_call(kernel, out_shape=out_shapes, in_specs=[scalars, scalars]...]
    all_to_all x2, waiting for transfers between devices: 21.4 us -> 14.5 us  [exchange(): return lax.all_to_all(pieces, axis, 0, 0, tiled=True)]
    all_gather x1, waiting for transfers between devices: 2.24 us -> 9.15 us  [stages(): iterate_col = lax.all_gather(iterate, 'row', axis=0, tiled=True)]
    unnamed x6 -> x16, local copies, waits for them, and re-layouts: 2.66 us -> 6.47 us
    broadcast_in_dim x3 -> x1, local copies, waits for them, and re-layouts: 5.1 us -> 2.46 us  [stages(): iterate_row = exchange(jnp.broadcast_to(iterate[None], tiles.shape), 'col')]
    all_gather x1, blocking collectives: 40.5 us -> 38 us  [stages(): everyone = lax.all_gather(records, 'row', axis=0)]
  transfers between devices with their start and end apart: 3 -> 3, of which waited for: 2 -> 2; matrix products, arithmetic and copies ran while one was open for 3% -> 1% of each run, Pallas kernels for 12% -> 10%
where the time goes in v3:
time: 194 us; the launch traced here: 193 us
  blocking collectives  107 us (55%)
  Pallas kernels  26.2 us (14%)
  waiting for transfers between devices  24.4 us (13%)
  between operations  14.1 us (7%)
  starting transfers between devices  12.2 us (6%)
  local copies, waits for them, and re-layouts  8.93 us (5%)
    all_to_all x3, blocking collectives, exchange(): return lax.all_to_all(pieces, axis, 0, 0, tiled=True)  68.6 us
    all_gather x1, blocking collectives, stages(): everyone = lax.all_gather(records, 'row', axis=0)  38 us
    pallas_call x6, Pallas kernels, call(): pl.pallas_call(kernel, out_shape=out_shapes, in_specs=[scalars, scalars]...  26.2 us
    all_to_all x2, waiting for transfers between devices, exchange(): return lax.all_to_all(pieces, axis, 0, 0, tiled=True)  14.5 us
    all_to_all x2, starting transfers between devices, exchange(): return lax.all_to_all(pieces, axis, 0, 0, tiled=True)  12.2 us
    all_gather x1, waiting for transfers between devices, stages(): iterate_col = lax.all_gather(iterate, 'row', axis=0, tiled=True)  9.15 us
    unnamed x16, local copies, waits for them, and re-layouts  6.47 us
  transfers between devices with their start and end apart: 3, of which 2 were waited for; matrix products, arithmetic and copies ran while one was open for 1% of the time, Pallas kernels for 10%

profile of v3, /device:TPU:1, one launch (start us, length us, event | category | flops | bytes accessed | tf_op | source)
XLA Modules:
  0.0 192.5 jit_solution(13528470382835671415)
XLA Ops:
  7.2 0.0 all-gather.4.cloned.1.call-start
  7.2 0.7 all-gather.4.cloned.1.call-update
  7.9 2.5 %broadcast_in_dim.2 = f32[16,128,256]{2,1,0:T(8,128)} broadcast(f32[128,256]{1,0:T(8,128)} %iterate.1), dimensions={1,2} | broadcast | bytes 2228224 | tf_op jit(solution)/shard_map/broadcast_in_dim | solution.py:207
  10.4 0.0 copy-start.7
  10.4 0.0 copy-start.6
  10.4 7.7 %all-to-all-start = ((f32[16,128,256]{2,1,0:T(8,128)}), f32[16,128,256]{2,1,0:T(8,128)S(1)}, u32[]{:S(2)}, u32[]{:S(2)}) async-start(f32[16,128,256]{2,1,0:T(8,128)} %broadcast_in_dim.2), calls=%async_computation | async-start | bytes 4194304 | tf_op jit(solution)/shard_map/all_to_all | solution.py:181
  18.1 0.0 copy-done.7
  18.1 38.0 %all-gather.1.records = f32[32,9,128]{2,1,0:T(8,128)S(1)} all-gather(f32[1,9,128]{2,1,0:T(8,128)S(1)} %bitcast.5), channel_id=2, replica_groups=mesh['row'=32,'col'=16] {'row'}, dimensions={0}, use_global_device_ids=true | all-gather | bytes 152064 | tf_op jit(solution)/shard_map/all_gather | solution.py:206
  56.1 0.1 pad_add_fusion.place
  56.2 0.0 copy-done.6
  56.2 3.8 %shard_map.50 = (f32[12,32,128]{2,1,0:T(8,128)S(1)}, f32[128,256]{1,0:T(8,128)}) custom-call(s32[2]{0:T(128)S(1)} %pad_add_fusion.place, s32[32,32]{1,0:T(8,128)S(1)} %copy-done.6, f32[32,9,128]{2,1,0:T(8,128)S(1)} %all-gather.1.records), custom_call_target="tpu_custom_call" | custom-call | tf_op jit(solution)/shard_map/pallas_call | solution.py:190
  60.0 0.0 all-to-all-done.iterate_row
  60.0 14.1 %shard_map.51 = f32[16,128,256]{2,1,0:T(8,128)S(1)} custom-call(s32[2]{0:T(128)S(1)} %pad_add_fusion.place, s32[32,32]{1,0:T(8,128)S(1)} %copy-done.6, f32[12,32,128]{2,1,0:T(8,128)S(1)} %get-tuple-element.7.fields, f32[16,128,256]{2,1,0:T(8,128)S(1)} %all-to-all-done.iterate_row), custom_call_target="tpu_custom_call" | custom-call | tf_op jit(solution)/shard_map/pallas_call | solution.py:190
  74.2 0.0 copy-start.3
  74.2 1.3 copy-done.3
  75.5 4.5 %all-to-all-start.1 = ((f32[16,128,256]{2,1,0:T(8,128)}), f32[16,128,256]{2,1,0:T(8,128)}, u32[]{:S(2)}, u32[]{:S(2)}) async-start(f32[16,128,256]{2,1,0:T(8,128)} %copy-done.3), calls=%async_computation.1 | async-start | bytes 4194304 | tf_op jit(solution)/shard_map/all_to_all | solution.py:181
  80.0 9.1 %all-gather.4.cloned.1.call-done.iterate_col = f32[4096,256]{1,0:T(8,128)} async-done(((f32[128,256]{1,0:T(8,128)}), f32[4096,256]{1,0:T(8,128)}) %all-gather.4.cloned.1.call-update) | async-done | bytes 4194320 | tf_op jit(solution)/shard_map/all_gather | solution.py:205
  89.2 0.0 copy-start.4
  89.2 2.2 %copy-done.4 = f32[4096,256]{1,0:T(8,128)S(1)} copy-done((f32[4096,256]{1,0:T(8,128)S(1)}, f32[4096,256]{1,0:T(8,128)}, u32[]{:S(2)}) %copy-start.4) | copy-done | bytes 4194328
  91.4 2.1 %shard_map.52 = (bf16[4096,256]{1,0:T(8,128)(2,1)S(1)}, bf16[4096,256]{1,0:T(8,128)(2,1)S(1)}) custom-call(s32[2]{0:T(128)S(1)} %pad_add_fusion.place, s32[32,32]{1,0:T(8,128)S(1)} %copy-done.6, f32[4096,256]{1,0:T(8,128)S(1)} %copy-done.4), custom_call_target="tpu_custom_call" | custom-call | tf_op jit(solution)/shard_map/pallas_call | solution.py:190
  93.4 0.0 copy-start
  93.4 1.3 copy-done
  94.8 14.5 %all-to-all-done.1.one_row = f32[16,128,256]{2,1,0:T(8,128)} async-done(((f32[16,128,256]{2,1,0:T(8,128)}), f32[16,128,256]{2,1,0:T(8,128)}, u32[]{:S(2)}, u32[]{:S(2)}) %all-to-all-start.1) | async-done | bytes 2097184 | tf_op jit(solution)/shard_map/all_to_all | solution.py:181
  109.3 0.0 copy-start.1
  109.3 1.6 copy-done.1
  110.9 2.7 %shard_map.53 = f32[16,2,8,128]{3,2,1,0:T(8,128)S(1)} custom-call(s32[2]{0:T(128)S(1)} %pad_add_fusion.place, s32[32,32]{1,0:T(8,128)S(1)} %copy-done.6, f32[16,128,256]{2,1,0:T(8,128)} %all-to-all-done.1.one_row, bf16[4096,256]{1,0:T(8,128)(2,1)S(1)} %get-tuple-element.8.high, bf16[4096,256]{1,0:T(8,128)(2,1)S(1)} %copy-done.1), custom_call_target="tpu_custom_call" | custom-call | tf_op jit(solution)/shard_map/pallas_call | solution.py:190
  113.6 11.1 %all_to_all.25 = f32[16,2,8,128]{3,2,1,0:T(8,128)S(1)} all-to-all(f32[16,2,8,128]{3,2,1,0:T(8,128)S(1)} %shard_map.53), channel_id=1, replica_groups=mesh['row'=32,'col'=16] {'col'}, dimensions={0} | all-to-all | bytes 262144 | tf_op jit(solution)/shard_map/all_to_all | solution.py:181
  124.7 28.0 %all_to_all.26.value = f32[32,8,128]{2,1,0:T(8,128)S(1)} all-to-all(f32[32,8,128]{2,1,0:T(8,128)S(1)} %bitcast.4), channel_id=1, replica_groups=mesh['row'=32,'col'=16] {'row'}, dimensions={0} | all-to-all | bytes 262144 | tf_op jit(solution)/shard_map/all_to_all | solution.py:181
  152.7 0.9 shard_map.54
  153.7 0.0 copy-start.2
  153.7 0.0 copy-start.5
  153.7 29.5 %all_to_all.27.two_row = f32[16,32,8,128]{3,2,1,0:T(8,128)S(1)} all-to-all(f32[16,32,8,128]{3,2,1,0:T(8,128)S(1)} %shard_map.54), channel_id=1, replica_groups=mesh['row'=32,'col'=16] {'col'}, dimensions={0} | all-to-all | bytes 4194304 | tf_op jit(solution)/shard_map/all_to_all | solution.py:181
  183.2 0.0 copy-done.2
  183.2 0.0 copy-done.5
  183.2 2.5 %shard_map.55 = f32[128,256]{1,0:T(8,128)} custom-call(s32[2]{0:T(128)S(1)} %pad_add_fusion.place, s32[32,32]{1,0:T(8,128)S(1)} %copy-done.6, f32[16,32,8,128]{3,2,1,0:T(8,128)S(1)} %all_to_all.27.two_row, bf16[4096,256]{1,0:T(8,128)(2,1)S(1)} %get-tuple-element.8.high, bf16[4096,256]{1,0:T(8,128)(2,1)S(1)} %copy-done.2, f32[128,256]{1,0:T(8,128)S(1)} %copy-done.5), custom_call_target="tpu_custom_call" | custom-call | tf_op jit(solution)/shard_map/pallas_call | solution.py:190
Async XLA Ops:
  7.2 82.0 %all-gather.4.cloned.1.call-start = ((), (), s32[]{:S(2)}) async-start(), calls=%async_computation.5 | async-start | bytes 4325376 | tf_op jit(solution)/shard_map/all_gather | solution.py:205
  10.4 7.7 %copy-start.7 = (f32[9,128]{1,0:T(8,128)S(1)}, f32[9,128]{1,0:T(8,128)}, u32[]{:S(2)}) copy-start(f32[9,128]{1,0:T(8,128)} %param.3) | copy-start | bytes 13828
  10.4 45.8 %copy-start.6 = (s32[32,32]{1,0:T(8,128)S(1)}, s32[32,32]{1,0:T(8,128)}, u32[]{:S(2)}) copy-start(s32[32,32]{1,0:T(8,128)} %pattern.11) | copy-start | bytes 12292
  10.4 49.7 %all-to-all-start = ((f32[16,128,256]{2,1,0:T(8,128)}), f32[16,128,256]{2,1,0:T(8,128)S(1)}, u32[]{:S(2)}, u32[]{:S(2)}) async-start(f32[16,128,256]{2,1,0:T(8,128)} %broadcast_in_dim.2), calls=%async_computation | async-start | bytes 4194304 | tf_op jit(solution)/shard_map/all_to_all | solution.py:181
  74.2 1.4 copy-start.3
  75.5 33.8 %all-to-all-start.1 = ((f32[16,128,256]{2,1,0:T(8,128)}), f32[16,128,256]{2,1,0:T(8,128)}, u32[]{:S(2)}, u32[]{:S(2)}) async-start(f32[16,128,256]{2,1,0:T(8,128)} %copy-done.3), calls=%async_computation.1 | async-start | bytes 4194304 | tf_op jit(solution)/shard_map/all_to_all | solution.py:181
  89.2 2.2 %copy-start.4 = (f32[4096,256]{1,0:T(8,128)S(1)}, f32[4096,256]{1,0:T(8,128)}, u32[]{:S(2)}) copy-start(f32[4096,256]{1,0:T(8,128)} %all-gather.4.cloned.1.call-done.iterate_col) | copy-start | bytes 12582916
  93.4 1.3 copy-start
  109.3 1.6 copy-start.1
  153.7 29.5 %copy-start.2 = (bf16[4096,256]{1,0:T(8,128)(2,1)S(1)}, bf16[4096,256]{1,0:T(8,128)(2,1)}, u32[]{:S(2)}) copy-start(bf16[4096,256]{1,0:T(8,128)(2,1)} %copy-done) | copy-start | bytes 6291460
  153.7 29.5 %copy-start.5 = (f32[128,256]{1,0:T(8,128)S(1)}, f32[128,256]{1,0:T(8,128)}, u32[]{:S(2)}) copy-start(f32[128,256]{1,0:T(8,128)} %iterate.1) | copy-start | bytes 393220
Sparse Core Ops, SparseCore 0:
  10.1 79.0 all-gather.3

commit v4 on v3

--- a/solution.py
+++ b/solution.py
@@ -155,20 +155,23 @@
     return (pattern[row, column] != 0).astype(jnp.float32)
 
 
-def second_kernel(place, pattern, one_row, high, low, slices):
+def second_kernel(place, pattern, one_row, high, low, kept, given, tile):
     row, col = place[0], place[1]
     total = contract([one_row[k] for k in range(16)], high, low)
     for half in range(2):
         own = total[:, half * BLOCK : (half + 1) * BLOCK]
-        own = (live(pattern, row, 2 * col + half) * own).T
-        slices[:, half] = own.reshape(BLOCK // 8, 8, BLOCK)
+        tile[half] = (live(pattern, row, 2 * col + half) * own).T
+    core = row % 2
+    kept[...] = tile[core].reshape(BLOCK // 8, 8, BLOCK)
+    given[...] = tile[1 - core].reshape(BLOCK // 8, 8, BLOCK)
 
 
 def third_kernel(place, pattern, two_row, high, low, iterate, updated):
     row, col = place[0], place[1]
+    core = row % 2
     pieces = []
     for k in range(16):
-        pair = [two_row[:, 2 * k + h].reshape(BLOCK, BLOCK) for h in range(2)]
+        pair = [two_row[:, k, core ^ h].reshape(BLOCK, BLOCK) for h in range(2)]
         pieces.append(jnp.concatenate(pair, axis=1))
     total = contract(pieces, high, low)
     for half in range(2):
@@ -215,13 +218,18 @@
     )
     one_row = exchange(product_one, "col")
     high, low = call(prepare_kernel, (panel, panel), [], place, pattern, iterate_col)
-    slices = VMEM((16, 2, 8, BLOCK), jnp.float32)
-    slices = call(second_kernel, slices, [], place, pattern, one_row, high, low, on_chip=(2, 3, 4))
-    slices = exchange(slices, "col").reshape(NB, 8, BLOCK)
-    slices = exchange(slices, "row")
-    slices = call(
-        replicate_kernel, VMEM((16, NB, 8, BLOCK), jnp.float32), [], place, pattern, slices, on_chip=(2,)
+    half = VMEM((16, 8, BLOCK), jnp.float32)
+    turned = VMEM((2, BLOCK, BLOCK), jnp.float32)
+    kept, given = call(
+        second_kernel, (half, half), [turned], place, pattern, one_row, high, low, on_chip=(2, 3, 4)
     )
+    given = lax.ppermute(given, "row", [(r, r ^ 1) for r in range(NB)])
+    slices = jnp.stack([kept, given], axis=1)
+    slices = exchange(slices, "col")
+    cores = [[2 * z + core for z in range(16)] for core in range(2)]
+    slices = lax.all_to_all(slices, "row", 0, 0, tiled=True, axis_index_groups=cores)
+    copies = VMEM((16,) + slices.shape, jnp.float32)
+    slices = call(replicate_kernel, copies, [], place, pattern, slices, on_chip=(2,))
     two_row = exchange(slices, "col")
     updated = call(third_kernel, tile, [], place, pattern, two_row, high, low, iterate, on_chip=(2, 3, 4))
     return (margin, updated)

time: 194 us -> 193 us (level); the launches traced: 193 us -> 189 us
  blocking collectives: 107 us -> 97.9 us
  starting transfers between devices: 12.2 us -> 16.7 us
    all_to_all x3 -> x2, blocking collectives: 68.6 us -> 37.6 us  [exchange(): return lax.all_to_all(pieces, axis, 0, 0, tiled=True)]
    all_to_all x0 -> x1, blocking collectives: none -> 22.2 us  [stages(): lax.all_to_all(slices, 'row', 0, 0, tiled=True, axis_index_groups=cores)]
    ppermute x0 -> x1, starting transfers between devices: none -> 4.43 us  [stages(): given = lax.ppermute(given, 'row', [(r, r ^ 1) for r in range(NB)])]
  transfers between devices with their start and end apart: 3 -> 4, of which waited for: 2 -> 3; matrix products, arithmetic and copies ran while one was open for 1% -> 1% of each run, Pallas kernels for 10% -> 11%
where the time goes in v4:
time: 193 us; the launch traced here: 189 us
  blocking collectives  97.9 us (51%)
  Pallas kernels  26.3 us (14%)
  waiting for transfers between devices  25.2 us (13%)
  starting transfers between devices  16.7 us (9%)
  between operations  14.1 us (7%)
  local copies, waits for them, and re-layouts  8.95 us (5%)
    all_gather x1, blocking collectives, stages(): everyone = lax.all_gather(records, 'row', axis=0)  38 us
    all_to_all x2, blocking collectives, exchange(): return lax.all_to_all(pieces, axis, 0, 0, tiled=True)  37.6 us
    pallas_call x6, Pallas kernels, call(): pl.pallas_call(kernel, out_shape=out_shapes, in_specs=[scalars, scalars]...  26.3 us
    all_to_all x1, blocking collectives, stages(): lax.all_to_all(slices, 'row', 0, 0, tiled=True, axis_index_groups=cores)  22.2 us
    all_to_all x2, waiting for transfers between devices, exchange(): return lax.all_to_all(pieces, axis, 0, 0, tiled=True)  14.5 us
    all_to_all x2, starting transfers between devices, exchange(): return lax.all_to_all(pieces, axis, 0, 0, tiled=True)  12.2 us
    all_gather x1, waiting for transfers between devices, stages(): iterate_col = lax.all_gather(iterate, 'row', axis=0, tiled=True)  9.16 us
    unnamed x16, local copies, waits for them, and re-layouts  6.48 us
  transfers between devices with their start and end apart: 4, of which 3 were waited for; matrix products, arithmetic and copies ran while one was open for 1% of the time, Pallas kernels for 11%

profile of v4, /device:TPU:1, one launch (start us, length us, event | category | flops | bytes accessed | tf_op | source)
XLA Modules:
  0.0 189.2 jit_solution(17243239081278434938)
XLA Ops:
  7.2 0.0 all-gather.4.cloned.1.call-start
  7.2 0.7 all-gather.4.cloned.1.call-update
  7.9 2.5 %broadcast_in_dim.2 = f32[16,128,256]{2,1,0:T(8,128)} broadcast(f32[128,256]{1,0:T(8,128)} %iterate.1), dimensions={1,2} | broadcast | bytes 2228224 | tf_op jit(solution)/shard_map/broadcast_in_dim | solution.py:210
  10.4 0.0 copy-start.7
  10.4 0.0 copy-start.6
  10.4 7.7 %all-to-all-start = ((f32[16,128,256]{2,1,0:T(8,128)}), f32[16,128,256]{2,1,0:T(8,128)S(1)}, u32[]{:S(2)}, u32[]{:S(2)}) async-start(f32[16,128,256]{2,1,0:T(8,128)} %broadcast_in_dim.2), calls=%async_computation | async-start | bytes 4194304 | tf_op jit(solution)/shard_map/all_to_all | solution.py:184
  18.1 0.0 copy-done.7
  18.1 38.0 %all-gather.1.records = f32[32,9,128]{2,1,0:T(8,128)S(1)} all-gather(f32[1,9,128]{2,1,0:T(8,128)S(1)} %bitcast.7), channel_id=2, replica_groups=mesh['row'=32,'col'=16] {'row'}, dimensions={0}, use_global_device_ids=true | all-gather | bytes 152064 | tf_op jit(solution)/shard_map/all_gather | solution.py:209
  56.1 0.1 pad_add_fusion.place
  56.2 0.0 copy-done.6
  56.2 3.8 %shard_map.50 = (f32[12,32,128]{2,1,0:T(8,128)S(1)}, f32[128,256]{1,0:T(8,128)}) custom-call(s32[2]{0:T(128)S(1)} %pad_add_fusion.place, s32[32,32]{1,0:T(8,128)S(1)} %copy-done.6, f32[32,9,128]{2,1,0:T(8,128)S(1)} %all-gather.1.records), custom_call_target="tpu_custom_call" | custom-call | tf_op jit(solution)/shard_map/pallas_call | solution.py:193
  60.0 0.0 all-to-all-done.iterate_row
  60.0 14.1 %shard_map.51 = f32[16,128,256]{2,1,0:T(8,128)S(1)} custom-call(s32[2]{0:T(128)S(1)} %pad_add_fusion.place, s32[32,32]{1,0:T(8,128)S(1)} %copy-done.6, f32[12,32,128]{2,1,0:T(8,128)S(1)} %get-tuple-element.9.fields, f32[16,128,256]{2,1,0:T(8,128)S(1)} %all-to-all-done.iterate_row), custom_call_target="tpu_custom_call" | custom-call | tf_op jit(solution)/shard_map/pallas_call | solution.py:193
  74.2 0.0 copy-start.3
  74.2 1.4 copy-done.3
  75.5 4.5 %all-to-all-start.1 = ((f32[16,128,256]{2,1,0:T(8,128)}), f32[16,128,256]{2,1,0:T(8,128)}, u32[]{:S(2)}, u32[]{:S(2)}) async-start(f32[16,128,256]{2,1,0:T(8,128)} %copy-done.3), calls=%async_computation.1 | async-start | bytes 4194304 | tf_op jit(solution)/shard_map/all_to_all | solution.py:184
  80.0 9.2 %all-gather.4.cloned.1.call-done.iterate_col = f32[4096,256]{1,0:T(8,128)} async-done(((f32[128,256]{1,0:T(8,128)}), f32[4096,256]{1,0:T(8,128)}) %all-gather.4.cloned.1.call-update) | async-done | bytes 4194320 | tf_op jit(solution)/shard_map/all_gather | solution.py:208
  89.2 0.0 copy-start.4
  89.2 2.2 %copy-done.4 = f32[4096,256]{1,0:T(8,128)S(1)} copy-done((f32[4096,256]{1,0:T(8,128)S(1)}, f32[4096,256]{1,0:T(8,128)}, u32[]{:S(2)}) %copy-start.4) | copy-done | bytes 4194328
  91.4 2.1 %shard_map.52 = (bf16[4096,256]{1,0:T(8,128)(2,1)S(1)}, bf16[4096,256]{1,0:T(8,128)(2,1)S(1)}) custom-call(s32[2]{0:T(128)S(1)} %pad_add_fusion.place, s32[32,32]{1,0:T(8,128)S(1)} %copy-done.6, f32[4096,256]{1,0:T(8,128)S(1)} %copy-done.4), custom_call_target="tpu_custom_call" | custom-call | tf_op jit(solution)/shard_map/pallas_call | solution.py:193
  93.4 0.0 copy-start
  93.5 1.3 copy-done
  94.8 14.5 %all-to-all-done.1.one_row = f32[16,128,256]{2,1,0:T(8,128)} async-done(((f32[16,128,256]{2,1,0:T(8,128)}), f32[16,128,256]{2,1,0:T(8,128)}, u32[]{:S(2)}, u32[]{:S(2)}) %all-to-all-start.1) | async-done | bytes 2097184 | tf_op jit(solution)/shard_map/all_to_all | solution.py:184
  109.3 0.0 copy-start.1
  109.3 1.6 copy-done.1
  110.9 2.8 %shard_map.53 = (f32[16,8,128]{2,1,0:T(8,128)S(1)}, f32[16,8,128]{2,1,0:T(8,128)S(1)}) custom-call(s32[2]{0:T(128)S(1)} %pad_add_fusion.place, s32[32,32]{1,0:T(8,128)S(1)} %copy-done.6, f32[16,128,256]{2,1,0:T(8,128)} %all-to-all-done.1.one_row, bf16[4096,256]{1,0:T(8,128)(2,1)S(1)} %get-tuple-element.10.high, bf16[4096,256]{1,0:T(8,128)(2,1)S(1)} %copy-done.1), custom_call_target="tpu_custom_call" | custom-call | tf_op jit(solution)/shard_map/pallas_call | solution.py:193
  113.7 4.4 %collective-permute-start = (f32[16,8,128]{2,1,0:T(8,128)S(1)}, f32[16,8,128]{2,1,0:T(8,128)S(1)}, u32[]{:S(2)}, u32[]{:S(2)}) collective-permute-start(f32[16,8,128]{2,1,0:T(8,128)S(1)} %get-tuple-element.13), channel_id=1, source_target_pairs={{0,16},{16,0},{32,48},{48,32},{64,80},{80,64},{96,112},{112,96},{1... | collective-permute-start | bytes 196616 | tf_op jit(solution)/shard_map/ppermute | solution.py:226
  118.1 0.9 collective-permute-done
  119.0 10.1 %all_to_all.25 = f32[16,2,8,128]{3,2,1,0:T(8,128)S(1)} all-to-all(f32[16,2,8,128]{3,2,1,0:T(8,128)S(1)} %pad_maximum_fusion), channel_id=1, replica_groups=mesh['row'=32,'col'=16] {'col'}, dimensions={0} | all-to-all | bytes 262144 | tf_op jit(solution)/shard_map/all_to_all | solution.py:184
  129.1 22.2 %all_to_all.26.value = f32[16,2,8,128]{3,2,1,0:T(8,128)S(1)} all-to-all(f32[16,2,8,128]{3,2,1,0:T(8,128)S(1)} %all_to_all.25), channel_id=1, replica_groups={{0,32,64,96,128,160,192,224,256,288,320,352,384,416,448,480},{16,48,80,..., dimensions={0} | all-to-all | bytes 262144 | tf_op jit(solution)/shard_map/all_to_all | solution.py:230
  151.3 0.9 shard_map.54
  152.3 0.0 copy-start.2
  152.3 0.0 copy-start.5
  152.3 27.5 %all_to_all.27.two_row = f32[16,16,2,8,128]{4,3,2,1,0:T(8,128)S(1)} all-to-all(f32[16,16,2,8,128]{4,3,2,1,0:T(8,128)S(1)} %shard_map.54), channel_id=1, replica_groups=mesh['row'=32,'col'=16] {'col'}, dimensions={0} | all-to-all | bytes 4194304 | tf_op jit(solution)/shard_map/all_to_all | solution.py:184
  179.8 0.0 copy-done.2
  179.8 0.0 copy-done.5
  179.8 2.5 %shard_map.55 = f32[128,256]{1,0:T(8,128)} custom-call(s32[2]{0:T(128)S(1)} %pad_add_fusion.place, s32[32,32]{1,0:T(8,128)S(1)} %copy-done.6, f32[16,16,2,8,128]{4,3,2,1,0:T(8,128)S(1)} %all_to_all.27.two_row, bf16[4096,256]{1,0:T(8,128)(2,1)S(1)} %get-tuple-element.10.high, bf16[4096,256]{1,0:T(8,128)(2,1)S(1)} %copy-done.2, f32[128,256]{1,0:T(8,128)S(1)} %copy-done.5), custom_call_target="tpu_custom_call" | custom-call | tf_op jit(solution)/shard_map/pallas_call | solution.py:193
  (1 shorter events, 0.0 us)
Async XLA Ops:
  7.2 82.0 %all-gather.4.cloned.1.call-start = ((), (), s32[]{:S(2)}) async-start(), calls=%async_computation.5 | async-start | bytes 4325376 | tf_op jit(solution)/shard_map/all_gather | solution.py:208
  10.4 7.7 %copy-start.7 = (f32[9,128]{1,0:T(8,128)S(1)}, f32[9,128]{1,0:T(8,128)}, u32[]{:S(2)}) copy-start(f32[9,128]{1,0:T(8,128)} %param.3) | copy-start | bytes 13828
  10.4 45.8 %copy-start.6 = (s32[32,32]{1,0:T(8,128)S(1)}, s32[32,32]{1,0:T(8,128)}, u32[]{:S(2)}) copy-start(s32[32,32]{1,0:T(8,128)} %pattern.11) | copy-start | bytes 12292
  10.4 49.7 %all-to-all-start = ((f32[16,128,256]{2,1,0:T(8,128)}), f32[16,128,256]{2,1,0:T(8,128)S(1)}, u32[]{:S(2)}, u32[]{:S(2)}) async-start(f32[16,128,256]{2,1,0:T(8,128)} %broadcast_in_dim.2), calls=%async_computation | async-start | bytes 4194304 | tf_op jit(solution)/shard_map/all_to_all | solution.py:184
  74.2 1.4 copy-start.3
  75.5 33.8 %all-to-all-start.1 = ((f32[16,128,256]{2,1,0:T(8,128)}), f32[16,128,256]{2,1,0:T(8,128)}, u32[]{:S(2)}, u32[]{:S(2)}) async-start(f32[16,128,256]{2,1,0:T(8,128)} %copy-done.3), calls=%async_computation.1 | async-start | bytes 4194304 | tf_op jit(solution)/shard_map/all_to_all | solution.py:184
  89.2 2.2 %copy-start.4 = (f32[4096,256]{1,0:T(8,128)S(1)}, f32[4096,256]{1,0:T(8,128)}, u32[]{:S(2)}) copy-start(f32[4096,256]{1,0:T(8,128)} %all-gather.4.cloned.1.call-done.iterate_col) | copy-start | bytes 12582916
  93.4 1.3 copy-start
  109.3 1.6 copy-start.1
  113.7 5.3 %collective-permute-start = (f32[16,8,128]{2,1,0:T(8,128)S(1)}, f32[16,8,128]{2,1,0:T(8,128)S(1)}, u32[]{:S(2)}, u32[]{:S(2)}) collective-permute-start(f32[16,8,128]{2,1,0:T(8,128)S(1)} %get-tuple-element.13), channel_id=1, source_target_pairs={{0,16},{16,0},{32,48},{48,32},{64,80},{80,64},{96,112},{112,96},{1... | collective-permute-start | bytes 196616 | tf_op jit(solution)/shard_map/ppermute | solution.py:226
  152.3 27.6 %copy-start.2 = (bf16[4096,256]{1,0:T(8,128)(2,1)S(1)}, bf16[4096,256]{1,0:T(8,128)(2,1)}, u32[]{:S(2)}) copy-start(bf16[4096,256]{1,0:T(8,128)(2,1)} %copy-done) | copy-start | bytes 6291460
  152.3 27.5 %copy-start.5 = (f32[128,256]{1,0:T(8,128)S(1)}, f32[128,256]{1,0:T(8,128)}, u32[]{:S(2)}) copy-start(f32[128,256]{1,0:T(8,128)} %iterate.1) | copy-start | bytes 393220
Sparse Core Ops, SparseCore 0:
  10.1 79.0 all-gather.3

commit v5 on v4

--- a/solution.py
+++ b/solution.py
@@ -9,8 +9,8 @@
 BLOCK = 128
 PRIMS = 3
 NB = 32
-FIELDS = 3 + 3 * PRIMS
-CHUNK = 32
+FIELDS = 3 + 2 * PRIMS
+CHUNK = 64
 LOG2E = 1.4426950408889634
 VMEM = pltpu.VMEM
 SMEM = pltpu.SMEM
@@ -20,17 +20,6 @@
     high = value.astype(jnp.bfloat16)
     low = (value - high.astype(jnp.float32)).astype(jnp.bfloat16)
     return high, low
-
-
-def product(left, right, right_dim):
-    left_high, left_low = split(left)
-    right_high, right_low = split(right)
-    dims = (((1,), (right_dim,)), ((), ()))
-
-    def dot(a, b):
-        return lax.dot_general(a, b, dims, preferred_element_type=jnp.float32)
-
-    return dot(left_high, right_high) + (dot(left_high, right_low) + dot(left_low, right_high))
 
 
 def half_tile(fields_ref, left_ref, tile_ref, half, block):
@@ -44,81 +33,94 @@
         distance = (distance + (left[2] - right[2]) ** 2) * -LOG2E
         total = jnp.zeros_like(distance)
         for p in range(PRIMS):
-            inner = jnp.zeros_like(distance)
+            stretched = left[3 + p] * distance
             for q in range(PRIMS):
-                summed = left[3 + p] + right[3 + q]
-                root = (left[6 + p] * lax.rsqrt(summed)) * right[6 + q]
-                ratio = root * root
-                decay = jnp.exp2(((ratio * summed) * ratio) * distance)
-                inner = inner + right[9 + q] * ((ratio * root) * decay)
-            total = total + left[9 + p] * inner
+                inverse_root = lax.rsqrt(left[3 + p] + right[3 + q])
+                root = (left[6 + p] * inverse_root) * right[6 + q]
+                decay = jnp.exp2((stretched * (inverse_root * inverse_root)) * right[3 + q])
+                total = total + ((root * root) * root) * decay
         tile_ref[rows, :] = total
         return carry
 
     lax.fori_loop(0, BLOCK // CHUNK, chunk, 0)
 
 
-def spread_own(fields, left, col):
+def slot(core, block):
+    return (core ^ (block % 2)) * (NB // 2) + block // 2
+
+
+def spread_own(fields, left, core, col):
     for half in range(2):
         for f in range(FIELDS):
-            own = jnp.broadcast_to(fields[f, pl.ds(2 * col + half, 1), :], (BLOCK, BLOCK))
-            left[half, f] = own.T
-
-
-def margin_kernel(place, pattern, records, fields, margin, left, tile):
-    row, col = place[0], place[1]
-    exponents = [records[:, 3 + p, :] for p in range(PRIMS)]
-    coefficients = [records[:, 3 + PRIMS + p, :] for p in range(PRIMS)]
-    roots = [jnp.sqrt(e) for e in exponents]
-    norm = jnp.zeros_like(exponents[0])
-    for p in range(PRIMS):
-        for q in range(PRIMS):
-            ratio = 2.0 * roots[p] * roots[q] / (exponents[p] + exponents[q])
-            norm = norm + coefficients[p] * coefficients[q] * (ratio * jnp.sqrt(ratio))
-    scale = (2.0**0.75) * lax.rsqrt(norm)
-    for f in range(3):
-        fields[f] = records[:, f, :]
-    for p in range(PRIMS):
-        fields[3 + p] = exponents[p]
-        fields[6 + p] = jnp.sqrt(roots[p])
-        fields[9 + p] = coefficients[p] * scale
-    spread_own(fields, left, col)
-    for half in range(2):
-        margin_live = pattern[row, 2 * col + half] != 0
-        lanes = slice(half * BLOCK, (half + 1) * BLOCK)
-
-        @pl.when(margin_live)
-        def _():
-            half_tile(fields, left, tile, half, row)
-            margin[:, lanes] = tile[...].T
-
-        @pl.when(jnp.logical_not(margin_live))
-        def _():
-            margin[:, lanes] = jnp.zeros((BLOCK, BLOCK), jnp.float32)
-
-
-def first_kernel(place, pattern, fields, iterate_row, product_one, left, tile, acc):
-    row, col = place[0], place[1]
-    spread_own(fields, left, col)
-    acc[...] = jnp.zeros_like(acc)
+            own = fields[f, pl.ds(slot(core, 2 * col + half), 1), :]
+            left[half, f] = jnp.broadcast_to(own, (BLOCK, BLOCK)).T
+
+
+def tiles_kernel(place, pattern, records, fields, high, low, left, tile):
+    row, col = place[0], place[1]
+    core = row % 2
+    for part in range(2):
+        half_table = slice(part * NB // 2, (part + 1) * NB // 2)
+        exponents = [records[:, part, 3 + p, :] for p in range(PRIMS)]
+        coefficients = [records[:, part, 3 + PRIMS + p, :] for p in range(PRIMS)]
+        roots = [jnp.sqrt(e) for e in exponents]
+        norm = jnp.zeros_like(exponents[0])
+        for p in range(PRIMS):
+            for q in range(PRIMS):
+                ratio = 2.0 * roots[p] * roots[q] / (exponents[p] + exponents[q])
+                norm = norm + coefficients[p] * coefficients[q] * (ratio * jnp.sqrt(ratio))
+        scale = (2.0**0.75) * lax.rsqrt(norm)
+        for f in range(3):
+            fields[f, half_table] = records[:, part, f, :]
+        for p in range(PRIMS):
+            weight = jnp.exp2(jnp.log2(coefficients[p] * scale) * (1.0 / 3.0))
+            fields[3 + p, half_table] = exponents[p]
+            fields[6 + p, half_table] = weight * jnp.sqrt(roots[p])
+    spread_own(fields, left, core, col)
 
     def step(index, carry):
         half, block = index // NB, index % NB
         own = 2 * col + half
         needed = pattern[own, block] * pattern[block, row] * pattern[row, own]
+        rows = pl.ds(pl.multiple_of(block * BLOCK, BLOCK), BLOCK)
+        lanes = pl.ds(pl.multiple_of(half * BLOCK, BLOCK), BLOCK)
 
         @pl.when(needed != 0)
         def _():
-            half_tile(fields, left, tile, half, block)
-            lanes = pl.ds(pl.multiple_of((block % 2) * BLOCK, BLOCK), BLOCK)
-            acc[half] += product(iterate_row[block // 2, :, lanes], tile[...], 1)
+            half_tile(fields, left, tile, half, slot(core, block))
+            high[rows, lanes], low[rows, lanes] = split(tile[...].T)
+
+        @pl.when(needed == 0)
+        def _():
+            high[rows, lanes] = jnp.zeros((BLOCK, BLOCK), jnp.bfloat16)
+            low[rows, lanes] = jnp.zeros((BLOCK, BLOCK), jnp.bfloat16)
 
         return carry
 
     lax.fori_loop(0, 2 * NB, step, 0)
+
+
+def margin_kernel(place, pattern, fields, margin, left, tile):
+    row, col = place[0], place[1]
+    spread_own(fields, left, row % 2, col)
+    for half in range(2):
+        margin_live = pattern[row, 2 * col + half] != 0
+        lanes = slice(half * BLOCK, (half + 1) * BLOCK)
+
+        @pl.when(margin_live)
+        def _():
+            half_tile(fields, left, tile, half, slot(row % 2, row))
+            margin[:, lanes] = tile[...].T
+
+        @pl.when(jnp.logical_not(margin_live))
+        def _():
+            margin[:, lanes] = jnp.zeros((BLOCK, BLOCK), jnp.float32)
+
+
+def first_kernel(place, pattern, iterate_row, high, low, product_one):
+    total = contract([iterate_row[k] for k in range(16)], high, low)
     for copy in range(16):
-        product_one[copy, :, :BLOCK] = acc[0]
-        product_one[copy, :, BLOCK:] = acc[1]
+        product_one[copy] = total
 
 
 def replicate_kernel(place, pattern, value, copies):
@@ -206,16 +208,19 @@
     panel = VMEM((NB * BLOCK, 2 * BLOCK), jnp.bfloat16)
     tiles = jax.ShapeDtypeStruct((16, BLOCK, 2 * BLOCK), jnp.float32)
     iterate_col = lax.all_gather(iterate, "row", axis=0, tiled=True)
-    everyone = lax.all_gather(records, "row", axis=0)
-    iterate_row = exchange(jnp.broadcast_to(iterate[None], tiles.shape), "col")
+    cores = [[2 * z + core for z in range(16)] for core in range(2)]
+    partner = [(r, r ^ 1) for r in range(NB)]
     left = VMEM((2, FIELDS, BLOCK, BLOCK), jnp.float32)
     square = VMEM((BLOCK, BLOCK), jnp.float32)
-    acc = VMEM((2, BLOCK, BLOCK), jnp.float32)
-    table = jax.ShapeDtypeStruct((FIELDS, NB, BLOCK), jnp.float32)
-    fields, margin = call(margin_kernel, (table, tile), [left, square], place, pattern, everyone)
-    product_one = call(
-        first_kernel, tiles, [left, square, acc], place, pattern, fields, iterate_row, on_chip=(3,)
+    table = VMEM((FIELDS, NB, BLOCK), jnp.float32)
+    both = jnp.stack([records, lax.ppermute(records, "row", partner)])
+    everyone = lax.all_gather(both, "row", axis=0, axis_index_groups=cores)
+    iterate_row = exchange(jnp.broadcast_to(iterate[None], tiles.shape), "col")
+    fields, margin_high, margin_low = call(
+        tiles_kernel, (table, panel, panel), [left, square], place, pattern, everyone
     )
+    product_one = call(first_kernel, tiles, [], place, pattern, iterate_row, margin_high, margin_low, on_chip=(2, 3, 4))
+    margin = call(margin_kernel, tile, [left, square], place, pattern, fields, on_chip=(2,))
     one_row = exchange(product_one, "col")
     high, low = call(prepare_kernel, (panel, panel), [], place, pattern, iterate_col)
     half = VMEM((16, 8, BLOCK), jnp.float32)
@@ -223,10 +228,9 @@
     kept, given = call(
         second_kernel, (half, half), [turned], place, pattern, one_row, high, low, on_chip=(2, 3, 4)
     )
-    given = lax.ppermute(given, "row", [(r, r ^ 1) for r in range(NB)])
+    given = lax.ppermute(given, "row", partner)
     slices = jnp.stack([kept, given], axis=1)
     slices = exchange(slices, "col")
-    cores = [[2 * z + core for z in range(16)] for core in range(2)]
     slices = lax.all_to_all(slices, "row", 0, 0, tiled=True, axis_index_groups=cores)
     copies = VMEM((16,) + slices.shape, jnp.float32)
     slices = call(replicate_kernel, copies, [], place, pattern, slices, on_chip=(2,))

time: 193 us -> 202 us (1.047)
  the two profiles are of different devices: /device:TPU:1 before, /device:TPU:32 now
where the time goes in v5:
time: 202 us; the launch traced here: 201 us
  blocking collectives  76 us (38%)
  waiting for transfers between devices  45.3 us (22%)
  starting transfers between devices  26.3 us (13%)
  Pallas kernels  21 us (10%)
  local copies, waits for them, and re-layouts  17.9 us (9%)
  between operations  14.2 us (7%)
    all_to_all x3, waiting for transfers between devices, exchange(): return lax.all_to_all(pieces, axis, 0, 0, tiled=True)  37.6 us
    all_gather x1, blocking collectives, stages(): everyone = lax.all_gather(both, 'row', axis=0, axis_index_groups=cores)  35 us
    all_to_all x1, blocking collectives, stages(): lax.all_to_all(slices, 'row', 0, 0, tiled=True, axis_index_groups=cores)  27.8 us
    all_to_all x3, starting transfers between devices, exchange(): return lax.all_to_all(pieces, axis, 0, 0, tiled=True)  22.5 us
    pallas_call x7, Pallas kernels, call(): pl.pallas_call(kernel, out_shape=out_shapes, in_specs=[scalars, scalars]...  21 us
    unnamed x26, local copies, waits for them, and re-layouts  15.4 us
    all_to_all x1, blocking collectives, exchange(): return lax.all_to_all(pieces, axis, 0, 0, tiled=True)  13.3 us
    all_gather x1, waiting for transfers between devices, stages(): iterate_col = lax.all_gather(iterate, 'row', axis=0, tiled=True)  4.75 us
  transfers between devices with their start and end apart: 6, of which 5 were waited for; matrix products, arithmetic and copies ran while one was open for 1% of the time, Pallas kernels for 7%

profile of v5, /device:TPU:32, one launch (start us, length us, event | category | flops | bytes accessed | tf_op | source)
XLA Modules:
  0.0 200.9 jit_solution(13765279504930164145)
XLA Ops:
  7.2 0.0 all-gather.3.cloned.1.call-start
  7.2 0.7 all-gather.3.cloned.1.call-update
  7.9 2.5 %broadcast_in_dim.2 = f32[16,128,256]{2,1,0:T(8,128)} broadcast(f32[128,256]{1,0:T(8,128)} %iterate.1), dimensions={1,2} | broadcast | bytes 2228224 | tf_op jit(solution)/shard_map/broadcast_in_dim | solution.py:218
  10.4 0.0 copy-start.12
  10.4 0.0 copy-start.11
  10.4 7.2 %all-to-all-start = ((f32[16,128,256]{2,1,0:T(8,128)}), f32[16,128,256]{2,1,0:T(8,128)S(1)}, u32[]{:S(2)}, u32[]{:S(2)}) async-start(f32[16,128,256]{2,1,0:T(8,128)} %broadcast_in_dim.2), calls=%async_computation | async-start | bytes 4194304 | tf_op jit(solution)/shard_map/all_to_all | solution.py:186
  17.5 0.0 copy-done.12
  17.6 1.9 collective-permute-start
  19.5 0.1 pad_add_fusion.place
  19.6 1.1 collective-permute-done
  20.6 35.0 %all-gather = f32[32,9,128]{2,1,0:T(8,128)S(1)} all-gather(f32[2,9,128]{2,1,0:T(8,128)S(1)} %pad_maximum_fusion.1), channel_id=2, replica_groups={{0,32,64,96,128,160,192,224,256,288,320,352,384,416,448,480},{16,48,80,..., dimensions={0}, use_global_device_ids=true | all-gather | bytes 156672 | tf_op jit(solution)/shard_map/all_gather | solution.py:217
  55.6 0.0 copy-done.11
  55.6 7.8 %shard_map.50 = (f32[9,32,128]{2,1,0:T(8,128)S(1)}, bf16[4096,256]{1,0:T(8,128)(2,1)S(1)}, bf16[4096,256]{1,0:T(8,128)(2,1)S(1)}) custom-call(s32[2]{0:T(128)S(1)} %pad_add_fusion.place, s32[32,32]{1,0:T(8,128)S(1)} %copy-done.11, f32[16,2,9,128]{3,2,1,0:T(8,128)S(1)} %bitcast.7), custom_call_target="tpu_custom_call" | custom-call | tf_op jit(solution)/shard_map/pallas_call | solution.py:195
  63.4 0.0 copy-start.6
  63.4 1.4 copy-done.6
  64.8 0.0 copy-start.8
  64.8 1.4 copy-done.8
  66.2 0.0 all-to-all-done.iterate_row
  66.2 0.0 copy-start.7
  66.2 1.6 copy-done.7
  67.8 0.0 copy-start.9
  67.8 1.6 copy-done.9
  69.4 2.0 shard_map.52
  71.4 0.0 copy-start.4
  71.4 1.4 copy-done.4
  72.8 10.7 %all-to-all-start.1 = ((f32[16,128,256]{2,1,0:T(8,128)}), f32[16,128,256]{2,1,0:T(8,128)}, u32[]{:S(2)}, u32[]{:S(2)}) async-start(f32[16,128,256]{2,1,0:T(8,128)} %copy-done.4), calls=%async_computation.1 | async-start | bytes 4194304 | tf_op jit(solution)/shard_map/all_to_all | solution.py:186
  83.5 4.8 %all-gather.3.cloned.1.call-done.iterate_col = f32[4096,256]{1,0:T(8,128)} async-done(((f32[128,256]{1,0:T(8,128)}), f32[4096,256]{1,0:T(8,128)}) %all-gather.3.cloned.1.call-update) | async-done | bytes 4194320 | tf_op jit(solution)/shard_map/all_gather | solution.py:210
  88.3 0.0 copy-start.5
  88.3 2.2 %copy-done.5 = f32[4096,256]{1,0:T(8,128)S(1)} copy-done((f32[4096,256]{1,0:T(8,128)S(1)}, f32[4096,256]{1,0:T(8,128)}, u32[]{:S(2)}) %copy-start.5) | copy-done | bytes 4194328
  90.4 2.1 %shard_map.53 = (bf16[4096,256]{1,0:T(8,128)(2,1)S(1)}, bf16[4096,256]{1,0:T(8,128)(2,1)S(1)}) custom-call(s32[2]{0:T(128)S(1)} %pad_add_fusion.place, s32[32,32]{1,0:T(8,128)S(1)} %copy-done.11, f32[4096,256]{1,0:T(8,128)S(1)} %copy-done.5), custom_call_target="tpu_custom_call" | custom-call | tf_op jit(solution)/shard_map/pallas_call | solution.py:195
  92.5 0.0 copy-start
  92.5 1.3 copy-done
  93.8 12.2 %all-to-all-done.1.one_row = f32[16,128,256]{2,1,0:T(8,128)} async-done(((f32[16,128,256]{2,1,0:T(8,128)}), f32[16,128,256]{2,1,0:T(8,128)}, u32[]{:S(2)}, u32[]{:S(2)}) %all-to-all-start.1) | async-done | bytes 2097184 | tf_op jit(solution)/shard_map/all_to_all | solution.py:186
  106.0 1.6 copy-done.1
  107.6 2.8 %shard_map.54 = (f32[16,8,128]{2,1,0:T(8,128)S(1)}, f32[16,8,128]{2,1,0:T(8,128)S(1)}) custom-call(s32[2]{0:T(128)S(1)} %pad_add_fusion.place, s32[32,32]{1,0:T(8,128)S(1)} %copy-done.11, f32[16,128,256]{2,1,0:T(8,128)} %all-to-all-done.1.one_row, bf16[4096,256]{1,0:T(8,128)(2,1)S(1)} %get-tuple-element.12.high, bf16[4096,256]{1,0:T(8,128)(2,1)S(1)} %copy-done.1), custom_call_target="tpu_custom_call" | custom-call | tf_op jit(solution)/shard_map/pallas_call | solution.py:195
  110.4 1.9 collective-permute-start.1
  112.3 1.2 collective-permute-done.1
  113.6 13.3 %all_to_all.25 = f32[16,2,8,128]{3,2,1,0:T(8,128)S(1)} all-to-all(f32[16,2,8,128]{3,2,1,0:T(8,128)S(1)} %pad_maximum_fusion), channel_id=1, replica_groups=mesh['row'=32,'col'=16] {'col'}, dimensions={0} | all-to-all | bytes 262144 | tf_op jit(solution)/shard_map/all_to_all | solution.py:186
  126.9 27.8 %all_to_all.26.value = f32[16,2,8,128]{3,2,1,0:T(8,128)S(1)} all-to-all(f32[16,2,8,128]{3,2,1,0:T(8,128)S(1)} %all_to_all.25), channel_id=1, replica_groups={{0,32,64,96,128,160,192,224,256,288,320,352,384,416,448,480},{16,48,80,..., dimensions={0} | all-to-all | bytes 262144 | tf_op jit(solution)/shard_map/all_to_all | solution.py:234
  154.6 0.9 shard_map.55
  155.6 0.0 copy-start.3
  155.6 1.4 copy-done.3
  156.9 4.6 %all-to-all-start.4 = ((f32[16,16,2,8,128]{4,3,2,1,0:T(8,128)}), f32[16,16,2,8,128]{4,3,2,1,0:T(8,128)}, u32[]{:S(2)}, u32[]{:S(2)}) async-start(f32[16,16,2,8,128]{4,3,2,1,0:T(8,128)} %copy-done.3), calls=%async_computation.4 | async-start | bytes 4194304 | tf_op jit(solution)/shard_map/all_to_all | solution.py:186
  161.5 2.2 %shard_map.51 = f32[128,256]{1,0:T(8,128)} custom-call(s32[2]{0:T(128)S(1)} %pad_add_fusion.place, s32[32,32]{1,0:T(8,128)S(1)} %copy-done.11, f32[9,32,128]{2,1,0:T(8,128)S(1)} %get-tuple-element.9.fields), custom_call_target="tpu_custom_call" | custom-call | tf_op jit(solution)/shard_map/pallas_call | solution.py:195
  163.7 25.4 %all-to-all-done.4.two_row = f32[16,16,2,8,128]{4,3,2,1,0:T(8,128)} async-done(((f32[16,16,2,8,128]{4,3,2,1,0:T(8,128)}), f32[16,16,2,8,128]{4,3,2,1,0:T(8,128)}, u32[]{:S(2)}, u32[]{:S(2)}) %all-to-all-start.4) | async-done | bytes 2097184 | tf_op jit(solution)/shard_map/all_to_all | solution.py:186
  189.2 0.0 copy-done.10
  189.2 1.6 copy-done.2
  190.8 3.3 %shard_map.56 = f32[128,256]{1,0:T(8,128)} custom-call(s32[2]{0:T(128)S(1)} %pad_add_fusion.place, s32[32,32]{1,0:T(8,128)S(1)} %copy-done.11, f32[16,16,2,8,128]{4,3,2,1,0:T(8,128)} %all-to-all-done.4.two_row, bf16[4096,256]{1,0:T(8,128)(2,1)S(1)} %get-tuple-element.12.high, bf16[4096,256]{1,0:T(8,128)(2,1)S(1)} %copy-done.2, f32[128,256]{1,0:T(8,128)S(1)} %copy-done.10), custom_call_target="tpu_custom_call" | custom-call | tf_op jit(solution)/shard_map/pallas_call | solution.py:195
  (5 shorter events, 0.0 us)
Async XLA Ops:
  7.2 81.1 %all-gather.3.cloned.1.call-start = ((), (), s32[]{:S(2)}) async-start(), calls=%async_computation.5 | async-start | bytes 4325376 | tf_op jit(solution)/shard_map/all_gather | solution.py:210
  10.4 7.2 %copy-start.12 = (f32[9,128]{1,0:T(8,128)S(1)}, f32[9,128]{1,0:T(8,128)}, u32[]{:S(2)}) copy-start(f32[9,128]{1,0:T(8,128)} %param.3) | copy-start | bytes 13828
  10.4 45.2 %copy-start.11 = (s32[32,32]{1,0:T(8,128)S(1)}, s32[32,32]{1,0:T(8,128)}, u32[]{:S(2)}) copy-start(s32[32,32]{1,0:T(8,128)} %pattern.13) | copy-start | bytes 12292
  10.4 55.8 %all-to-all-start = ((f32[16,128,256]{2,1,0:T(8,128)}), f32[16,128,256]{2,1,0:T(8,128)S(1)}, u32[]{:S(2)}, u32[]{:S(2)}) async-start(f32[16,128,256]{2,1,0:T(8,128)} %broadcast_in_dim.2), calls=%async_computation | async-start | bytes 4194304 | tf_op jit(solution)/shard_map/all_to_all | solution.py:186
  17.6 3.1 %collective-permute-start = (f32[9,128]{1,0:T(8,128)S(1)}, f32[9,128]{1,0:T(8,128)S(1)}, u32[]{:S(2)}, u32[]{:S(2)}) collective-permute-start(f32[9,128]{1,0:T(8,128)S(1)} %copy-done.12), channel_id=1, source_target_pairs={{0,16},{16,0},{32,48},{48,32},{64,80},{80,64},{96,112},{112,96},{1... | collective-permute-start | bytes 13832 | tf_op jit(solution)/shard_map/ppermute | solution.py:216
  63.4 1.4 copy-start.6
  64.8 1.4 copy-start.8
  66.2 1.6 copy-start.7
  67.8 1.6 copy-start.9
  71.4 1.4 copy-start.4
  72.8 33.3 %all-to-all-start.1 = ((f32[16,128,256]{2,1,0:T(8,128)}), f32[16,128,256]{2,1,0:T(8,128)}, u32[]{:S(2)}, u32[]{:S(2)}) async-start(f32[16,128,256]{2,1,0:T(8,128)} %copy-done.4), calls=%async_computation.1 | async-start | bytes 4194304 | tf_op jit(solution)/shard_map/all_to_all | solution.py:186
  88.3 2.2 %copy-start.5 = (f32[4096,256]{1,0:T(8,128)S(1)}, f32[4096,256]{1,0:T(8,128)}, u32[]{:S(2)}) copy-start(f32[4096,256]{1,0:T(8,128)} %all-gather.3.cloned.1.call-done.iterate_col) | copy-start | bytes 12582916
  92.5 1.3 copy-start
  106.0 1.6 copy-start.1
  110.4 3.1 %collective-permute-start.1 = (f32[16,8,128]{2,1,0:T(8,128)S(1)}, f32[16,8,128]{2,1,0:T(8,128)S(1)}, u32[]{:S(2)}, u32[]{:S(2)}) collective-permute-start(f32[16,8,128]{2,1,0:T(8,128)S(1)} %get-tuple-element.15), channel_id=1, source_target_pairs={{0,16},{16,0},{32,48},{48,32},{64,80},{80,64},{96,112},{112,96},{1... | collective-permute-start | bytes 196616 | tf_op jit(solution)/shard_map/ppermute | solution.py:231
  155.6 1.4 copy-start.3
  156.9 32.2 %copy-start.10 = (f32[128,256]{1,0:T(8,128)S(1)}, f32[128,256]{1,0:T(8,128)}, u32[]{:S(2)}) copy-start(f32[128,256]{1,0:T(8,128)} %iterate.1) | copy-start | bytes 393220
  156.9 32.2 %all-to-all-start.4 = ((f32[16,16,2,8,128]{4,3,2,1,0:T(8,128)}), f32[16,16,2,8,128]{4,3,2,1,0:T(8,128)}, u32[]{:S(2)}, u32[]{:S(2)}) async-start(f32[16,16,2,8,128]{4,3,2,1,0:T(8,128)} %copy-done.3), calls=%async_computation.4 | async-start | bytes 4194304 | tf_op jit(solution)/shard_map/all_to_all | solution.py:186
  189.2 1.6 copy-start.2
Sparse Core Ops, SparseCore 0:
  10.1 78.1 all-gather.2

commit v6 on v5

--- a/solution.py
+++ b/solution.py
@@ -14,6 +14,7 @@
 LOG2E = 1.4426950408889634
 VMEM = pltpu.VMEM
 SMEM = pltpu.SMEM
+HBM = pltpu.HBM
 
 
 def split(value):
@@ -56,7 +57,15 @@
             left[half, f] = jnp.broadcast_to(own, (BLOCK, BLOCK)).T
 
 
-def tiles_kernel(place, pattern, records, fields, high, low, left, tile):
+def send_copies(tile, copies, sems):
+    moves = [pltpu.make_async_copy(tile, copies.at[k], sems.at[k]) for k in range(16)]
+    for move in moves:
+        move.start()
+    for move in moves:
+        move.wait()
+
+
+def first_kernel(place, pattern, records, iterate_row, fields, copies, left, tile, high, low, one, sems):
     row, col = place[0], place[1]
     core = row % 2
     for part in range(2):
@@ -98,6 +107,8 @@
         return carry
 
     lax.fori_loop(0, 2 * NB, step, 0)
+    one[...] = contract([iterate_row[k] for k in range(16)], high, low)
+    send_copies(one, copies, sems)
 
 
 def margin_kernel(place, pattern, fields, margin, left, tile):
@@ -117,13 +128,11 @@
             margin[:, lanes] = jnp.zeros((BLOCK, BLOCK), jnp.float32)
 
 
-def first_kernel(place, pattern, iterate_row, high, low, product_one):
-    total = contract([iterate_row[k] for k in range(16)], high, low)
-    for copy in range(16):
-        product_one[copy] = total
-
-
-def replicate_kernel(place, pattern, value, copies):
+def hbm_copies_kernel(value, copies, sems):
+    send_copies(value, copies, sems)
+
+
+def replicate_kernel(value, copies):
     for copy in range(copies.shape[0]):
         copies[copy] = value[...]
 
@@ -186,17 +195,22 @@
     return lax.all_to_all(pieces, axis, 0, 0, tiled=True)
 
 
-def call(kernel, out_shapes, scratch, *operands, on_chip=()):
+def call(kernel, out_shapes, scratch, *operands, on_chip=(), outs=None, scalars=2):
     whole = pl.BlockSpec(memory_space=VMEM)
-    scalars = pl.BlockSpec(memory_space=SMEM)
+    in_specs = [pl.BlockSpec(memory_space=SMEM)] * scalars + [whole] * (len(operands) - scalars)
     operands = list(operands)
     for k in on_chip:
         operands[k] = pltpu.with_memory_space_constraint(operands[k], VMEM)
+    if outs is None:
+        out_specs = jax.tree.map(lambda _: whole, out_shapes)
+    else:
+        out_specs = tuple(pl.BlockSpec(memory_space=space) for space in outs)
+        out_specs = out_specs if isinstance(out_shapes, tuple) else out_specs[0]
     return pl.pallas_call(
         kernel,
         out_shape=out_shapes,
-        in_specs=[scalars, scalars] + [whole] * (len(operands) - 2),
-        out_specs=jax.tree.map(lambda _: whole, out_shapes),
+        in_specs=in_specs,
+        out_specs=out_specs,
         scratch_shapes=scratch,
         compiler_params=pltpu.CompilerParams(vmem_limit_bytes=24 * 2**20),
     )(*operands)
@@ -206,7 +220,7 @@
     place = jnp.stack([lax.axis_index("row"), lax.axis_index("col")]).astype(jnp.int32)
     tile = jax.ShapeDtypeStruct((BLOCK, 2 * BLOCK), jnp.float32)
     panel = VMEM((NB * BLOCK, 2 * BLOCK), jnp.bfloat16)
-    tiles = jax.ShapeDtypeStruct((16, BLOCK, 2 * BLOCK), jnp.float32)
+    tiles = HBM((16, BLOCK, 2 * BLOCK), jnp.float32)
     iterate_col = lax.all_gather(iterate, "row", axis=0, tiled=True)
     cores = [[2 * z + core for z in range(16)] for core in range(2)]
     partner = [(r, r ^ 1) for r in range(NB)]
@@ -215,11 +229,20 @@
     table = VMEM((FIELDS, NB, BLOCK), jnp.float32)
     both = jnp.stack([records, lax.ppermute(records, "row", partner)])
     everyone = lax.all_gather(both, "row", axis=0, axis_index_groups=cores)
-    iterate_row = exchange(jnp.broadcast_to(iterate[None], tiles.shape), "col")
-    fields, margin_high, margin_low = call(
-        tiles_kernel, (table, panel, panel), [left, square], place, pattern, everyone
+    sems = pltpu.SemaphoreType.DMA((16,))
+    copies = call(hbm_copies_kernel, tiles, [sems], iterate, outs=(HBM,), scalars=0)
+    iterate_row = exchange(copies, "col")
+    fields, product_one = call(
+        first_kernel,
+        (table, tiles),
+        [left, square, panel, panel, VMEM((BLOCK, 2 * BLOCK), jnp.float32), sems],
+        place,
+        pattern,
+        everyone,
+        iterate_row,
+        on_chip=(2, 3),
+        outs=(VMEM, HBM),
     )
-    product_one = call(first_kernel, tiles, [], place, pattern, iterate_row, margin_high, margin_low, on_chip=(2, 3, 4))
     margin = call(margin_kernel, tile, [left, square], place, pattern, fields, on_chip=(2,))
     one_row = exchange(product_one, "col")
     high, low = call(prepare_kernel, (panel, panel), [], place, pattern, iterate_col)
@@ -233,7 +256,7 @@
     slices = exchange(slices, "col")
     slices = lax.all_to_all(slices, "row", 0, 0, tiled=True, axis_index_groups=cores)
     copies = VMEM((16,) + slices.shape, jnp.float32)
-    slices = call(replicate_kernel, copies, [], place, pattern, slices, on_chip=(2,))
+    slices = call(replicate_kernel, copies, [], slices, on_chip=(0,), scalars=0)
     two_row = exchange(slices, "col")
     updated = call(third_kernel, tile, [], place, pattern, two_row, high, low, iterate, on_chip=(2, 3, 4))
     return (margin, updated)

time: 202 us -> 194 us (0.960)
  local copies, waits for them, and re-layouts: 17.9 us -> 8.94 us
    all_gather x1, waiting for transfers between devices: 4.75 us -> 11.4 us  [stages(): iterate_col = lax.all_gather(iterate, 'row', axis=0, tiled=True)]
    all_to_all x3, waiting for transfers between devices: 37.6 us -> 31 us  [exchange(): return lax.all_to_all(pieces, axis, 0, 0, tiled=True)]
    unnamed x26 -> x18, local copies, waits for them, and re-layouts: 15.4 us -> 8.94 us
    broadcast_in_dim x1 -> x0, local copies, waits for them, and re-layouts: 2.47 us -> none  [stages(): iterate_row = exchange(jnp.broadcast_to(iterate[None], tiles.shape), 'col')]
  transfers between devices with their start and end apart: 6 -> 6, of which waited for: 5 -> 5; matrix products, arithmetic and copies ran while one was open for 1% -> 0% of each run, Pallas kernels for 7% -> 8%
where the time goes in v6:
time: 194 us; the launch traced here: 193 us
  blocking collectives  76.3 us (39%)
  waiting for transfers between devices  45.3 us (23%)
  starting transfers between devices  26.1 us (13%)
  Pallas kernels  22.1 us (11%)
  between operations  14.2 us (7%)
  local copies, waits for them, and re-layouts  8.94 us (5%)
    all_gather x1, blocking collectives, stages(): everyone = lax.all_gather(both, 'row', axis=0, axis_index_groups=cores)  35.3 us
    all_to_all x3, waiting for transfers between devices, exchange(): return lax.all_to_all(pieces, axis, 0, 0, tiled=True)  31 us
    all_to_all x1, blocking collectives, stages(): lax.all_to_all(slices, 'row', 0, 0, tiled=True, axis_index_groups=cores)  27.7 us
    all_to_all x3, starting transfers between devices, exchange(): return lax.all_to_all(pieces, axis, 0, 0, tiled=True)  22.2 us
    pallas_call x7, Pallas kernels, call(): pl.pallas_call(kernel, out_shape=out_shapes, in_specs=in_specs, out_specs...  22.1 us
    all_to_all x1, blocking collectives, exchange(): return lax.all_to_all(pieces, axis, 0, 0, tiled=True)  13.3 us
    all_gather x1, waiting for transfers between devices, stages(): iterate_col = lax.all_gather(iterate, 'row', axis=0, tiled=True)  11.4 us
    unnamed x18, local copies, waits for them, and re-layouts  8.94 us
  transfers between devices with their start and end apart: 6, of which 5 were waited for; matrix products, arithmetic and copies ran while one was open for 0% of the time, Pallas kernels for 8%

profile of v6, /device:TPU:32, one launch (start us, length us, event | category | flops | bytes accessed | tf_op | source)
XLA Modules:
  0.0 193.0 jit_solution(10726409416383837452)
XLA Ops:
  7.2 0.0 all-gather.3.cloned.1.call-start
  7.2 0.7 all-gather.3.cloned.1.call-update
  7.9 0.0 copy-start.5
  7.9 0.9 copy-done.5
  8.8 1.5 shard_map.50
  10.3 0.0 copy-start.8
  10.3 0.0 copy-start.7
  10.3 7.0 %all-to-all-start = ((f32[16,128,256]{2,1,0:T(8,128)}), f32[16,128,256]{2,1,0:T(8,128)S(1)}, u32[]{:S(2)}, u32[]{:S(2)}) async-start(f32[16,128,256]{2,1,0:T(8,128)} %shard_map.50), calls=%async_computation | async-start | bytes 4194304 | tf_op jit(solution)/shard_map/all_to_all | solution.py:195
  17.4 0.0 copy-done.8
  17.4 1.9 collective-permute-start
  19.3 0.1 pad_add_fusion.place
  19.4 1.1 collective-permute-done
  20.5 35.3 %all-gather = f32[32,9,128]{2,1,0:T(8,128)S(1)} all-gather(f32[2,9,128]{2,1,0:T(8,128)S(1)} %pad_maximum_fusion.1), channel_id=2, replica_groups={{0,32,64,96,128,160,192,224,256,288,320,352,384,416,448,480},{16,48,80,..., dimensions={0}, use_global_device_ids=true | all-gather | bytes 156672 | tf_op jit(solution)/shard_map/all_gather | solution.py:231
  55.7 0.0 all-to-all-done.iterate_row
  55.7 0.0 copy-done.7
  55.7 10.1 %shard_map.51 = (f32[9,32,128]{2,1,0:T(8,128)S(1)}, f32[16,128,256]{2,1,0:T(8,128)}) custom-call(s32[2]{0:T(128)S(1)} %pad_add_fusion.place, s32[32,32]{1,0:T(8,128)S(1)} %copy-done.7, f32[16,2,9,128]{3,2,1,0:T(8,128)S(1)} %bitcast.7, f32[16,128,256]{2,1,0:T(8,128)S(1)} %all-to-all-done.iterate_row), custom_call_target="tpu_custom_call" | custom-call | tf_op jit(solution)/shard_map/pallas_call | solution.py:209
  65.9 10.6 %all-to-all-start.1 = ((f32[16,128,256]{2,1,0:T(8,128)}), f32[16,128,256]{2,1,0:T(8,128)}, u32[]{:S(2)}, u32[]{:S(2)}) async-start(f32[16,128,256]{2,1,0:T(8,128)} %get-tuple-element.9), calls=%async_computation.1 | async-start | bytes 4194304 | tf_op jit(solution)/shard_map/all_to_all | solution.py:195
  76.5 11.4 %all-gather.3.cloned.1.call-done.iterate_col = f32[4096,256]{1,0:T(8,128)} async-done(((f32[128,256]{1,0:T(8,128)}), f32[4096,256]{1,0:T(8,128)}) %all-gather.3.cloned.1.call-update) | async-done | bytes 4194320 | tf_op jit(solution)/shard_map/all_gather | solution.py:224
  87.9 0.0 copy-start.4
  87.9 2.2 %copy-done.4 = f32[4096,256]{1,0:T(8,128)S(1)} copy-done((f32[4096,256]{1,0:T(8,128)S(1)}, f32[4096,256]{1,0:T(8,128)}, u32[]{:S(2)}) %copy-start.4) | copy-done | bytes 4194328
  90.1 2.1 %shard_map.53 = (bf16[4096,256]{1,0:T(8,128)(2,1)S(1)}, bf16[4096,256]{1,0:T(8,128)(2,1)S(1)}) custom-call(s32[2]{0:T(128)S(1)} %pad_add_fusion.place, s32[32,32]{1,0:T(8,128)S(1)} %copy-done.7, f32[4096,256]{1,0:T(8,128)S(1)} %copy-done.4), custom_call_target="tpu_custom_call" | custom-call | tf_op jit(solution)/shard_map/pallas_call | solution.py:209
  92.1 0.0 copy-start
  92.2 1.3 copy-done
  93.5 5.6 %all-to-all-done.1.one_row = f32[16,128,256]{2,1,0:T(8,128)} async-done(((f32[16,128,256]{2,1,0:T(8,128)}), f32[16,128,256]{2,1,0:T(8,128)}, u32[]{:S(2)}, u32[]{:S(2)}) %all-to-all-start.1) | async-done | bytes 2097184 | tf_op jit(solution)/shard_map/all_to_all | solution.py:195
  99.0 0.0 copy-start.1
  99.0 1.6 copy-done.1
  100.6 2.8 %shard_map.54 = (f32[16,8,128]{2,1,0:T(8,128)S(1)}, f32[16,8,128]{2,1,0:T(8,128)S(1)}) custom-call(s32[2]{0:T(128)S(1)} %pad_add_fusion.place, s32[32,32]{1,0:T(8,128)S(1)} %copy-done.7, f32[16,128,256]{2,1,0:T(8,128)} %all-to-all-done.1.one_row, bf16[4096,256]{1,0:T(8,128)(2,1)S(1)} %get-tuple-element.10.high, bf16[4096,256]{1,0:T(8,128)(2,1)S(1)} %copy-done.1), custom_call_target="tpu_custom_call" | custom-call | tf_op jit(solution)/shard_map/pallas_call | solution.py:209
  103.4 1.9 collective-permute-start.1
  105.3 1.2 collective-permute-done.1
  106.6 13.3 %all_to_all.25 = f32[16,2,8,128]{3,2,1,0:T(8,128)S(1)} all-to-all(f32[16,2,8,128]{3,2,1,0:T(8,128)S(1)} %pad_maximum_fusion), channel_id=1, replica_groups=mesh['row'=32,'col'=16] {'col'}, dimensions={0} | all-to-all | bytes 262144 | tf_op jit(solution)/shard_map/all_to_all | solution.py:195
  119.8 27.7 %all_to_all.26.value = f32[16,2,8,128]{3,2,1,0:T(8,128)S(1)} all-to-all(f32[16,2,8,128]{3,2,1,0:T(8,128)S(1)} %all_to_all.25), channel_id=1, replica_groups={{0,32,64,96,128,160,192,224,256,288,320,352,384,416,448,480},{16,48,80,..., dimensions={0} | all-to-all | bytes 262144 | tf_op jit(solution)/shard_map/all_to_all | solution.py:257
  147.6 0.1 shard_map.55
  147.7 0.0 copy-start.3
  147.7 1.3 copy-done.3
  149.1 0.0 copy-start.6
  149.1 4.6 %all-to-all-start.4 = ((f32[16,16,2,8,128]{4,3,2,1,0:T(8,128)}), f32[16,16,2,8,128]{4,3,2,1,0:T(8,128)}, u32[]{:S(2)}, u32[]{:S(2)}) async-start(f32[16,16,2,8,128]{4,3,2,1,0:T(8,128)} %copy-done.3), calls=%async_computation.4 | async-start | bytes 4194304 | tf_op jit(solution)/shard_map/all_to_all | solution.py:195
  153.6 2.2 %shard_map.52 = f32[128,256]{1,0:T(8,128)} custom-call(s32[2]{0:T(128)S(1)} %pad_add_fusion.place, s32[32,32]{1,0:T(8,128)S(1)} %copy-done.7, f32[9,32,128]{2,1,0:T(8,128)S(1)} %get-tuple-element.8.fields), custom_call_target="tpu_custom_call" | custom-call | tf_op jit(solution)/shard_map/pallas_call | solution.py:209
  155.9 25.4 %all-to-all-done.4.two_row = f32[16,16,2,8,128]{4,3,2,1,0:T(8,128)} async-done(((f32[16,16,2,8,128]{4,3,2,1,0:T(8,128)}), f32[16,16,2,8,128]{4,3,2,1,0:T(8,128)}, u32[]{:S(2)}, u32[]{:S(2)}) %all-to-all-start.4) | async-done | bytes 2097184 | tf_op jit(solution)/shard_map/all_to_all | solution.py:195
  181.3 0.0 copy-done.6
  181.3 0.0 copy-start.2
  181.3 1.6 copy-done.2
  182.9 3.3 %shard_map.56 = f32[128,256]{1,0:T(8,128)} custom-call(s32[2]{0:T(128)S(1)} %pad_add_fusion.place, s32[32,32]{1,0:T(8,128)S(1)} %copy-done.7, f32[16,16,2,8,128]{4,3,2,1,0:T(8,128)} %all-to-all-done.4.two_row, bf16[4096,256]{1,0:T(8,128)(2,1)S(1)} %get-tuple-element.10.high, bf16[4096,256]{1,0:T(8,128)(2,1)S(1)} %copy-done.2, f32[128,256]{1,0:T(8,128)S(1)} %copy-done.6), custom_call_target="tpu_custom_call" | custom-call | tf_op jit(solution)/shard_map/pallas_call | solution.py:209
  (2 shorter events, 0.0 us)
Async XLA Ops:
  7.2 80.7 %all-gather.3.cloned.1.call-start = ((), (), s32[]{:S(2)}) async-start(), calls=%async_computation.5 | async-start | bytes 4325376 | tf_op jit(solution)/shard_map/all_gather | solution.py:224
  7.9 0.9 copy-start.5
  10.3 7.1 %copy-start.8 = (f32[9,128]{1,0:T(8,128)S(1)}, f32[9,128]{1,0:T(8,128)}, u32[]{:S(2)}) copy-start(f32[9,128]{1,0:T(8,128)} %param.3) | copy-start | bytes 13828
  10.3 45.4 %copy-start.7 = (s32[32,32]{1,0:T(8,128)S(1)}, s32[32,32]{1,0:T(8,128)}, u32[]{:S(2)}) copy-start(s32[32,32]{1,0:T(8,128)} %pattern.9) | copy-start | bytes 12292
  10.3 45.4 %all-to-all-start = ((f32[16,128,256]{2,1,0:T(8,128)}), f32[16,128,256]{2,1,0:T(8,128)S(1)}, u32[]{:S(2)}, u32[]{:S(2)}) async-start(f32[16,128,256]{2,1,0:T(8,128)} %shard_map.50), calls=%async_computation | async-start | bytes 4194304 | tf_op jit(solution)/shard_map/all_to_all | solution.py:195
  17.4 3.1 %collective-permute-start = (f32[9,128]{1,0:T(8,128)S(1)}, f32[9,128]{1,0:T(8,128)S(1)}, u32[]{:S(2)}, u32[]{:S(2)}) collective-permute-start(f32[9,128]{1,0:T(8,128)S(1)} %copy-done.8), channel_id=1, source_target_pairs={{0,16},{16,0},{32,48},{48,32},{64,80},{80,64},{96,112},{112,96},{1... | collective-permute-start | bytes 13832 | tf_op jit(solution)/shard_map/ppermute | solution.py:230
  65.9 33.2 %all-to-all-start.1 = ((f32[16,128,256]{2,1,0:T(8,128)}), f32[16,128,256]{2,1,0:T(8,128)}, u32[]{:S(2)}, u32[]{:S(2)}) async-start(f32[16,128,256]{2,1,0:T(8,128)} %get-tuple-element.9), calls=%async_computation.1 | async-start | bytes 4194304 | tf_op jit(solution)/shard_map/all_to_all | solution.py:195
  87.9 2.2 %copy-start.4 = (f32[4096,256]{1,0:T(8,128)S(1)}, f32[4096,256]{1,0:T(8,128)}, u32[]{:S(2)}) copy-start(f32[4096,256]{1,0:T(8,128)} %all-gather.3.cloned.1.call-done.iterate_col) | copy-start | bytes 12582916
  92.1 1.3 copy-start
  99.0 1.6 copy-start.1
  103.4 3.1 %collective-permute-start.1 = (f32[16,8,128]{2,1,0:T(8,128)S(1)}, f32[16,8,128]{2,1,0:T(8,128)S(1)}, u32[]{:S(2)}, u32[]{:S(2)}) collective-permute-start(f32[16,8,128]{2,1,0:T(8,128)S(1)} %get-tuple-element.13), channel_id=1, source_target_pairs={{0,16},{16,0},{32,48},{48,32},{64,80},{80,64},{96,112},{112,96},{1... | collective-permute-start | bytes 196616 | tf_op jit(solution)/shard_map/ppermute | solution.py:254
  147.7 1.3 copy-start.3
  149.1 32.2 %copy-start.6 = (f32[128,256]{1,0:T(8,128)S(1)}, f32[128,256]{1,0:T(8,128)}, u32[]{:S(2)}) copy-start(f32[128,256]{1,0:T(8,128)} %iterate.1) | copy-start | bytes 393220
  149.1 32.2 %all-to-all-start.4 = ((f32[16,16,2,8,128]{4,3,2,1,0:T(8,128)}), f32[16,16,2,8,128]{4,3,2,1,0:T(8,128)}, u32[]{:S(2)}, u32[]{:S(2)}) async-start(f32[16,16,2,8,128]{4,3,2,1,0:T(8,128)} %copy-done.3), calls=%async_computation.4 | async-start | bytes 4194304 | tf_op jit(solution)/shard_map/all_to_all | solution.py:195
  181.3 1.6 copy-start.2
Sparse Core Ops, SparseCore 0:
  10.1 77.7 all-gather.2

commit v7 on v6

--- a/solution.py
+++ b/solution.py
@@ -10,7 +10,9 @@
 PRIMS = 3
 NB = 32
 FIELDS = 3 + 2 * PRIMS
-CHUNK = 64
+CHUNK = 128
+PANEL = 512
+PART = 1024
 LOG2E = 1.4426950408889634
 VMEM = pltpu.VMEM
 SMEM = pltpu.SMEM
@@ -21,6 +23,10 @@
     high = value.astype(jnp.bfloat16)
     low = (value - high.astype(jnp.float32)).astype(jnp.bfloat16)
     return high, low
+
+
+def dot_transposed(left, right):
+    return lax.dot_general(left, right, (((1,), (1,)), ((), ())), preferred_element_type=jnp.float32)
 
 
 def half_tile(fields_ref, left_ref, tile_ref, half, block):
@@ -97,17 +103,24 @@
         @pl.when(needed != 0)
         def _():
             half_tile(fields, left, tile, half, slot(core, block))
-            high[rows, lanes], low[rows, lanes] = split(tile[...].T)
+            high[lanes, rows], low[lanes, rows] = split(tile[...])
 
         @pl.when(needed == 0)
         def _():
-            high[rows, lanes] = jnp.zeros((BLOCK, BLOCK), jnp.bfloat16)
-            low[rows, lanes] = jnp.zeros((BLOCK, BLOCK), jnp.bfloat16)
+            high[lanes, rows] = jnp.zeros((BLOCK, BLOCK), jnp.bfloat16)
+            low[lanes, rows] = jnp.zeros((BLOCK, BLOCK), jnp.bfloat16)
 
         return carry
 
     lax.fori_loop(0, 2 * NB, step, 0)
-    one[...] = contract([iterate_row[k] for k in range(16)], high, low)
+    total = jnp.zeros((BLOCK, 2 * BLOCK), jnp.float32)
+    for k in range(16):
+        columns = slice(2 * BLOCK * k, 2 * BLOCK * (k + 1))
+        piece_high, piece_low = split(iterate_row[k])
+        total = total + dot_transposed(piece_high, high[:, columns])
+        total = total + dot_transposed(piece_high, low[:, columns])
+        total = total + dot_transposed(piece_low, high[:, columns])
+    one[...] = total
     send_copies(one, copies, sems)
 
 
@@ -139,16 +152,13 @@
 
 def prepare_kernel(place, pattern, iterate_col, high, low):
     col = place[1]
-
-    def step(block, carry):
-        rows = pl.ds(pl.multiple_of(block * BLOCK, BLOCK), BLOCK)
+    first = pl.program_id(0) * (PANEL // BLOCK)
+    for block in range(PANEL // BLOCK):
+        rows = slice(block * BLOCK, (block + 1) * BLOCK)
         for half in range(2):
             lanes = slice(half * BLOCK, (half + 1) * BLOCK)
-            mask = (pattern[block, 2 * col + half] != 0).astype(jnp.float32)
+            mask = live(pattern, first + block, 2 * col + half)
             high[rows, lanes], low[rows, lanes] = split(mask * iterate_col[rows, lanes])
-        return carry
-
-    lax.fori_loop(0, NB, step, 0)
 
 
 def contract(pieces, high, low):
@@ -166,15 +176,28 @@
     return (pattern[row, column] != 0).astype(jnp.float32)
 
 
-def second_kernel(place, pattern, one_row, high, low, kept, given, tile):
+def second_kernel(place, pattern, one_row, high, low, kept, given, total, tile):
     row, col = place[0], place[1]
-    total = contract([one_row[k] for k in range(16)], high, low)
-    for half in range(2):
-        own = total[:, half * BLOCK : (half + 1) * BLOCK]
-        tile[half] = (live(pattern, row, 2 * col + half) * own).T
-    core = row % 2
-    kept[...] = tile[core].reshape(BLOCK // 8, 8, BLOCK)
-    given[...] = tile[1 - core].reshape(BLOCK // 8, 8, BLOCK)
+    part = pl.program_id(0)
+    pieces = PART // (2 * BLOCK)
+    product = contract([one_row[part * pieces + k] for k in range(pieces)], high, low)
+
+    @pl.when(part == 0)
+    def _():
+        total[...] = product
+
+    @pl.when(part > 0)
+    def _():
+        total[...] += product
+
+    @pl.when(part == pl.num_programs(0) - 1)
+    def _():
+        for half in range(2):
+            own = total[:, half * BLOCK : (half + 1) * BLOCK]
+            tile[half] = (live(pattern, row, 2 * col + half) * own).T
+        core = row % 2
+        kept[...] = tile[core].reshape(BLOCK // 8, 8, BLOCK)
+        given[...] = tile[1 - core].reshape(BLOCK // 8, 8, BLOCK)
 
 
 def third_kernel(place, pattern, two_row, high, low, iterate, updated):
@@ -195,20 +218,32 @@
     return lax.all_to_all(pieces, axis, 0, 0, tiled=True)
 
 
-def call(kernel, out_shapes, scratch, *operands, on_chip=(), outs=None, scalars=2):
+def call(kernel, out_shapes, scratch, *operands, on_chip=(), outs=None, scalars=2, grid=(), blocks=None, source=VMEM, stay=()):
     whole = pl.BlockSpec(memory_space=VMEM)
-    in_specs = [pl.BlockSpec(memory_space=SMEM)] * scalars + [whole] * (len(operands) - scalars)
+    in_specs = [pl.BlockSpec(memory_space=SMEM)] * scalars + [pl.BlockSpec(memory_space=source)] * (
+        len(operands) - scalars
+    )
+    blocks = blocks or {}
+    for k, block in blocks.items():
+        if k < len(operands):
+            in_specs[k] = pl.BlockSpec(block, lambda i: (i, 0))
     operands = list(operands)
     for k in on_chip:
         operands[k] = pltpu.with_memory_space_constraint(operands[k], VMEM)
+    for k in stay:
+        operands[k] = pltpu.with_memory_space_constraint(operands[k], HBM)
     if outs is None:
         out_specs = jax.tree.map(lambda _: whole, out_shapes)
     else:
-        out_specs = tuple(pl.BlockSpec(memory_space=space) for space in outs)
+        out_specs = tuple(
+            pl.BlockSpec(space, lambda i: (i, 0)) if isinstance(space, tuple) else pl.BlockSpec(memory_space=space)
+            for space in outs
+        )
         out_specs = out_specs if isinstance(out_shapes, tuple) else out_specs[0]
     return pl.pallas_call(
         kernel,
         out_shape=out_shapes,
+        grid=grid,
         in_specs=in_specs,
         out_specs=out_specs,
         scratch_shapes=scratch,
@@ -219,7 +254,7 @@
 def stages(records, pattern, iterate):
     place = jnp.stack([lax.axis_index("row"), lax.axis_index("col")]).astype(jnp.int32)
     tile = jax.ShapeDtypeStruct((BLOCK, 2 * BLOCK), jnp.float32)
-    panel = VMEM((NB * BLOCK, 2 * BLOCK), jnp.bfloat16)
+    stored = HBM((NB * BLOCK, 2 * BLOCK), jnp.bfloat16)
     tiles = HBM((16, BLOCK, 2 * BLOCK), jnp.float32)
     iterate_col = lax.all_gather(iterate, "row", axis=0, tiled=True)
     cores = [[2 * z + core for z in range(16)] for core in range(2)]
@@ -230,12 +265,15 @@
     both = jnp.stack([records, lax.ppermute(records, "row", partner)])
     everyone = lax.all_gather(both, "row", axis=0, axis_index_groups=cores)
     sems = pltpu.SemaphoreType.DMA((16,))
-    copies = call(hbm_copies_kernel, tiles, [sems], iterate, outs=(HBM,), scalars=0)
+    wide = VMEM((2 * BLOCK, NB * BLOCK), jnp.bfloat16)
+    copies = call(
+        hbm_copies_kernel, tiles, [sems], iterate, outs=(HBM,), scalars=0, source=HBM, stay=(0,)
+    )
     iterate_row = exchange(copies, "col")
     fields, product_one = call(
         first_kernel,
         (table, tiles),
-        [left, square, panel, panel, VMEM((BLOCK, 2 * BLOCK), jnp.float32), sems],
+        [left, square, wide, wide, VMEM((BLOCK, 2 * BLOCK), jnp.float32), sems],
         place,
         pattern,
         everyone,
@@ -245,11 +283,35 @@
     )
     margin = call(margin_kernel, tile, [left, square], place, pattern, fields, on_chip=(2,))
     one_row = exchange(product_one, "col")
-    high, low = call(prepare_kernel, (panel, panel), [], place, pattern, iterate_col)
+    window = (PANEL, 2 * BLOCK)
+    high, low = call(
+        prepare_kernel,
+        (stored, stored),
+        [],
+        place,
+        pattern,
+        iterate_col,
+        outs=(window, window),
+        grid=(NB * BLOCK // PANEL,),
+        blocks={2: window},
+        stay=(2,),
+    )
     half = VMEM((16, 8, BLOCK), jnp.float32)
     turned = VMEM((2, BLOCK, BLOCK), jnp.float32)
+    window = (PART, 2 * BLOCK)
     kept, given = call(
-        second_kernel, (half, half), [turned], place, pattern, one_row, high, low, on_chip=(2, 3, 4)
+        second_kernel,
+        (half, half),
+        [VMEM((BLOCK, 2 * BLOCK), jnp.float32), turned],
+        place,
+        pattern,
+        one_row,
+        high,
+        low,
+        on_chip=(2,),
+        grid=(NB * BLOCK // PART,),
+        blocks={3: window, 4: window},
+        stay=(3, 4),
     )
     given = lax.ppermute(given, "row", partner)
     slices = jnp.stack([kept, given], axis=1)

time: 194 us -> 252 us (1.30)
  the two profiles are of different devices: /device:TPU:32 before, /device:TPU:1 now
where the time goes in v7:
time: 252 us; the launch traced here: 248 us
  Pallas kernels  95.2 us (38%)
  blocking collectives  63.3 us (25%)
  waiting for transfers between devices  40.7 us (16%)
  starting transfers between devices  31.4 us (12%)
  between operations  14.1 us (6%)
  local copies, waits for them, and re-layouts  2.92 us (1%)
    pallas_call x7, Pallas kernels, call(): pl.pallas_call(kernel, out_shape=out_shapes, grid=grid, in_specs=in_specs...  95.2 us
    all_to_all x3, waiting for transfers between devices, exchange(): return lax.all_to_all(pieces, axis, 0, 0, tiled=True)  38.4 us
    all_gather x1, blocking collectives, stages(): everyone = lax.all_gather(both, 'row', axis=0, axis_index_groups=cores)  29.3 us
    all_to_all x1, blocking collectives, stages(): lax.all_to_all(slices, 'row', 0, 0, tiled=True, axis_index_groups=cores)  22 us
    all_to_all x3, starting transfers between devices, exchange(): return lax.all_to_all(pieces, axis, 0, 0, tiled=True)  17.8 us
    all_to_all x1, blocking collectives, exchange(): return lax.all_to_all(pieces, axis, 0, 0, tiled=True)  11.9 us
    ppermute x1, starting transfers between devices, stages(): given = lax.ppermute(given, 'row', partner)  8.64 us
  transfers between devices with their start and end apart: 6, of which 4 were waited for; matrix products, arithmetic and copies ran while one was open for 0% of the time, Pallas kernels for 35%

profile of v7, /device:TPU:1, one launch (start us, length us, event | category | flops | bytes accessed | tf_op | source)
XLA Modules:
  0.0 247.7 jit_solution(4431500523565732908)
XLA Ops:
  7.2 0.0 all-gather.3.cloned.1.call-start
  7.2 0.7 all-gather.3.cloned.1.call-update
  7.9 64.8 %shard_map.50 = f32[16,128,256]{2,1,0:T(8,128)} custom-call(f32[128,256]{1,0:T(8,128)} %iterate.1), custom_call_target="tpu_custom_call" | custom-call | tf_op jit(solution)/shard_map/pallas_call | solution.py:243
  72.7 0.0 copy-start.5
  72.7 0.0 copy-start.4
  72.7 7.6 %all-to-all-start = ((f32[16,128,256]{2,1,0:T(8,128)}), f32[16,128,256]{2,1,0:T(8,128)S(1)}, u32[]{:S(2)}, u32[]{:S(2)}) async-start(f32[16,128,256]{2,1,0:T(8,128)} %shard_map.50), calls=%async_computation | async-start | bytes 4194304 | tf_op jit(solution)/shard_map/all_to_all | solution.py:218
  80.3 0.0 copy-done.5
  80.3 4.9 %collective-permute-start = (f32[9,128]{1,0:T(8,128)S(1)}, f32[9,128]{1,0:T(8,128)S(1)}, u32[]{:S(2)}, u32[]{:S(2)}) collective-permute-start(f32[9,128]{1,0:T(8,128)S(1)} %copy-done.5), channel_id=1, source_target_pairs={{0,16},{16,0},{32,48},{48,32},{64,80},{80,64},{96,112},{112,96},{1... | collective-permute-start | bytes 13832 | tf_op jit(solution)/shard_map/ppermute | solution.py:265
  85.2 0.1 pad_add_fusion.place
  85.3 0.7 collective-permute-done
  86.0 29.3 %all-gather = f32[32,9,128]{2,1,0:T(8,128)S(1)} all-gather(f32[2,9,128]{2,1,0:T(8,128)S(1)} %pad_maximum_fusion.1), channel_id=2, replica_groups={{0,32,64,96,128,160,192,224,256,288,320,352,384,416,448,480},{16,48,80,..., dimensions={0}, use_global_device_ids=true | all-gather | bytes 156672 | tf_op jit(solution)/shard_map/all_gather | solution.py:266
  115.3 0.0 all-to-all-done.iterate_row
  115.3 0.0 copy-done.4
  115.3 13.6 %shard_map.51 = (f32[9,32,128]{2,1,0:T(8,128)S(1)}, f32[16,128,256]{2,1,0:T(8,128)}) custom-call(s32[2]{0:T(128)S(1)} %pad_add_fusion.place, s32[32,32]{1,0:T(8,128)S(1)} %copy-done.4, f32[16,2,9,128]{3,2,1,0:T(8,128)S(1)} %bitcast.7, f32[16,128,256]{2,1,0:T(8,128)S(1)} %all-to-all-done.iterate_row), custom_call_target="tpu_custom_call" | custom-call | tf_op jit(solution)/shard_map/pallas_call | solution.py:243
  128.9 5.6 %all-to-all-start.1 = ((f32[16,128,256]{2,1,0:T(8,128)}), f32[16,128,256]{2,1,0:T(8,128)S(1)}, u32[]{:S(2)}, u32[]{:S(2)}) async-start(f32[16,128,256]{2,1,0:T(8,128)} %get-tuple-element.9), calls=%async_computation.1 | async-start | bytes 4194304 | tf_op jit(solution)/shard_map/all_to_all | solution.py:218
  134.6 0.0 all-gather.3.cloned.1.call-done.iterate_col
  134.6 7.0 %shard_map.53 = (bf16[4096,256]{1,0:T(8,128)(2,1)}, bf16[4096,256]{1,0:T(8,128)(2,1)}) custom-call(s32[2]{0:T(128)S(1)} %pad_add_fusion.place, s32[32,32]{1,0:T(8,128)S(1)} %copy-done.4, f32[4096,256]{1,0:T(8,128)} %all-gather.3.cloned.1.call-done.iterate_col), custom_call_target="tpu_custom_call" | custom-call | tf_op jit(solution)/shard_map/pallas_call | solution.py:243
  141.6 15.9 %all-to-all-done.1.one_row = f32[16,128,256]{2,1,0:T(8,128)S(1)} async-done(((f32[16,128,256]{2,1,0:T(8,128)}), f32[16,128,256]{2,1,0:T(8,128)S(1)}, u32[]{:S(2)}, u32[]{:S(2)}) %all-to-all-start.1) | async-done | bytes 2097184 | tf_op jit(solution)/shard_map/all_to_all | solution.py:218
  157.5 3.9 %shard_map.54 = (f32[16,8,128]{2,1,0:T(8,128)S(1)}, f32[16,8,128]{2,1,0:T(8,128)S(1)}) custom-call(s32[2]{0:T(128)S(1)} %pad_add_fusion.place, s32[32,32]{1,0:T(8,128)S(1)} %copy-done.4, f32[16,128,256]{2,1,0:T(8,128)S(1)} %all-to-all-done.1.one_row, bf16[4096,256]{1,0:T(8,128)(2,1)} %get-tuple-element.10.high, bf16[4096,256]{1,0:T(8,128)(2,1)} %get-tuple-element.11.low), custom_call_target="tpu_custom_call" | custom-call | tf_op jit(solution)/shard_map/pallas_call | solution.py:243
  161.4 8.6 %collective-permute-start.1 = (f32[16,8,128]{2,1,0:T(8,128)S(1)}, f32[16,8,128]{2,1,0:T(8,128)S(1)}, u32[]{:S(2)}, u32[]{:S(2)}) collective-permute-start(f32[16,8,128]{2,1,0:T(8,128)S(1)} %get-tuple-element.13), channel_id=1, source_target_pairs={{0,16},{16,0},{32,48},{48,32},{64,80},{80,64},{96,112},{112,96},{1... | collective-permute-start | bytes 196616 | tf_op jit(solution)/shard_map/ppermute | solution.py:316
  170.0 0.9 collective-permute-done.1
  170.9 11.9 %all_to_all.25 = f32[16,2,8,128]{3,2,1,0:T(8,128)S(1)} all-to-all(f32[16,2,8,128]{3,2,1,0:T(8,128)S(1)} %pad_maximum_fusion), channel_id=1, replica_groups=mesh['row'=32,'col'=16] {'col'}, dimensions={0} | all-to-all | bytes 262144 | tf_op jit(solution)/shard_map/all_to_all | solution.py:218
  182.8 22.0 %all_to_all.26.value = f32[16,2,8,128]{3,2,1,0:T(8,128)S(1)} all-to-all(f32[16,2,8,128]{3,2,1,0:T(8,128)S(1)} %all_to_all.25), channel_id=1, replica_groups={{0,32,64,96,128,160,192,224,256,288,320,352,384,416,448,480},{16,48,80,..., dimensions={0} | all-to-all | bytes 262144 | tf_op jit(solution)/shard_map/all_to_all | solution.py:319
  204.9 0.1 shard_map.55
  205.0 0.0 copy-start.2
  205.0 1.3 copy-done.2
  206.3 0.0 copy-start
  206.3 0.0 copy-start.3
  206.3 4.6 %all-to-all-start.4 = ((f32[16,16,2,8,128]{4,3,2,1,0:T(8,128)}), f32[16,16,2,8,128]{4,3,2,1,0:T(8,128)}, u32[]{:S(2)}, u32[]{:S(2)}) async-start(f32[16,16,2,8,128]{4,3,2,1,0:T(8,128)} %copy-done.2), calls=%async_computation.4 | async-start | bytes 4194304 | tf_op jit(solution)/shard_map/all_to_all | solution.py:218
  210.9 2.6 %shard_map.52 = f32[128,256]{1,0:T(8,128)} custom-call(s32[2]{0:T(128)S(1)} %pad_add_fusion.place, s32[32,32]{1,0:T(8,128)S(1)} %copy-done.4, f32[9,32,128]{2,1,0:T(8,128)S(1)} %get-tuple-element.8.fields), custom_call_target="tpu_custom_call" | custom-call | tf_op jit(solution)/shard_map/pallas_call | solution.py:243
  213.5 22.5 %all-to-all-done.4.two_row = f32[16,16,2,8,128]{4,3,2,1,0:T(8,128)} async-done(((f32[16,16,2,8,128]{4,3,2,1,0:T(8,128)}), f32[16,16,2,8,128]{4,3,2,1,0:T(8,128)}, u32[]{:S(2)}, u32[]{:S(2)}) %all-to-all-start.4) | async-done | bytes 2097184 | tf_op jit(solution)/shard_map/all_to_all | solution.py:218
  236.0 0.0 copy-done
  236.0 0.0 copy-done.3
  236.0 0.0 copy-start.1
  236.0 1.6 copy-done.1
  237.6 3.3 %shard_map.56 = f32[128,256]{1,0:T(8,128)} custom-call(s32[2]{0:T(128)S(1)} %pad_add_fusion.place, s32[32,32]{1,0:T(8,128)S(1)} %copy-done.4, f32[16,16,2,8,128]{4,3,2,1,0:T(8,128)} %all-to-all-done.4.two_row, bf16[4096,256]{1,0:T(8,128)(2,1)S(1)} %copy-done, bf16[4096,256]{1,0:T(8,128)(2,1)S(1)} %copy-done.1, f32[128,256]{1,0:T(8,128)S(1)} %copy-done.3), custom_call_target="tpu_custom_call" | custom-call | tf_op jit(solution)/shard_map/pallas_call | solution.py:243
  (2 shorter events, 0.0 us)
Async XLA Ops:
  7.2 127.4 %all-gather.3.cloned.1.call-start = ((), (), s32[]{:S(2)}) async-start(), calls=%async_computation.5 | async-start | bytes 4325376 | tf_op jit(solution)/shard_map/all_gather | solution.py:259
  72.7 7.6 %copy-start.5 = (f32[9,128]{1,0:T(8,128)S(1)}, f32[9,128]{1,0:T(8,128)}, u32[]{:S(2)}) copy-start(f32[9,128]{1,0:T(8,128)} %param.3) | copy-start | bytes 13828
  72.7 42.6 %copy-start.4 = (s32[32,32]{1,0:T(8,128)S(1)}, s32[32,32]{1,0:T(8,128)}, u32[]{:S(2)}) copy-start(s32[32,32]{1,0:T(8,128)} %pattern.9) | copy-start | bytes 12292
  72.7 42.6 %all-to-all-start = ((f32[16,128,256]{2,1,0:T(8,128)}), f32[16,128,256]{2,1,0:T(8,128)S(1)}, u32[]{:S(2)}, u32[]{:S(2)}) async-start(f32[16,128,256]{2,1,0:T(8,128)} %shard_map.50), calls=%async_computation | async-start | bytes 4194304 | tf_op jit(solution)/shard_map/all_to_all | solution.py:218
  80.3 5.7 %collective-permute-start = (f32[9,128]{1,0:T(8,128)S(1)}, f32[9,128]{1,0:T(8,128)S(1)}, u32[]{:S(2)}, u32[]{:S(2)}) collective-permute-start(f32[9,128]{1,0:T(8,128)S(1)} %copy-done.5), channel_id=1, source_target_pairs={{0,16},{16,0},{32,48},{48,32},{64,80},{80,64},{96,112},{112,96},{1... | collective-permute-start | bytes 13832 | tf_op jit(solution)/shard_map/ppermute | solution.py:265
  128.9 28.6 %all-to-all-start.1 = ((f32[16,128,256]{2,1,0:T(8,128)}), f32[16,128,256]{2,1,0:T(8,128)S(1)}, u32[]{:S(2)}, u32[]{:S(2)}) async-start(f32[16,128,256]{2,1,0:T(8,128)} %get-tuple-element.9), calls=%async_computation.1 | async-start | bytes 4194304 | tf_op jit(solution)/shard_map/all_to_all | solution.py:218
  161.4 9.5 %collective-permute-start.1 = (f32[16,8,128]{2,1,0:T(8,128)S(1)}, f32[16,8,128]{2,1,0:T(8,128)S(1)}, u32[]{:S(2)}, u32[]{:S(2)}) collective-permute-start(f32[16,8,128]{2,1,0:T(8,128)S(1)} %get-tuple-element.13), channel_id=1, source_target_pairs={{0,16},{16,0},{32,48},{48,32},{64,80},{80,64},{96,112},{112,96},{1... | collective-permute-start | bytes 196616 | tf_op jit(solution)/shard_map/ppermute | solution.py:316
  205.0 1.3 copy-start.2
  206.3 29.7 %copy-start = (bf16[4096,256]{1,0:T(8,128)(2,1)S(1)}, bf16[4096,256]{1,0:T(8,128)(2,1)}, u32[]{:S(2)}) copy-start(bf16[4096,256]{1,0:T(8,128)(2,1)} %get-tuple-element.10.high) | copy-start | bytes 6291460
  206.3 29.7 %copy-start.3 = (f32[128,256]{1,0:T(8,128)S(1)}, f32[128,256]{1,0:T(8,128)}, u32[]{:S(2)}) copy-start(f32[128,256]{1,0:T(8,128)} %iterate.1) | copy-start | bytes 393220
  206.3 29.7 %all-to-all-start.4 = ((f32[16,16,2,8,128]{4,3,2,1,0:T(8,128)}), f32[16,16,2,8,128]{4,3,2,1,0:T(8,128)}, u32[]{:S(2)}, u32[]{:S(2)}) async-start(f32[16,16,2,8,128]{4,3,2,1,0:T(8,128)} %copy-done.2), calls=%async_computation.4 | async-start | bytes 4194304 | tf_op jit(solution)/shard_map/all_to_all | solution.py:218
  236.0 1.6 copy-start.1
Sparse Core Ops, SparseCore 0:
  10.1 79.0 all-gather.2

commit v8 on v7

--- a/solution.py
+++ b/solution.py
@@ -11,7 +11,7 @@
 NB = 32
 FIELDS = 3 + 2 * PRIMS
 CHUNK = 128
-PANEL = 512
+PANEL = 1024
 PART = 1024
 LOG2E = 1.4426950408889634
 VMEM = pltpu.VMEM
@@ -218,11 +218,9 @@
     return lax.all_to_all(pieces, axis, 0, 0, tiled=True)
 
 
-def call(kernel, out_shapes, scratch, *operands, on_chip=(), outs=None, scalars=2, grid=(), blocks=None, source=VMEM, stay=()):
+def call(kernel, out_shapes, scratch, *operands, on_chip=(), outs=None, scalars=2, grid=(), blocks=None, stay=()):
     whole = pl.BlockSpec(memory_space=VMEM)
-    in_specs = [pl.BlockSpec(memory_space=SMEM)] * scalars + [pl.BlockSpec(memory_space=source)] * (
-        len(operands) - scalars
-    )
+    in_specs = [pl.BlockSpec(memory_space=SMEM)] * scalars + [whole] * (len(operands) - scalars)
     blocks = blocks or {}
     for k, block in blocks.items():
         if k < len(operands):
@@ -266,9 +264,7 @@
     everyone = lax.all_gather(both, "row", axis=0, axis_index_groups=cores)
     sems = pltpu.SemaphoreType.DMA((16,))
     wide = VMEM((2 * BLOCK, NB * BLOCK), jnp.bfloat16)
-    copies = call(
-        hbm_copies_kernel, tiles, [sems], iterate, outs=(HBM,), scalars=0, source=HBM, stay=(0,)
-    )
+    copies = call(hbm_copies_kernel, tiles, [sems], iterate, outs=(HBM,), scalars=0)
     iterate_row = exchange(copies, "col")
     fields, product_one = call(
         first_kernel,

time: 252 us -> 191 us (0.76)
  the two profiles are of different devices: /device:TPU:1 before, /device:TPU:32 now
where the time goes in v8:
time: 191 us; the launch traced here: 190 us
  blocking collectives  74.9 us (39%)
  waiting for transfers between devices  45.8 us (24%)
  Pallas kernels  26.5 us (14%)
  starting transfers between devices  25 us (13%)
  between operations  14.1 us (7%)
  local copies, waits for them, and re-layouts  3.81 us (2%)
    all_gather x1, blocking collectives, stages(): everyone = lax.all_gather(both, 'row', axis=0, axis_index_groups=cores)  35.3 us
    all_to_all x3, waiting for transfers between devices, exchange(): return lax.all_to_all(pieces, axis, 0, 0, tiled=True)  30.7 us
    pallas_call x7, Pallas kernels, call(): pl.pallas_call(kernel, out_shape=out_shapes, grid=grid, in_specs=in_specs...  26.5 us
    all_to_all x1, blocking collectives, stages(): lax.all_to_all(slices, 'row', 0, 0, tiled=True, axis_index_groups=cores)  26.3 us
    all_to_all x3, starting transfers between devices, exchange(): return lax.all_to_all(pieces, axis, 0, 0, tiled=True)  21.1 us
    all_to_all x1, blocking collectives, exchange(): return lax.all_to_all(pieces, axis, 0, 0, tiled=True)  13.3 us
    all_gather x1, waiting for transfers between devices, stages(): iterate_col = lax.all_gather(iterate, 'row', axis=0, tiled=True)  12.2 us
  transfers between devices with their start and end apart: 6, of which 5 were waited for; matrix products, arithmetic and copies ran while one was open for 0% of the time, Pallas kernels for 10%

profile of v8, /device:TPU:32, one launch (start us, length us, event | category | flops | bytes accessed | tf_op | source)
XLA Modules:
  0.0 190.3 jit_solution(11648678501413525685)
XLA Ops:
  7.2 0.0 all-gather.3.cloned.1.call-start
  7.2 0.7 all-gather.3.cloned.1.call-update
  7.9 0.0 copy-start.3
  7.9 0.9 copy-done.3
  8.8 1.5 shard_map.50
  10.3 0.0 copy-start.6
  10.3 0.0 copy-start.5
  10.3 7.0 %all-to-all-start = ((f32[16,128,256]{2,1,0:T(8,128)}), f32[16,128,256]{2,1,0:T(8,128)S(1)}, u32[]{:S(2)}, u32[]{:S(2)}) async-start(f32[16,128,256]{2,1,0:T(8,128)} %shard_map.50), calls=%async_computation | async-start | bytes 4194304 | tf_op jit(solution)/shard_map/all_to_all | solution.py:218
  17.4 0.0 copy-done.6
  17.4 1.9 %collective-permute-start = (f32[9,128]{1,0:T(8,128)S(1)}, f32[9,128]{1,0:T(8,128)S(1)}, u32[]{:S(2)}, u32[]{:S(2)}) collective-permute-start(f32[9,128]{1,0:T(8,128)S(1)} %copy-done.6), channel_id=1, source_target_pairs={{0,16},{16,0},{32,48},{48,32},{64,80},{80,64},{96,112},{112,96},{1... | collective-permute-start | bytes 13832 | tf_op jit(solution)/shard_map/ppermute | solution.py:263
  19.3 0.1 pad_add_fusion.place
  19.4 1.1 collective-permute-done
  20.5 35.3 %all-gather = f32[32,9,128]{2,1,0:T(8,128)S(1)} all-gather(f32[2,9,128]{2,1,0:T(8,128)S(1)} %pad_maximum_fusion.1), channel_id=2, replica_groups={{0,32,64,96,128,160,192,224,256,288,320,352,384,416,448,480},{16,48,80,..., dimensions={0}, use_global_device_ids=true | all-gather | bytes 156672 | tf_op jit(solution)/shard_map/all_gather | solution.py:264
  55.7 0.0 all-to-all-done.iterate_row
  55.7 0.0 copy-done.5
  55.7 10.4 %shard_map.51 = (f32[9,32,128]{2,1,0:T(8,128)S(1)}, f32[16,128,256]{2,1,0:T(8,128)}) custom-call(s32[2]{0:T(128)S(1)} %pad_add_fusion.place, s32[32,32]{1,0:T(8,128)S(1)} %copy-done.5, f32[16,2,9,128]{3,2,1,0:T(8,128)S(1)} %bitcast.7, f32[16,128,256]{2,1,0:T(8,128)S(1)} %all-to-all-done.iterate_row), custom_call_target="tpu_custom_call" | custom-call | tf_op jit(solution)/shard_map/pallas_call | solution.py:241
  66.2 9.5 %all-to-all-start.1 = ((f32[16,128,256]{2,1,0:T(8,128)}), f32[16,128,256]{2,1,0:T(8,128)S(1)}, u32[]{:S(2)}, u32[]{:S(2)}) async-start(f32[16,128,256]{2,1,0:T(8,128)} %get-tuple-element.9), calls=%async_computation.1 | async-start | bytes 4194304 | tf_op jit(solution)/shard_map/all_to_all | solution.py:218
  75.7 12.2 %all-gather.3.cloned.1.call-done.iterate_col = f32[4096,256]{1,0:T(8,128)} async-done(((f32[128,256]{1,0:T(8,128)}), f32[4096,256]{1,0:T(8,128)}) %all-gather.3.cloned.1.call-update) | async-done | bytes 4194320 | tf_op jit(solution)/shard_map/all_gather | solution.py:257
  87.9 5.1 %shard_map.53 = (bf16[4096,256]{1,0:T(8,128)(2,1)}, bf16[4096,256]{1,0:T(8,128)(2,1)}) custom-call(s32[2]{0:T(128)S(1)} %pad_add_fusion.place, s32[32,32]{1,0:T(8,128)S(1)} %copy-done.5, f32[4096,256]{1,0:T(8,128)} %all-gather.3.cloned.1.call-done.iterate_col), custom_call_target="tpu_custom_call" | custom-call | tf_op jit(solution)/shard_map/pallas_call | solution.py:241
  92.9 5.2 %all-to-all-done.1.one_row = f32[16,128,256]{2,1,0:T(8,128)S(1)} async-done(((f32[16,128,256]{2,1,0:T(8,128)}), f32[16,128,256]{2,1,0:T(8,128)S(1)}, u32[]{:S(2)}, u32[]{:S(2)}) %all-to-all-start.1) | async-done | bytes 2097184 | tf_op jit(solution)/shard_map/all_to_all | solution.py:218
  98.2 3.9 %shard_map.54 = (f32[16,8,128]{2,1,0:T(8,128)S(1)}, f32[16,8,128]{2,1,0:T(8,128)S(1)}) custom-call(s32[2]{0:T(128)S(1)} %pad_add_fusion.place, s32[32,32]{1,0:T(8,128)S(1)} %copy-done.5, f32[16,128,256]{2,1,0:T(8,128)S(1)} %all-to-all-done.1.one_row, bf16[4096,256]{1,0:T(8,128)(2,1)} %get-tuple-element.10.high, bf16[4096,256]{1,0:T(8,128)(2,1)} %get-tuple-element.11.low), custom_call_target="tpu_custom_call" | custom-call | tf_op jit(solution)/shard_map/pallas_call | solution.py:241
  102.1 1.9 %collective-permute-start.1 = (f32[16,8,128]{2,1,0:T(8,128)S(1)}, f32[16,8,128]{2,1,0:T(8,128)S(1)}, u32[]{:S(2)}, u32[]{:S(2)}) collective-permute-start(f32[16,8,128]{2,1,0:T(8,128)S(1)} %get-tuple-element.13), channel_id=1, source_target_pairs={{0,16},{16,0},{32,48},{48,32},{64,80},{80,64},{96,112},{112,96},{1... | collective-permute-start | bytes 196616 | tf_op jit(solution)/shard_map/ppermute | solution.py:312
  104.0 1.2 collective-permute-done.1
  105.2 13.3 %all_to_all.25 = f32[16,2,8,128]{3,2,1,0:T(8,128)S(1)} all-to-all(f32[16,2,8,128]{3,2,1,0:T(8,128)S(1)} %pad_maximum_fusion), channel_id=1, replica_groups=mesh['row'=32,'col'=16] {'col'}, dimensions={0} | all-to-all | bytes 262144 | tf_op jit(solution)/shard_map/all_to_all | solution.py:218
  118.5 26.3 %all_to_all.26.value = f32[16,2,8,128]{3,2,1,0:T(8,128)S(1)} all-to-all(f32[16,2,8,128]{3,2,1,0:T(8,128)S(1)} %all_to_all.25), channel_id=1, replica_groups={{0,32,64,96,128,160,192,224,256,288,320,352,384,416,448,480},{16,48,80,..., dimensions={0} | all-to-all | bytes 262144 | tf_op jit(solution)/shard_map/all_to_all | solution.py:315
  144.8 0.1 shard_map.55
  145.0 0.0 copy-start.2
  145.0 1.3 copy-done.2
  146.3 0.0 copy-start
  146.3 0.0 copy-start.4
  146.3 4.6 %all-to-all-start.4 = ((f32[16,16,2,8,128]{4,3,2,1,0:T(8,128)}), f32[16,16,2,8,128]{4,3,2,1,0:T(8,128)}, u32[]{:S(2)}, u32[]{:S(2)}) async-start(f32[16,16,2,8,128]{4,3,2,1,0:T(8,128)} %copy-done.2), calls=%async_computation.4 | async-start | bytes 4194304 | tf_op jit(solution)/shard_map/all_to_all | solution.py:218
  150.9 2.2 %shard_map.52 = f32[128,256]{1,0:T(8,128)} custom-call(s32[2]{0:T(128)S(1)} %pad_add_fusion.place, s32[32,32]{1,0:T(8,128)S(1)} %copy-done.5, f32[9,32,128]{2,1,0:T(8,128)S(1)} %get-tuple-element.8.fields), custom_call_target="tpu_custom_call" | custom-call | tf_op jit(solution)/shard_map/pallas_call | solution.py:241
  153.1 25.4 %all-to-all-done.4.two_row = f32[16,16,2,8,128]{4,3,2,1,0:T(8,128)} async-done(((f32[16,16,2,8,128]{4,3,2,1,0:T(8,128)}), f32[16,16,2,8,128]{4,3,2,1,0:T(8,128)}, u32[]{:S(2)}, u32[]{:S(2)}) %all-to-all-start.4) | async-done | bytes 2097184 | tf_op jit(solution)/shard_map/all_to_all | solution.py:218
  178.5 0.0 copy-done
  178.5 0.0 copy-done.4
  178.5 0.0 copy-start.1
  178.5 1.6 copy-done.1
  180.1 3.3 %shard_map.56 = f32[128,256]{1,0:T(8,128)} custom-call(s32[2]{0:T(128)S(1)} %pad_add_fusion.place, s32[32,32]{1,0:T(8,128)S(1)} %copy-done.5, f32[16,16,2,8,128]{4,3,2,1,0:T(8,128)} %all-to-all-done.4.two_row, bf16[4096,256]{1,0:T(8,128)(2,1)S(1)} %copy-done, bf16[4096,256]{1,0:T(8,128)(2,1)S(1)} %copy-done.1, f32[128,256]{1,0:T(8,128)S(1)} %copy-done.4), custom_call_target="tpu_custom_call" | custom-call | tf_op jit(solution)/shard_map/pallas_call | solution.py:241
  (2 shorter events, 0.0 us)
Async XLA Ops:
  7.2 80.7 %all-gather.3.cloned.1.call-start = ((), (), s32[]{:S(2)}) async-start(), calls=%async_computation.5 | async-start | bytes 4325376 | tf_op jit(solution)/shard_map/all_gather | solution.py:257
  7.9 0.9 copy-start.3
  10.3 7.1 %copy-start.6 = (f32[9,128]{1,0:T(8,128)S(1)}, f32[9,128]{1,0:T(8,128)}, u32[]{:S(2)}) copy-start(f32[9,128]{1,0:T(8,128)} %param.3) | copy-start | bytes 13828
  10.3 45.4 %copy-start.5 = (s32[32,32]{1,0:T(8,128)S(1)}, s32[32,32]{1,0:T(8,128)}, u32[]{:S(2)}) copy-start(s32[32,32]{1,0:T(8,128)} %pattern.9) | copy-start | bytes 12292
  10.3 45.4 %all-to-all-start = ((f32[16,128,256]{2,1,0:T(8,128)}), f32[16,128,256]{2,1,0:T(8,128)S(1)}, u32[]{:S(2)}, u32[]{:S(2)}) async-start(f32[16,128,256]{2,1,0:T(8,128)} %shard_map.50), calls=%async_computation | async-start | bytes 4194304 | tf_op jit(solution)/shard_map/all_to_all | solution.py:218
  17.4 3.1 %collective-permute-start = (f32[9,128]{1,0:T(8,128)S(1)}, f32[9,128]{1,0:T(8,128)S(1)}, u32[]{:S(2)}, u32[]{:S(2)}) collective-permute-start(f32[9,128]{1,0:T(8,128)S(1)} %copy-done.6), channel_id=1, source_target_pairs={{0,16},{16,0},{32,48},{48,32},{64,80},{80,64},{96,112},{112,96},{1... | collective-permute-start | bytes 13832 | tf_op jit(solution)/shard_map/ppermute | solution.py:263
  66.2 32.0 %all-to-all-start.1 = ((f32[16,128,256]{2,1,0:T(8,128)}), f32[16,128,256]{2,1,0:T(8,128)S(1)}, u32[]{:S(2)}, u32[]{:S(2)}) async-start(f32[16,128,256]{2,1,0:T(8,128)} %get-tuple-element.9), calls=%async_computation.1 | async-start | bytes 4194304 | tf_op jit(solution)/shard_map/all_to_all | solution.py:218
  102.1 3.1 %collective-permute-start.1 = (f32[16,8,128]{2,1,0:T(8,128)S(1)}, f32[16,8,128]{2,1,0:T(8,128)S(1)}, u32[]{:S(2)}, u32[]{:S(2)}) collective-permute-start(f32[16,8,128]{2,1,0:T(8,128)S(1)} %get-tuple-element.13), channel_id=1, source_target_pairs={{0,16},{16,0},{32,48},{48,32},{64,80},{80,64},{96,112},{112,96},{1... | collective-permute-start | bytes 196616 | tf_op jit(solution)/shard_map/ppermute | solution.py:312
  145.0 1.3 copy-start.2
  146.3 32.2 %copy-start = (bf16[4096,256]{1,0:T(8,128)(2,1)S(1)}, bf16[4096,256]{1,0:T(8,128)(2,1)}, u32[]{:S(2)}) copy-start(bf16[4096,256]{1,0:T(8,128)(2,1)} %get-tuple-element.10.high) | copy-start | bytes 6291460
  146.3 32.2 %copy-start.4 = (f32[128,256]{1,0:T(8,128)S(1)}, f32[128,256]{1,0:T(8,128)}, u32[]{:S(2)}) copy-start(f32[128,256]{1,0:T(8,128)} %iterate.1) | copy-start | bytes 393220
  146.3 32.2 %all-to-all-start.4 = ((f32[16,16,2,8,128]{4,3,2,1,0:T(8,128)}), f32[16,16,2,8,128]{4,3,2,1,0:T(8,128)}, u32[]{:S(2)}, u32[]{:S(2)}) async-start(f32[16,16,2,8,128]{4,3,2,1,0:T(8,128)} %copy-done.2), calls=%async_computation.4 | async-start | bytes 4194304 | tf_op jit(solution)/shard_map/all_to_all | solution.py:218
  178.5 1.6 copy-start.1
Sparse Core Ops, SparseCore 0:
  10.1 77.7 all-gather.2

commit v9 on v8

--- a/solution.py
+++ b/solution.py
@@ -13,6 +13,7 @@
 CHUNK = 128
 PANEL = 1024
 PART = 1024
+ROOMS = (24,)
 LOG2E = 1.4426950408889634
 VMEM = pltpu.VMEM
 SMEM = pltpu.SMEM
@@ -145,9 +146,29 @@
     send_copies(value, copies, sems)
 
 
-def replicate_kernel(value, copies):
-    for copy in range(copies.shape[0]):
-        copies[copy] = value[...]
+def list_live(pattern, row, order):
+    for k in range(NB):
+        order[k] = 0
+
+    def step(k, count):
+        @pl.when(pattern[row, k] != 0)
+        def _():
+            order[count] = k
+
+        return count + (pattern[row, k] != 0).astype(jnp.int32)
+
+    return lax.fori_loop(0, NB, step, jnp.int32(0))
+
+
+def compact_kernel(place, pattern, slices, copies, order, line):
+    row = place[0]
+    core = row % 2
+    count = list_live(pattern, row, order)
+    for i in range(line.shape[0]):
+        kept = (i < count).astype(jnp.float32)
+        line[i] = kept * slices[order[i] // 2, core ^ (order[i] % 2)]
+    for copy in range(16):
+        copies[copy] = line[...]
 
 
 def prepare_kernel(place, pattern, iterate_col, high, low):
@@ -180,7 +201,7 @@
     row, col = place[0], place[1]
     part = pl.program_id(0)
     pieces = PART // (2 * BLOCK)
-    product = contract([one_row[part * pieces + k] for k in range(pieces)], high, low)
+    product = contract([one_row[k] for k in range(pieces)], high, low)
 
     @pl.when(part == 0)
     def _():
@@ -200,14 +221,19 @@
         given[...] = tile[1 - core].reshape(BLOCK // 8, 8, BLOCK)
 
 
-def third_kernel(place, pattern, two_row, high, low, iterate, updated):
+def third_kernel(place, pattern, two_row, high, low, iterate, updated, order):
     row, col = place[0], place[1]
-    core = row % 2
-    pieces = []
-    for k in range(16):
-        pair = [two_row[:, k, core ^ h].reshape(BLOCK, BLOCK) for h in range(2)]
-        pieces.append(jnp.concatenate(pair, axis=1))
-    total = contract(pieces, high, low)
+    list_live(pattern, row, order)
+    total = jnp.zeros((BLOCK, 2 * BLOCK), jnp.float32)
+    for i in range(0, two_row.shape[1], 2):
+        pair = [two_row[:, i + h].reshape(BLOCK, BLOCK) for h in range(2)]
+        rows = [pl.ds(pl.multiple_of(order[i + h] * BLOCK, BLOCK), BLOCK) for h in range(2)]
+        piece_high, piece_low = split(jnp.concatenate(pair, axis=1))
+        part_high = jnp.concatenate([high[r, :] for r in rows], axis=0)
+        part_low = jnp.concatenate([low[r, :] for r in rows], axis=0)
+        total = total + jnp.dot(piece_high, part_high, preferred_element_type=jnp.float32)
+        total = total + jnp.dot(piece_high, part_low, preferred_element_type=jnp.float32)
+        total = total + jnp.dot(piece_low, part_high, preferred_element_type=jnp.float32)
     for half in range(2):
         lanes = slice(half * BLOCK, (half + 1) * BLOCK)
         mask = live(pattern, row, 2 * col + half)
@@ -224,7 +250,7 @@
     blocks = blocks or {}
     for k, block in blocks.items():
         if k < len(operands):
-            in_specs[k] = pl.BlockSpec(block, lambda i: (i, 0))
+            in_specs[k] = pl.BlockSpec(block, lambda i, rest=len(block) - 1: (i,) + (0,) * rest)
     operands = list(operands)
     for k in on_chip:
         operands[k] = pltpu.with_memory_space_constraint(operands[k], VMEM)
@@ -251,6 +277,8 @@
 
 def stages(records, pattern, iterate):
     place = jnp.stack([lax.axis_index("row"), lax.axis_index("col")]).astype(jnp.int32)
+    fullest = jnp.max(jnp.sum((pattern != 0).astype(jnp.int32), axis=1))
+    place, roomy = lax.optimization_barrier((place, fullest > ROOMS[0]))
     tile = jax.ShapeDtypeStruct((BLOCK, 2 * BLOCK), jnp.float32)
     stored = HBM((NB * BLOCK, 2 * BLOCK), jnp.bfloat16)
     tiles = HBM((16, BLOCK, 2 * BLOCK), jnp.float32)
@@ -304,19 +332,30 @@
         one_row,
         high,
         low,
-        on_chip=(2,),
         grid=(NB * BLOCK // PART,),
-        blocks={3: window, 4: window},
-        stay=(3, 4),
+        blocks={2: (PART // (2 * BLOCK), BLOCK, 2 * BLOCK), 3: window, 4: window},
+        stay=(2, 3, 4),
     )
     given = lax.ppermute(given, "row", partner)
     slices = jnp.stack([kept, given], axis=1)
     slices = exchange(slices, "col")
     slices = lax.all_to_all(slices, "row", 0, 0, tiled=True, axis_index_groups=cores)
-    copies = VMEM((16,) + slices.shape, jnp.float32)
-    slices = call(replicate_kernel, copies, [], slices, on_chip=(0,), scalars=0)
-    two_row = exchange(slices, "col")
-    updated = call(third_kernel, tile, [], place, pattern, two_row, high, low, iterate, on_chip=(2, 3, 4))
+    order = SMEM((NB,), jnp.int32)
+
+    def finish(room):
+        def branch(place, pattern, slices, high, low, iterate):
+            line = VMEM((room, 8, BLOCK), jnp.float32)
+            copies = VMEM((16, room, 8, BLOCK), jnp.float32)
+            copies = call(compact_kernel, copies, [order, line], place, pattern, slices, on_chip=(2,))
+            two_row = exchange(copies, "col")
+            return call(
+                third_kernel, tile, [order], place, pattern, two_row, high, low, iterate, on_chip=(2, 3, 4)
+            )
+
+        return branch
+
+    slices, roomy = lax.optimization_barrier((slices, roomy))
+    updated = lax.cond(roomy, finish(NB), finish(ROOMS[0]), place, pattern, slices, high, low, iterate)
     return (margin, updated)
 
 

time: 191 us -> 183 us (0.958)
  the two profiles are of different devices: /device:TPU:32 before, /device:TPU:1 now
where the time goes in v9:
time: 183 us; the launch traced here: 179 us
  blocking collectives  64.7 us (35%)
  starting transfers between devices  36.5 us (20%)
  Pallas kernels  31.4 us (17%)
  waiting for transfers between devices  29.1 us (16%)
  between operations  14.8 us (8%)
  local copies, waits for them, and re-layouts  2.03 us (1%)
    all_to_all x2, blocking collectives, exchange(): return lax.all_to_all(pieces, axis, 0, 0, tiled=True)  34.1 us
    pallas_call x7, Pallas kernels, call(): pl.pallas_call(kernel, out_shape=out_shapes, grid=grid, in_specs=in_specs...  31.4 us
    all_gather x1, blocking collectives, stages(): everyone = lax.all_gather(both, 'row', axis=0, axis_index_groups=cores)  30.6 us
    all_gather x1, waiting for transfers between devices, stages(): iterate_col = lax.all_gather(iterate, 'row', axis=0, tiled=True)  15.8 us
    all_to_all x2, starting transfers between devices, exchange(): return lax.all_to_all(pieces, axis, 0, 0, tiled=True)  12.8 us
    all_to_all x1, starting transfers between devices, stages(): lax.all_to_all(slices, 'row', 0, 0, tiled=True, axis_index_groups=cores)  10.3 us
    all_to_all x1, waiting for transfers between devices, stages(): lax.all_to_all(slices, 'row', 0, 0, tiled=True, axis_index_groups=cores)  9.41 us
    ppermute x1, starting transfers between devices, stages(): given = lax.ppermute(given, 'row', partner)  8.51 us
  transfers between devices with their start and end apart: 6, of which 4 were waited for; matrix products, arithmetic and copies ran while one was open for 0% of the time, Pallas kernels for 13%

profile of v9, /device:TPU:1, one launch (start us, length us, event | category | flops | bytes accessed | tf_op | source)
XLA Modules:
  0.0 179.5 jit_solution(228782407364360588)
XLA Ops:
  7.2 0.0 all-gather.3.cloned.1.call-start
  7.2 0.7 all-gather.3.cloned.1.call-update
  7.9 2.4 %shard_map.50 = f32[16,128,256]{2,1,0:T(8,128)} custom-call(f32[128,256]{1,0:T(8,128)} %value.1), custom_call_target="tpu_custom_call" | custom-call | tf_op jit(solution)/shard_map/pallas_call | solution.py:267
  10.3 0.0 copy-start.7
  10.3 0.0 copy-start.5
  10.3 7.6 %all-to-all-start.2 = ((f32[16,128,256]{2,1,0:T(8,128)}), f32[16,128,256]{2,1,0:T(8,128)S(1)}, u32[]{:S(2)}, u32[]{:S(2)}) async-start(f32[16,128,256]{2,1,0:T(8,128)} %shard_map.50), calls=%async_computation.2 | async-start | bytes 4194304 | tf_op jit(solution)/shard_map/all_to_all | solution.py:244
  17.9 0.0 copy-done.7
  17.9 4.9 %collective-permute-start = (f32[9,128]{1,0:T(8,128)S(1)}, f32[9,128]{1,0:T(8,128)S(1)}, u32[]{:S(2)}, u32[]{:S(2)}) collective-permute-start(f32[9,128]{1,0:T(8,128)S(1)} %copy-done.7), channel_id=1, source_target_pairs={{0,16},{16,0},{32,48},{48,32},{64,80},{80,64},{96,112},{112,96},{1... | collective-permute-start | bytes 13832 | tf_op jit(solution)/shard_map/ppermute | solution.py:291
  22.8 0.0 copy-done.5
  22.9 0.1 convert_reduce_fusion
  23.0 0.1 pad_add_fusion.place
  23.0 0.6 reduce_max.9
  24.3 0.0 collective-permute-done
  24.4 30.6 %all-gather = f32[32,9,128]{2,1,0:T(8,128)S(1)} all-gather(f32[2,9,128]{2,1,0:T(8,128)S(1)} %pad_maximum_fusion.1), channel_id=2, replica_groups={{0,32,64,96,128,160,192,224,256,288,320,352,384,416,448,480},{16,48,80,..., dimensions={0}, use_global_device_ids=true | all-gather | bytes 156672 | tf_op jit(solution)/shard_map/all_gather | solution.py:292
  54.9 0.0 all-to-all-done.2.iterate_row
  54.9 13.5 %shard_map.51 = (f32[9,32,128]{2,1,0:T(8,128)S(1)}, f32[16,128,256]{2,1,0:T(8,128)}) custom-call(s32[2]{0:T(128)S(1)} %pad_add_fusion.place, s32[32,32]{1,0:T(8,128)S(1)} %copy-done.5, f32[16,2,9,128]{3,2,1,0:T(8,128)S(1)} %bitcast.7, f32[16,128,256]{2,1,0:T(8,128)S(1)} %all-to-all-done.2.iterate_row), custom_call_target="tpu_custom_call" | custom-call | tf_op jit(solution)/shard_map/pallas_call | solution.py:267
  68.5 5.3 %all-to-all-start.3 = ((f32[16,128,256]{2,1,0:T(8,128)}), f32[16,128,256]{2,1,0:T(8,128)S(1)}, u32[]{:S(2)}, u32[]{:S(2)}) async-start(f32[16,128,256]{2,1,0:T(8,128)} %get-tuple-element.53), calls=%async_computation.3 | async-start | bytes 4194304 | tf_op jit(solution)/shard_map/all_to_all | solution.py:244
  73.7 15.8 %all-gather.3.cloned.1.call-done.iterate_col = f32[4096,256]{1,0:T(8,128)} async-done(((f32[128,256]{1,0:T(8,128)}), f32[4096,256]{1,0:T(8,128)}) %all-gather.3.cloned.1.call-update) | async-done | bytes 4194320 | tf_op jit(solution)/shard_map/all_gather | solution.py:285
  89.6 5.1 %shard_map.53 = (bf16[4096,256]{1,0:T(8,128)(2,1)}, bf16[4096,256]{1,0:T(8,128)(2,1)}) custom-call(s32[2]{0:T(128)S(1)} %pad_add_fusion.place, s32[32,32]{1,0:T(8,128)S(1)} %copy-done.5, f32[4096,256]{1,0:T(8,128)} %all-gather.3.cloned.1.call-done.iterate_col), custom_call_target="tpu_custom_call" | custom-call | tf_op jit(solution)/shard_map/pallas_call | solution.py:267
  94.7 2.3 %all-to-all-done.3.one_row = f32[16,128,256]{2,1,0:T(8,128)S(1)} async-done(((f32[16,128,256]{2,1,0:T(8,128)}), f32[16,128,256]{2,1,0:T(8,128)S(1)}, u32[]{:S(2)}, u32[]{:S(2)}) %all-to-all-start.3) | async-done | bytes 2097184 | tf_op jit(solution)/shard_map/all_to_all | solution.py:244
  97.0 0.0 copy-start.3
  97.0 1.3 copy-done.3
  98.3 0.0 copy-start
  98.3 0.0 copy-start.4
  98.3 4.4 %shard_map.54 = (f32[16,8,128]{2,1,0:T(8,128)S(1)}, f32[16,8,128]{2,1,0:T(8,128)S(1)}) custom-call(s32[2]{0:T(128)S(1)} %pad_add_fusion.place, s32[32,32]{1,0:T(8,128)S(1)} %copy-done.5, f32[16,128,256]{2,1,0:T(8,128)} %copy-done.3, bf16[4096,256]{1,0:T(8,128)(2,1)} %get-tuple-element.54.high, bf16[4096,256]{1,0:T(8,128)(2,1)} %get-tuple-element.55.low), custom_call_target="tpu_custom_call" | custom-call | tf_op jit(solution)/shard_map/pallas_call | solution.py:267
  102.8 8.5 %collective-permute-start.1 = (f32[16,8,128]{2,1,0:T(8,128)S(1)}, f32[16,8,128]{2,1,0:T(8,128)S(1)}, u32[]{:S(2)}, u32[]{:S(2)}) collective-permute-start(f32[16,8,128]{2,1,0:T(8,128)S(1)} %get-tuple-element.57), channel_id=1, source_target_pairs={{0,16},{16,0},{32,48},{48,32},{64,80},{80,64},{96,112},{112,96},{1... | collective-permute-start | bytes 196616 | tf_op jit(solution)/shard_map/ppermute | solution.py:339
  111.3 0.9 collective-permute-done.1
  112.2 12.0 %all_to_all.30 = f32[16,2,8,128]{3,2,1,0:T(8,128)} all-to-all(f32[16,2,8,128]{3,2,1,0:T(8,128)S(1)} %copy.7), channel_id=1, replica_groups=mesh['row'=32,'col'=16] {'col'}, dimensions={0} | all-to-all | bytes 262144 | tf_op jit(solution)/shard_map/all_to_all | solution.py:244
  124.2 10.3 %all-to-all-start.5 = ((f32[16,2,8,128]{3,2,1,0:T(8,128)}), f32[16,2,8,128]{3,2,1,0:T(8,128)S(1)}, u32[]{:S(2)}, u32[]{:S(2)}) async-start(f32[16,2,8,128]{3,2,1,0:T(8,128)} %all_to_all.30), calls=%async_computation.5 | async-start | bytes 262144 | tf_op jit(solution)/shard_map/all_to_all | solution.py:342
  134.5 2.6 %shard_map.52 = f32[128,256]{1,0:T(8,128)} custom-call(s32[2]{0:T(128)S(1)} %pad_add_fusion.place, s32[32,32]{1,0:T(8,128)S(1)} %copy-done.5, f32[9,32,128]{2,1,0:T(8,128)S(1)} %get-tuple-element.52.fields), custom_call_target="tpu_custom_call" | custom-call | tf_op jit(solution)/shard_map/pallas_call | solution.py:267
  137.0 9.4 %all-to-all-done.5 = f32[16,2,8,128]{3,2,1,0:T(8,128)S(1)} async-done(((f32[16,2,8,128]{3,2,1,0:T(8,128)}), f32[16,2,8,128]{3,2,1,0:T(8,128)S(1)}, u32[]{:S(2)}, u32[]{:S(2)}) %all-to-all-start.5) | async-done | bytes 131104 | tf_op jit(solution)/shard_map/all_to_all | solution.py:342
  146.5 0.0 copy-done
  146.5 0.0 copy-done.4
  146.5 25.5 %conditional.1 = (f32[128,256]{1,0:T(8,128)S(1)}) conditional(s32[]{:T(128)} %convert_element_type.7, (s32[2]{0:T(128)S(1)}, s32[32,32]{1,0:T(8,128)S(1)}, f32[16,2,8,128]{3,2,1,0:T(8,128)S(1)}, bf16[4096,256]{1,0:T(8,128)(2,1)S(1)}, bf16[4096,256]{1,0:T(8,128)(2,1)}, /*index=5*/f32[128,256]{1,0:T(8,128)S(1)}) %tuple.30, (s32[2]{0:T(128)S(1)}, ...), branch_computations={%region_2.0_spmd, %region_3.0_spmd} | conditional | bytes 12582948 | solution.py:358
  146.5 0.0 copy-start.1
  146.5 1.4 branch_0_fun.2
  147.9 22.1 %all_to_all.28.two_row = f32[16,24,8,128]{3,2,1,0:T(8,128)S(1)} all-to-all(f32[16,24,8,128]{3,2,1,0:T(8,128)S(1)} %branch_0_fun.2), channel_id=1, replica_groups=mesh['row'=32,'col'=16] {'col'}, dimensions={0} | all-to-all | bytes 3145728 | tf_op jit(solution)/shard_map/cond/branch_0_fun/all_to_all | solution.py:244
  170.0 0.0 copy-done.1
  170.0 2.0 %branch_0_fun.3 = f32[128,256]{1,0:T(8,128)S(1)} custom-call(s32[2]{0:T(128)S(1)} %get-tuple-element.17.place, s32[32,32]{1,0:T(8,128)S(1)} %get-tuple-element.28.pattern, f32[16,24,8,128]{3,2,1,0:T(8,128)S(1)} %all_to_all.28.two_row, bf16[4096,256]{1,0:T(8,128)(2,1)S(1)} %get-tuple-element.30.high, bf16[4096,256]{1,0:T(8,128)(2,1)S(1)} %copy-done.1, ...), custom_call_target="tpu_custom_call" | custom-call | tf_op jit(solution)/shard_map/cond/branch_0_fun/pallas_call | solution.py:267
  172.0 0.0 copy-start.6
  172.0 0.6 copy-done.6
  (3 shorter events, 0.0 us)
Async XLA Ops:
  7.2 82.4 %all-gather.3.cloned.1.call-start = ((), (), s32[]{:S(2)}) async-start(), calls=%async_computation.6 | async-start | bytes 4325376 | tf_op jit(solution)/shard_map/all_gather | solution.py:285
  10.3 7.6 %copy-start.7 = (f32[9,128]{1,0:T(8,128)S(1)}, f32[9,128]{1,0:T(8,128)}, u32[]{:S(2)}) copy-start(f32[9,128]{1,0:T(8,128)} %param.5) | copy-start | bytes 13828
  10.3 12.5 %copy-start.5 = (s32[32,32]{1,0:T(8,128)S(1)}, s32[32,32]{1,0:T(8,128)}, u32[]{:S(2)}) copy-start(s32[32,32]{1,0:T(8,128)} %pattern.7) | copy-start | bytes 12292
  10.3 44.6 %all-to-all-start.2 = ((f32[16,128,256]{2,1,0:T(8,128)}), f32[16,128,256]{2,1,0:T(8,128)S(1)}, u32[]{:S(2)}, u32[]{:S(2)}) async-start(f32[16,128,256]{2,1,0:T(8,128)} %shard_map.50), calls=%async_computation.2 | async-start | bytes 4194304 | tf_op jit(solution)/shard_map/all_to_all | solution.py:244
  17.9 6.4 %collective-permute-start = (f32[9,128]{1,0:T(8,128)S(1)}, f32[9,128]{1,0:T(8,128)S(1)}, u32[]{:S(2)}, u32[]{:S(2)}) collective-permute-start(f32[9,128]{1,0:T(8,128)S(1)} %copy-done.7), channel_id=1, source_target_pairs={{0,16},{16,0},{32,48},{48,32},{64,80},{80,64},{96,112},{112,96},{1... | collective-permute-start | bytes 13832 | tf_op jit(solution)/shard_map/ppermute | solution.py:291
  68.5 28.5 %all-to-all-start.3 = ((f32[16,128,256]{2,1,0:T(8,128)}), f32[16,128,256]{2,1,0:T(8,128)S(1)}, u32[]{:S(2)}, u32[]{:S(2)}) async-start(f32[16,128,256]{2,1,0:T(8,128)} %get-tuple-element.53), calls=%async_computation.3 | async-start | bytes 4194304 | tf_op jit(solution)/shard_map/all_to_all | solution.py:244
  97.0 1.3 copy-start.3
  98.3 48.1 %copy-start = (bf16[4096,256]{1,0:T(8,128)(2,1)S(1)}, bf16[4096,256]{1,0:T(8,128)(2,1)}, u32[]{:S(2)}) copy-start(bf16[4096,256]{1,0:T(8,128)(2,1)} %get-tuple-element.54.high) | copy-start | bytes 6291460
  98.3 48.1 %copy-start.4 = (f32[128,256]{1,0:T(8,128)S(1)}, f32[128,256]{1,0:T(8,128)}, u32[]{:S(2)}) copy-start(f32[128,256]{1,0:T(8,128)} %value.1) | copy-start | bytes 393220
  102.8 9.4 %collective-permute-start.1 = (f32[16,8,128]{2,1,0:T(8,128)S(1)}, f32[16,8,128]{2,1,0:T(8,128)S(1)}, u32[]{:S(2)}, u32[]{:S(2)}) collective-permute-start(f32[16,8,128]{2,1,0:T(8,128)S(1)} %get-tuple-element.57), channel_id=1, source_target_pairs={{0,16},{16,0},{32,48},{48,32},{64,80},{80,64},{96,112},{112,96},{1... | collective-permute-start | bytes 196616 | tf_op jit(solution)/shard_map/ppermute | solution.py:339
  124.2 22.2 %all-to-all-start.5 = ((f32[16,2,8,128]{3,2,1,0:T(8,128)}), f32[16,2,8,128]{3,2,1,0:T(8,128)S(1)}, u32[]{:S(2)}, u32[]{:S(2)}) async-start(f32[16,2,8,128]{3,2,1,0:T(8,128)} %all_to_all.30), calls=%async_computation.5 | async-start | bytes 262144 | tf_op jit(solution)/shard_map/all_to_all | solution.py:342
  146.5 23.5 %copy-start.1 = (bf16[4096,256]{1,0:T(8,128)(2,1)S(1)}, bf16[4096,256]{1,0:T(8,128)(2,1)}, u32[]{:S(2)}) copy-start(bf16[4096,256]{1,0:T(8,128)(2,1)} %get-tuple-element.31.low) | copy-start | bytes 6291460 | tf_op jit(solution)/shard_map/cond
  172.0 0.7 copy-start.6
Sparse Core Ops, SparseCore 0:
  10.1 79.4 all-gather.2

commit v10 on v9

--- a/solution.py
+++ b/solution.py
@@ -13,7 +13,7 @@
 CHUNK = 128
 PANEL = 1024
 PART = 1024
-ROOMS = (24,)
+ROOMS = (20, 24, 28, NB)
 LOG2E = 1.4426950408889634
 VMEM = pltpu.VMEM
 SMEM = pltpu.SMEM
@@ -278,7 +278,8 @@
 def stages(records, pattern, iterate):
     place = jnp.stack([lax.axis_index("row"), lax.axis_index("col")]).astype(jnp.int32)
     fullest = jnp.max(jnp.sum((pattern != 0).astype(jnp.int32), axis=1))
-    place, roomy = lax.optimization_barrier((place, fullest > ROOMS[0]))
+    choice = sum((fullest > room).astype(jnp.int32) for room in ROOMS[:-1])
+    place, choice = lax.optimization_barrier((place, choice))
     tile = jax.ShapeDtypeStruct((BLOCK, 2 * BLOCK), jnp.float32)
     stored = HBM((NB * BLOCK, 2 * BLOCK), jnp.bfloat16)
     tiles = HBM((16, BLOCK, 2 * BLOCK), jnp.float32)
@@ -354,8 +355,9 @@
 
         return branch
 
-    slices, roomy = lax.optimization_barrier((slices, roomy))
-    updated = lax.cond(roomy, finish(NB), finish(ROOMS[0]), place, pattern, slices, high, low, iterate)
+    slices, choice = lax.optimization_barrier((slices, choice))
+    branches = [finish(room) for room in ROOMS]
+    updated = lax.switch(choice, branches, place, pattern, slices, high, low, iterate)
     return (margin, updated)
 
 

time: 183 us -> 184 us (level)
  blocking collectives: 64.7 us -> 62.8 us
  starting transfers between devices: 36.5 us -> 38.4 us
where the time goes in v10:
time: 184 us; the launch traced here: 181 us
  blocking collectives  62.8 us (34%)
  starting transfers between devices  38.4 us (21%)
  Pallas kernels  31.4 us (17%)
  waiting for transfers between devices  29.3 us (16%)
  between operations  16.1 us (9%)
  local copies, waits for them, and re-layouts  2.01 us (1%)
    all_to_all x2, blocking collectives, exchange(): return lax.all_to_all(pieces, axis, 0, 0, tiled=True)  32.3 us
    pallas_call x7, Pallas kernels, call(): pl.pallas_call(kernel, out_shape=out_shapes, grid=grid, in_specs=in_specs...  31.4 us
    all_gather x1, blocking collectives, stages(): everyone = lax.all_gather(both, 'row', axis=0, axis_index_groups=cores)  30.5 us
    all_gather x1, waiting for transfers between devices, stages(): iterate_col = lax.all_gather(iterate, 'row', axis=0, tiled=True)  14.5 us
    all_to_all x2, starting transfers between devices, exchange(): return lax.all_to_all(pieces, axis, 0, 0, tiled=True)  13.2 us
    all_to_all x1, starting transfers between devices, stages(): lax.all_to_all(slices, 'row', 0, 0, tiled=True, axis_index_groups=cores)  11.5 us
    all_to_all x1, waiting for transfers between devices, stages(): lax.all_to_all(slices, 'row', 0, 0, tiled=True, axis_index_groups=cores)  9.41 us
    ppermute x1, starting transfers between devices, stages(): given = lax.ppermute(given, 'row', partner)  8.77 us
  transfers between devices with their start and end apart: 6, of which 4 were waited for; matrix products, arithmetic and copies ran while one was open for 0% of the time, Pallas kernels for 13%

profile of v10, /device:TPU:1, one launch (start us, length us, event | category | flops | bytes accessed | tf_op | source)
XLA Modules:
  0.0 180.9 jit_solution(4354487552798937049)
XLA Ops:
  7.2 0.0 all-gather.3.cloned.1.call-start
  7.2 0.7 all-gather.3.cloned.1.call-update
  7.9 2.4 %shard_map.50 = f32[16,128,256]{2,1,0:T(8,128)} custom-call(f32[128,256]{1,0:T(8,128)} %value.1), custom_call_target="tpu_custom_call" | custom-call | tf_op jit(solution)/shard_map/pallas_call | solution.py:267
  10.3 0.0 copy-start.9
  10.3 0.0 copy-start.7
  10.3 7.6 %all-to-all-start.4 = ((f32[16,128,256]{2,1,0:T(8,128)}), f32[16,128,256]{2,1,0:T(8,128)S(1)}, u32[]{:S(2)}, u32[]{:S(2)}) async-start(f32[16,128,256]{2,1,0:T(8,128)} %shard_map.50), calls=%async_computation.4 | async-start | bytes 4194304 | tf_op jit(solution)/shard_map/all_to_all | solution.py:244
  17.9 0.0 copy-done.9
  17.9 4.9 %collective-permute-start = (f32[9,128]{1,0:T(8,128)S(1)}, f32[9,128]{1,0:T(8,128)S(1)}, u32[]{:S(2)}, u32[]{:S(2)}) collective-permute-start(f32[9,128]{1,0:T(8,128)S(1)} %copy-done.9), channel_id=1, source_target_pairs={{0,16},{16,0},{32,48},{48,32},{64,80},{80,64},{96,112},{112,96},{1... | collective-permute-start | bytes 13832 | tf_op jit(solution)/shard_map/ppermute | solution.py:292
  22.8 0.0 copy-done.7
  22.8 0.1 convert_reduce_fusion
  22.9 0.1 pad_add_fusion.place
  23.0 0.6 reduce_max.9
  25.6 0.0 collective-permute-done
  25.6 30.5 %all-gather = f32[32,9,128]{2,1,0:T(8,128)S(1)} all-gather(f32[2,9,128]{2,1,0:T(8,128)S(1)} %pad_maximum_fusion.1), channel_id=2, replica_groups={{0,32,64,96,128,160,192,224,256,288,320,352,384,416,448,480},{16,48,80,..., dimensions={0}, use_global_device_ids=true | all-gather | bytes 156672 | tf_op jit(solution)/shard_map/all_gather | solution.py:293
  56.1 0.0 all-to-all-done.4.iterate_row
  56.1 13.5 %shard_map.51 = (f32[9,32,128]{2,1,0:T(8,128)S(1)}, f32[16,128,256]{2,1,0:T(8,128)}) custom-call(s32[2]{0:T(128)S(1)} %pad_add_fusion.place, s32[32,32]{1,0:T(8,128)S(1)} %copy-done.7, f32[16,2,9,128]{3,2,1,0:T(8,128)S(1)} %bitcast.7, f32[16,128,256]{2,1,0:T(8,128)S(1)} %all-to-all-done.4.iterate_row), custom_call_target="tpu_custom_call" | custom-call | tf_op jit(solution)/shard_map/pallas_call | solution.py:267
  69.7 5.6 %all-to-all-start.5 = ((f32[16,128,256]{2,1,0:T(8,128)}), f32[16,128,256]{2,1,0:T(8,128)S(1)}, u32[]{:S(2)}, u32[]{:S(2)}) async-start(f32[16,128,256]{2,1,0:T(8,128)} %get-tuple-element.91), calls=%async_computation.5 | async-start | bytes 4194304 | tf_op jit(solution)/shard_map/all_to_all | solution.py:244
  75.3 14.5 %all-gather.3.cloned.1.call-done.iterate_col = f32[4096,256]{1,0:T(8,128)} async-done(((f32[128,256]{1,0:T(8,128)}), f32[4096,256]{1,0:T(8,128)}) %all-gather.3.cloned.1.call-update) | async-done | bytes 4194320 | tf_op jit(solution)/shard_map/all_gather | solution.py:286
  89.8 5.1 %shard_map.53 = (bf16[4096,256]{1,0:T(8,128)(2,1)}, bf16[4096,256]{1,0:T(8,128)(2,1)}) custom-call(s32[2]{0:T(128)S(1)} %pad_add_fusion.place, s32[32,32]{1,0:T(8,128)S(1)} %copy-done.7, f32[4096,256]{1,0:T(8,128)} %all-gather.3.cloned.1.call-done.iterate_col), custom_call_target="tpu_custom_call" | custom-call | tf_op jit(solution)/shard_map/pallas_call | solution.py:267
  94.9 3.8 %all-to-all-done.5.one_row = f32[16,128,256]{2,1,0:T(8,128)S(1)} async-done(((f32[16,128,256]{2,1,0:T(8,128)}), f32[16,128,256]{2,1,0:T(8,128)S(1)}, u32[]{:S(2)}, u32[]{:S(2)}) %all-to-all-start.5) | async-done | bytes 2097184 | tf_op jit(solution)/shard_map/all_to_all | solution.py:244
  98.7 0.0 copy-start.5
  98.7 1.3 copy-done.5
  100.0 0.0 copy-start
  100.0 0.0 copy-start.6
  100.1 4.4 %shard_map.54 = (f32[16,8,128]{2,1,0:T(8,128)S(1)}, f32[16,8,128]{2,1,0:T(8,128)S(1)}) custom-call(s32[2]{0:T(128)S(1)} %pad_add_fusion.place, s32[32,32]{1,0:T(8,128)S(1)} %copy-done.7, f32[16,128,256]{2,1,0:T(8,128)} %copy-done.5, bf16[4096,256]{1,0:T(8,128)(2,1)} %get-tuple-element.92.high, bf16[4096,256]{1,0:T(8,128)(2,1)} %get-tuple-element.93.low), custom_call_target="tpu_custom_call" | custom-call | tf_op jit(solution)/shard_map/pallas_call | solution.py:267
  104.5 8.8 %collective-permute-start.1 = (f32[16,8,128]{2,1,0:T(8,128)S(1)}, f32[16,8,128]{2,1,0:T(8,128)S(1)}, u32[]{:S(2)}, u32[]{:S(2)}) collective-permute-start(f32[16,8,128]{2,1,0:T(8,128)S(1)} %get-tuple-element.95), channel_id=1, source_target_pairs={{0,16},{16,0},{32,48},{48,32},{64,80},{80,64},{96,112},{112,96},{1... | collective-permute-start | bytes 196616 | tf_op jit(solution)/shard_map/ppermute | solution.py:340
  113.2 0.9 collective-permute-done.1
  114.2 10.2 %all_to_all.40 = f32[16,2,8,128]{3,2,1,0:T(8,128)} all-to-all(f32[16,2,8,128]{3,2,1,0:T(8,128)S(1)} %copy.9), channel_id=1, replica_groups=mesh['row'=32,'col'=16] {'col'}, dimensions={0} | all-to-all | bytes 262144 | tf_op jit(solution)/shard_map/all_to_all | solution.py:244
  124.4 11.5 %all-to-all-start.7 = ((f32[16,2,8,128]{3,2,1,0:T(8,128)}), f32[16,2,8,128]{3,2,1,0:T(8,128)S(1)}, u32[]{:S(2)}, u32[]{:S(2)}) async-start(f32[16,2,8,128]{3,2,1,0:T(8,128)} %all_to_all.40), calls=%async_computation.7 | async-start | bytes 262144 | tf_op jit(solution)/shard_map/all_to_all | solution.py:343
  135.9 2.6 %shard_map.52 = f32[128,256]{1,0:T(8,128)} custom-call(s32[2]{0:T(128)S(1)} %pad_add_fusion.place, s32[32,32]{1,0:T(8,128)S(1)} %copy-done.7, f32[9,32,128]{2,1,0:T(8,128)S(1)} %get-tuple-element.90.fields), custom_call_target="tpu_custom_call" | custom-call | tf_op jit(solution)/shard_map/pallas_call | solution.py:267
  138.5 9.4 %all-to-all-done.7 = f32[16,2,8,128]{3,2,1,0:T(8,128)S(1)} async-done(((f32[16,2,8,128]{3,2,1,0:T(8,128)}), f32[16,2,8,128]{3,2,1,0:T(8,128)S(1)}, u32[]{:S(2)}, u32[]{:S(2)}) %all-to-all-start.7) | async-done | bytes 131104 | tf_op jit(solution)/shard_map/all_to_all | solution.py:343
  147.9 0.0 copy-done
  147.9 0.0 copy-done.6
  147.9 25.5 %conditional.1 = (f32[128,256]{1,0:T(8,128)S(1)}) conditional(s32[]{:T(128)} %clamp.3, (s32[2]{0:T(128)S(1)}, s32[32,32]{1,0:T(8,128)S(1)}, f32[16,2,8,128]{3,2,1,0:T(8,128)S(1)}, bf16[4096,256]{1,0:T(8,128)(2,1)S(1)}, bf16[4096,256]{1,0:T(8,128)(2,1)}, /*index=5*/f32[128,256]{1,0:T(8,128)S(1)}) %tuple.44, ...), branch_computations={%region_2.0_spmd, %region_3.0_spmd, %region_4.0_spmd, %region_5.0_... | conditional | bytes 12582948 | solution.py:360
  147.9 0.0 copy-start.2
  147.9 1.4 branch_1_fun.2
  149.3 22.1 %all_to_all.37.two_row = f32[16,24,8,128]{3,2,1,0:T(8,128)S(1)} all-to-all(f32[16,24,8,128]{3,2,1,0:T(8,128)S(1)} %branch_1_fun.2), channel_id=1, replica_groups=mesh['row'=32,'col'=16] {'col'}, dimensions={0} | all-to-all | bytes 3145728 | tf_op jit(solution)/shard_map/cond/branch_1_fun/all_to_all | solution.py:244
  171.4 0.0 copy-done.2
  171.4 2.0 %branch_1_fun.3 = f32[128,256]{1,0:T(8,128)S(1)} custom-call(s32[2]{0:T(128)S(1)} %get-tuple-element.59.place, s32[32,32]{1,0:T(8,128)S(1)} %get-tuple-element.60.pattern, f32[16,24,8,128]{3,2,1,0:T(8,128)S(1)} %all_to_all.37.two_row, bf16[4096,256]{1,0:T(8,128)(2,1)S(1)} %get-tuple-element.62.high, bf16[4096,256]{1,0:T(8,128)(2,1)S(1)} %copy-done.2, ...), custom_call_target="tpu_custom_call" | custom-call | tf_op jit(solution)/shard_map/cond/branch_1_fun/pallas_call | solution.py:267
  173.4 0.0 copy-start.8
  173.4 0.6 copy-done.8
  (3 shorter events, 0.0 us)
Async XLA Ops:
  7.2 82.6 %all-gather.3.cloned.1.call-start = ((), (), s32[]{:S(2)}) async-start(), calls=%async_computation.8 | async-start | bytes 4325376 | tf_op jit(solution)/shard_map/all_gather | solution.py:286
  10.3 7.6 %copy-start.9 = (f32[9,128]{1,0:T(8,128)S(1)}, f32[9,128]{1,0:T(8,128)}, u32[]{:S(2)}) copy-start(f32[9,128]{1,0:T(8,128)} %param.7) | copy-start | bytes 13828
  10.3 12.5 %copy-start.7 = (s32[32,32]{1,0:T(8,128)S(1)}, s32[32,32]{1,0:T(8,128)}, u32[]{:S(2)}) copy-start(s32[32,32]{1,0:T(8,128)} %pattern.7) | copy-start | bytes 12292
  10.3 45.8 %all-to-all-start.4 = ((f32[16,128,256]{2,1,0:T(8,128)}), f32[16,128,256]{2,1,0:T(8,128)S(1)}, u32[]{:S(2)}, u32[]{:S(2)}) async-start(f32[16,128,256]{2,1,0:T(8,128)} %shard_map.50), calls=%async_computation.4 | async-start | bytes 4194304 | tf_op jit(solution)/shard_map/all_to_all | solution.py:244
  17.9 7.7 %collective-permute-start = (f32[9,128]{1,0:T(8,128)S(1)}, f32[9,128]{1,0:T(8,128)S(1)}, u32[]{:S(2)}, u32[]{:S(2)}) collective-permute-start(f32[9,128]{1,0:T(8,128)S(1)} %copy-done.9), channel_id=1, source_target_pairs={{0,16},{16,0},{32,48},{48,32},{64,80},{80,64},{96,112},{112,96},{1... | collective-permute-start | bytes 13832 | tf_op jit(solution)/shard_map/ppermute | solution.py:292
  69.7 29.0 %all-to-all-start.5 = ((f32[16,128,256]{2,1,0:T(8,128)}), f32[16,128,256]{2,1,0:T(8,128)S(1)}, u32[]{:S(2)}, u32[]{:S(2)}) async-start(f32[16,128,256]{2,1,0:T(8,128)} %get-tuple-element.91), calls=%async_computation.5 | async-start | bytes 4194304 | tf_op jit(solution)/shard_map/all_to_all | solution.py:244
  98.7 1.3 copy-start.5
  100.0 47.8 %copy-start = (bf16[4096,256]{1,0:T(8,128)(2,1)S(1)}, bf16[4096,256]{1,0:T(8,128)(2,1)}, u32[]{:S(2)}) copy-start(bf16[4096,256]{1,0:T(8,128)(2,1)} %get-tuple-element.92.high) | copy-start | bytes 6291460
  100.0 47.8 %copy-start.6 = (f32[128,256]{1,0:T(8,128)S(1)}, f32[128,256]{1,0:T(8,128)}, u32[]{:S(2)}) copy-start(f32[128,256]{1,0:T(8,128)} %value.1) | copy-start | bytes 393220
  104.5 9.7 %collective-permute-start.1 = (f32[16,8,128]{2,1,0:T(8,128)S(1)}, f32[16,8,128]{2,1,0:T(8,128)S(1)}, u32[]{:S(2)}, u32[]{:S(2)}) collective-permute-start(f32[16,8,128]{2,1,0:T(8,128)S(1)} %get-tuple-element.95), channel_id=1, source_target_pairs={{0,16},{16,0},{32,48},{48,32},{64,80},{80,64},{96,112},{112,96},{1... | collective-permute-start | bytes 196616 | tf_op jit(solution)/shard_map/ppermute | solution.py:340
  124.4 23.5 %all-to-all-start.7 = ((f32[16,2,8,128]{3,2,1,0:T(8,128)}), f32[16,2,8,128]{3,2,1,0:T(8,128)S(1)}, u32[]{:S(2)}, u32[]{:S(2)}) async-start(f32[16,2,8,128]{3,2,1,0:T(8,128)} %all_to_all.40), calls=%async_computation.7 | async-start | bytes 262144 | tf_op jit(solution)/shard_map/all_to_all | solution.py:343
  147.9 23.5 %copy-start.2 = (bf16[4096,256]{1,0:T(8,128)(2,1)S(1)}, bf16[4096,256]{1,0:T(8,128)(2,1)}, u32[]{:S(2)}) copy-start(bf16[4096,256]{1,0:T(8,128)(2,1)} %get-tuple-element.63.low) | copy-start | bytes 6291460 | tf_op jit(solution)/shard_map/cond
  173.4 0.7 copy-start.8
Sparse Core Ops, SparseCore 0:
  10.1 79.6 all-gather.2

commit v11 on v10

--- a/solution.py
+++ b/solution.py
@@ -30,8 +30,8 @@
     return lax.dot_general(left, right, (((1,), (1,)), ((), ())), preferred_element_type=jnp.float32)
 
 
-def half_tile(fields_ref, left_ref, tile_ref, half, block):
-    right = [fields_ref[f, pl.ds(block, 1), :] for f in range(FIELDS)]
+def half_tile(fields_ref, left_ref, tile_ref, half, core, block):
+    right = [row_of(fields_ref, core, block, f) for f in range(FIELDS)]
 
     def chunk(step, carry):
         rows = pl.ds(pl.multiple_of(step * CHUNK, CHUNK), CHUNK)
@@ -53,14 +53,14 @@
     lax.fori_loop(0, BLOCK // CHUNK, chunk, 0)
 
 
-def slot(core, block):
-    return (core ^ (block % 2)) * (NB // 2) + block // 2
+def row_of(fields, core, block, f):
+    return fields[block // 2, core ^ (block % 2), f : f + 1, :]
 
 
 def spread_own(fields, left, core, col):
     for half in range(2):
         for f in range(FIELDS):
-            own = fields[f, pl.ds(slot(core, 2 * col + half), 1), :]
+            own = row_of(fields, core, 2 * col + half, f)
             left[half, f] = jnp.broadcast_to(own, (BLOCK, BLOCK)).T
 
 
@@ -72,26 +72,9 @@
         move.wait()
 
 
-def first_kernel(place, pattern, records, iterate_row, fields, copies, left, tile, high, low, one, sems):
+def first_kernel(place, pattern, fields, iterate_row, copies, left, tile, high, low, one, sems):
     row, col = place[0], place[1]
     core = row % 2
-    for part in range(2):
-        half_table = slice(part * NB // 2, (part + 1) * NB // 2)
-        exponents = [records[:, part, 3 + p, :] for p in range(PRIMS)]
-        coefficients = [records[:, part, 3 + PRIMS + p, :] for p in range(PRIMS)]
-        roots = [jnp.sqrt(e) for e in exponents]
-        norm = jnp.zeros_like(exponents[0])
-        for p in range(PRIMS):
-            for q in range(PRIMS):
-                ratio = 2.0 * roots[p] * roots[q] / (exponents[p] + exponents[q])
-                norm = norm + coefficients[p] * coefficients[q] * (ratio * jnp.sqrt(ratio))
-        scale = (2.0**0.75) * lax.rsqrt(norm)
-        for f in range(3):
-            fields[f, half_table] = records[:, part, f, :]
-        for p in range(PRIMS):
-            weight = jnp.exp2(jnp.log2(coefficients[p] * scale) * (1.0 / 3.0))
-            fields[3 + p, half_table] = exponents[p]
-            fields[6 + p, half_table] = weight * jnp.sqrt(roots[p])
     spread_own(fields, left, core, col)
 
     def step(index, carry):
@@ -103,7 +86,7 @@
 
         @pl.when(needed != 0)
         def _():
-            half_tile(fields, left, tile, half, slot(core, block))
+            half_tile(fields, left, tile, half, core, block)
             high[lanes, rows], low[lanes, rows] = split(tile[...])
 
         @pl.when(needed == 0)
@@ -134,7 +117,7 @@
 
         @pl.when(margin_live)
         def _():
-            half_tile(fields, left, tile, half, slot(row % 2, row))
+            half_tile(fields, left, tile, half, row % 2, row)
             margin[:, lanes] = tile[...].T
 
         @pl.when(jnp.logical_not(margin_live))
@@ -142,8 +125,25 @@
             margin[:, lanes] = jnp.zeros((BLOCK, BLOCK), jnp.float32)
 
 
-def hbm_copies_kernel(value, copies, sems):
-    send_copies(value, copies, sems)
+def start_kernel(records, value, fields, copies, sems):
+    moves = [pltpu.make_async_copy(value, copies.at[k], sems.at[k]) for k in range(16)]
+    for move in moves:
+        move.start()
+    exponents = [records[3 + p : 4 + p, :] for p in range(PRIMS)]
+    coefficients = [records[3 + PRIMS + p : 4 + PRIMS + p, :] for p in range(PRIMS)]
+    roots = [jnp.sqrt(e) for e in exponents]
+    norm = jnp.zeros_like(exponents[0])
+    for p in range(PRIMS):
+        for q in range(PRIMS):
+            ratio = 2.0 * roots[p] * roots[q] / (exponents[p] + exponents[q])
+            norm = norm + coefficients[p] * coefficients[q] * (ratio * jnp.sqrt(ratio))
+    scale = (2.0**0.75) * lax.rsqrt(norm)
+    fields[:6, :] = records[:6, :]
+    for p in range(PRIMS):
+        weight = jnp.exp2(jnp.log2(coefficients[p] * scale) * (1.0 / 3.0))
+        fields[6 + p : 7 + p, :] = weight * jnp.sqrt(roots[p])
+    for move in moves:
+        move.wait()
 
 
 def list_live(pattern, row, order):
@@ -288,23 +288,23 @@
     partner = [(r, r ^ 1) for r in range(NB)]
     left = VMEM((2, FIELDS, BLOCK, BLOCK), jnp.float32)
     square = VMEM((BLOCK, BLOCK), jnp.float32)
-    table = VMEM((FIELDS, NB, BLOCK), jnp.float32)
-    both = jnp.stack([records, lax.ppermute(records, "row", partner)])
-    everyone = lax.all_gather(both, "row", axis=0, axis_index_groups=cores)
+    table = VMEM((FIELDS, BLOCK), jnp.float32)
     sems = pltpu.SemaphoreType.DMA((16,))
     wide = VMEM((2 * BLOCK, NB * BLOCK), jnp.bfloat16)
-    copies = call(hbm_copies_kernel, tiles, [sems], iterate, outs=(HBM,), scalars=0)
+    own, copies = call(start_kernel, (table, tiles), [sems], records, iterate, outs=(VMEM, HBM), scalars=0)
+    both = jnp.stack([own, lax.ppermute(own, "row", partner)])
+    fields = lax.all_gather(both, "row", axis=0, axis_index_groups=cores)
     iterate_row = exchange(copies, "col")
-    fields, product_one = call(
+    product_one = call(
         first_kernel,
-        (table, tiles),
+        tiles,
         [left, square, wide, wide, VMEM((BLOCK, 2 * BLOCK), jnp.float32), sems],
         place,
         pattern,
-        everyone,
+        fields,
         iterate_row,
         on_chip=(2, 3),
-        outs=(VMEM, HBM),
+        outs=(HBM,),
     )
     margin = call(margin_kernel, tile, [left, square], place, pattern, fields, on_chip=(2,))
     one_row = exchange(product_one, "col")

time: 184 us -> 183 us (level)
  starting transfers between devices: 38.4 us -> 36 us
  blocking collectives: 62.8 us -> 64.9 us
where the time goes in v11:
time: 183 us; the launch traced here: 180 us
  blocking collectives  64.9 us (35%)
  starting transfers between devices  36 us (20%)
  Pallas kernels  30.4 us (17%)
  waiting for transfers between devices  28.8 us (16%)
  between operations  16.1 us (9%)
  local copies, waits for them, and re-layouts  2.69 us (1%)
    all_to_all x2, blocking collectives, exchange(): return lax.all_to_all(pieces, axis, 0, 0, tiled=True)  34.1 us
    all_gather x1, blocking collectives, stages(): fields = lax.all_gather(both, 'row', axis=0, axis_index_groups=cores)  30.9 us
    pallas_call x7, Pallas kernels, call(): pl.pallas_call(kernel, out_shape=out_shapes, grid=grid, in_specs=in_specs...  30.4 us
    all_gather x1, waiting for transfers between devices, stages(): iterate_col = lax.all_gather(iterate, 'row', axis=0, tiled=True)  15.5 us
    all_to_all x2, starting transfers between devices, exchange(): return lax.all_to_all(pieces, axis, 0, 0, tiled=True)  12.1 us
    all_to_all x1, starting transfers between devices, stages(): lax.all_to_all(slices, 'row', 0, 0, tiled=True, axis_index_groups=cores)  10.2 us
    all_to_all x1, waiting for transfers between devices, stages(): lax.all_to_all(slices, 'row', 0, 0, tiled=True, axis_index_groups=cores)  9.41 us
    ppermute x1, starting transfers between devices, stages(): given = lax.ppermute(given, 'row', partner)  8.67 us
  transfers between devices with their start and end apart: 6, of which 4 were waited for; matrix products, arithmetic and copies ran while one was open for 0% of the time, Pallas kernels for 13%

profile of v11, /device:TPU:1, one launch (start us, length us, event | category | flops | bytes accessed | tf_op | source)
XLA Modules:
  0.0 179.8 jit_solution(5937667949749843637)
XLA Ops:
  7.2 0.0 all-gather.3.cloned.1.call-start
  7.2 0.7 all-gather.3.cloned.1.call-update
  7.9 0.0 copy-start.5
  7.9 0.7 copy-done.5
  8.6 2.4 %shard_map.50 = (f32[9,128]{1,0:T(8,128)S(1)}, f32[16,128,256]{2,1,0:T(8,128)}) custom-call(f32[9,128]{1,0:T(8,128)S(1)} %copy-done.5, f32[128,256]{1,0:T(8,128)} %value.1), custom_call_target="tpu_custom_call" | custom-call | tf_op jit(solution)/shard_map/pallas_call | solution.py:267
  11.0 0.0 copy-start.8
  11.0 7.6 %all-to-all-start.4 = ((f32[16,128,256]{2,1,0:T(8,128)}), f32[16,128,256]{2,1,0:T(8,128)S(1)}, u32[]{:S(2)}, u32[]{:S(2)}) async-start(f32[16,128,256]{2,1,0:T(8,128)} %get-tuple-element.91), calls=%async_computation.4 | async-start | bytes 4194304 | tf_op jit(solution)/shard_map/all_to_all | solution.py:244
  18.6 4.9 %collective-permute-start = (f32[9,128]{1,0:T(8,128)S(1)}, f32[9,128]{1,0:T(8,128)S(1)}, u32[]{:S(2)}, u32[]{:S(2)}) collective-permute-start(f32[9,128]{1,0:T(8,128)S(1)} %get-tuple-element.90), channel_id=1, source_target_pairs={{0,16},{16,0},{32,48},{48,32},{64,80},{80,64},{96,112},{112,96},{1... | collective-permute-start | bytes 13832 | tf_op jit(solution)/shard_map/ppermute | solution.py:295
  23.5 0.0 copy-done.8
  23.5 0.1 convert_reduce_fusion
  23.6 0.1 pad_add_fusion.place
  23.7 0.6 reduce_max.9
  26.3 0.0 collective-permute-done
  26.3 30.9 %all-gather = f32[32,9,128]{2,1,0:T(8,128)S(1)} all-gather(f32[2,9,128]{2,1,0:T(8,128)S(1)} %pad_maximum_fusion.1), channel_id=2, replica_groups={{0,32,64,96,128,160,192,224,256,288,320,352,384,416,448,480},{16,48,80,..., dimensions={0}, use_global_device_ids=true | all-gather | bytes 156672 | tf_op jit(solution)/shard_map/all_gather | solution.py:296
  57.2 0.0 all-to-all-done.4.iterate_row
  57.2 12.6 %shard_map.52 = f32[16,128,256]{2,1,0:T(8,128)} custom-call(s32[2]{0:T(128)S(1)} %pad_add_fusion.place, s32[32,32]{1,0:T(8,128)S(1)} %copy-done.8, f32[16,2,9,128]{3,2,1,0:T(8,128)S(1)} %bitcast.7, f32[16,128,256]{2,1,0:T(8,128)S(1)} %all-to-all-done.4.iterate_row), custom_call_target="tpu_custom_call" | custom-call | tf_op jit(solution)/shard_map/pallas_call | solution.py:267
  69.7 4.5 %all-to-all-start.5 = ((f32[16,128,256]{2,1,0:T(8,128)}), f32[16,128,256]{2,1,0:T(8,128)S(1)}, u32[]{:S(2)}, u32[]{:S(2)}) async-start(f32[16,128,256]{2,1,0:T(8,128)} %shard_map.52), calls=%async_computation.5 | async-start | bytes 4194304 | tf_op jit(solution)/shard_map/all_to_all | solution.py:244
  74.3 15.5 %all-gather.3.cloned.1.call-done.iterate_col = f32[4096,256]{1,0:T(8,128)} async-done(((f32[128,256]{1,0:T(8,128)}), f32[4096,256]{1,0:T(8,128)}) %all-gather.3.cloned.1.call-update) | async-done | bytes 4194320 | tf_op jit(solution)/shard_map/all_gather | solution.py:286
  89.8 5.1 %shard_map.53 = (bf16[4096,256]{1,0:T(8,128)(2,1)}, bf16[4096,256]{1,0:T(8,128)(2,1)}) custom-call(s32[2]{0:T(128)S(1)} %pad_add_fusion.place, s32[32,32]{1,0:T(8,128)S(1)} %copy-done.8, f32[4096,256]{1,0:T(8,128)} %all-gather.3.cloned.1.call-done.iterate_col), custom_call_target="tpu_custom_call" | custom-call | tf_op jit(solution)/shard_map/pallas_call | solution.py:267
  94.9 2.3 %all-to-all-done.5.one_row = f32[16,128,256]{2,1,0:T(8,128)S(1)} async-done(((f32[16,128,256]{2,1,0:T(8,128)}), f32[16,128,256]{2,1,0:T(8,128)S(1)}, u32[]{:S(2)}, u32[]{:S(2)}) %all-to-all-start.5) | async-done | bytes 2097184 | tf_op jit(solution)/shard_map/all_to_all | solution.py:244
  97.2 0.0 copy-start.6
  97.2 1.3 copy-done.6
  98.5 0.0 copy-start
  98.5 0.0 copy-start.7
  98.5 4.4 %shard_map.54 = (f32[16,8,128]{2,1,0:T(8,128)S(1)}, f32[16,8,128]{2,1,0:T(8,128)S(1)}) custom-call(s32[2]{0:T(128)S(1)} %pad_add_fusion.place, s32[32,32]{1,0:T(8,128)S(1)} %copy-done.8, f32[16,128,256]{2,1,0:T(8,128)} %copy-done.6, bf16[4096,256]{1,0:T(8,128)(2,1)} %get-tuple-element.92.high, bf16[4096,256]{1,0:T(8,128)(2,1)} %get-tuple-element.93.low), custom_call_target="tpu_custom_call" | custom-call | tf_op jit(solution)/shard_map/pallas_call | solution.py:267
  102.9 8.7 %collective-permute-start.1 = (f32[16,8,128]{2,1,0:T(8,128)S(1)}, f32[16,8,128]{2,1,0:T(8,128)S(1)}, u32[]{:S(2)}, u32[]{:S(2)}) collective-permute-start(f32[16,8,128]{2,1,0:T(8,128)S(1)} %get-tuple-element.95), channel_id=1, source_target_pairs={{0,16},{16,0},{32,48},{48,32},{64,80},{80,64},{96,112},{112,96},{1... | collective-permute-start | bytes 196616 | tf_op jit(solution)/shard_map/ppermute | solution.py:340
  111.6 0.9 collective-permute-done.1
  112.5 12.0 %all_to_all.40 = f32[16,2,8,128]{3,2,1,0:T(8,128)} all-to-all(f32[16,2,8,128]{3,2,1,0:T(8,128)S(1)} %copy.9), channel_id=1, replica_groups=mesh['row'=32,'col'=16] {'col'}, dimensions={0} | all-to-all | bytes 262144 | tf_op jit(solution)/shard_map/all_to_all | solution.py:244
  124.5 10.2 %all-to-all-start.7 = ((f32[16,2,8,128]{3,2,1,0:T(8,128)}), f32[16,2,8,128]{3,2,1,0:T(8,128)S(1)}, u32[]{:S(2)}, u32[]{:S(2)}) async-start(f32[16,2,8,128]{3,2,1,0:T(8,128)} %all_to_all.40), calls=%async_computation.7 | async-start | bytes 262144 | tf_op jit(solution)/shard_map/all_to_all | solution.py:343
  134.8 2.6 %shard_map.51 = f32[128,256]{1,0:T(8,128)} custom-call(s32[2]{0:T(128)S(1)} %pad_add_fusion.place, s32[32,32]{1,0:T(8,128)S(1)} %copy-done.8, f32[16,2,9,128]{3,2,1,0:T(8,128)S(1)} %bitcast.8), custom_call_target="tpu_custom_call" | custom-call | tf_op jit(solution)/shard_map/pallas_call | solution.py:267
  137.4 9.4 %all-to-all-done.7 = f32[16,2,8,128]{3,2,1,0:T(8,128)S(1)} async-done(((f32[16,2,8,128]{3,2,1,0:T(8,128)}), f32[16,2,8,128]{3,2,1,0:T(8,128)S(1)}, u32[]{:S(2)}, u32[]{:S(2)}) %all-to-all-start.7) | async-done | bytes 131104 | tf_op jit(solution)/shard_map/all_to_all | solution.py:343
  146.8 0.0 copy-done
  146.8 0.0 copy-done.7
  146.8 25.5 %conditional.1 = (f32[128,256]{1,0:T(8,128)S(1)}) conditional(s32[]{:T(128)} %clamp.3, (s32[2]{0:T(128)S(1)}, s32[32,32]{1,0:T(8,128)S(1)}, f32[16,2,8,128]{3,2,1,0:T(8,128)S(1)}, bf16[4096,256]{1,0:T(8,128)(2,1)S(1)}, bf16[4096,256]{1,0:T(8,128)(2,1)}, /*index=5*/f32[128,256]{1,0:T(8,128)S(1)}) %tuple.44, ...), branch_computations={%region_2.0_spmd, %region_3.0_spmd, %region_4.0_spmd, %region_5.0_... | conditional | bytes 12582948 | solution.py:360
  146.8 0.0 copy-start.2
  146.8 1.4 branch_1_fun.2
  148.2 22.1 %all_to_all.37.two_row = f32[16,24,8,128]{3,2,1,0:T(8,128)S(1)} all-to-all(f32[16,24,8,128]{3,2,1,0:T(8,128)S(1)} %branch_1_fun.2), channel_id=1, replica_groups=mesh['row'=32,'col'=16] {'col'}, dimensions={0} | all-to-all | bytes 3145728 | tf_op jit(solution)/shard_map/cond/branch_1_fun/all_to_all | solution.py:244
  170.3 0.0 copy-done.2
  170.3 2.0 %branch_1_fun.3 = f32[128,256]{1,0:T(8,128)S(1)} custom-call(s32[2]{0:T(128)S(1)} %get-tuple-element.59.place, s32[32,32]{1,0:T(8,128)S(1)} %get-tuple-element.60.pattern, f32[16,24,8,128]{3,2,1,0:T(8,128)S(1)} %all_to_all.37.two_row, bf16[4096,256]{1,0:T(8,128)(2,1)S(1)} %get-tuple-element.62.high, bf16[4096,256]{1,0:T(8,128)(2,1)S(1)} %copy-done.2, ...), custom_call_target="tpu_custom_call" | custom-call | tf_op jit(solution)/shard_map/cond/branch_1_fun/pallas_call | solution.py:267
  172.3 0.0 copy-start.9
  172.3 0.6 copy-done.9
  (3 shorter events, 0.0 us)
Async XLA Ops:
  7.2 82.6 %all-gather.3.cloned.1.call-start = ((), (), s32[]{:S(2)}) async-start(), calls=%async_computation.8 | async-start | bytes 4325376 | tf_op jit(solution)/shard_map/all_gather | solution.py:286
  7.9 0.7 copy-start.5
  11.0 12.5 %copy-start.8 = (s32[32,32]{1,0:T(8,128)S(1)}, s32[32,32]{1,0:T(8,128)}, u32[]{:S(2)}) copy-start(s32[32,32]{1,0:T(8,128)} %pattern.7) | copy-start | bytes 12292
  11.0 46.2 %all-to-all-start.4 = ((f32[16,128,256]{2,1,0:T(8,128)}), f32[16,128,256]{2,1,0:T(8,128)S(1)}, u32[]{:S(2)}, u32[]{:S(2)}) async-start(f32[16,128,256]{2,1,0:T(8,128)} %get-tuple-element.91), calls=%async_computation.4 | async-start | bytes 4194304 | tf_op jit(solution)/shard_map/all_to_all | solution.py:244
  18.6 7.7 %collective-permute-start = (f32[9,128]{1,0:T(8,128)S(1)}, f32[9,128]{1,0:T(8,128)S(1)}, u32[]{:S(2)}, u32[]{:S(2)}) collective-permute-start(f32[9,128]{1,0:T(8,128)S(1)} %get-tuple-element.90), channel_id=1, source_target_pairs={{0,16},{16,0},{32,48},{48,32},{64,80},{80,64},{96,112},{112,96},{1... | collective-permute-start | bytes 13832 | tf_op jit(solution)/shard_map/ppermute | solution.py:295
  69.7 27.4 %all-to-all-start.5 = ((f32[16,128,256]{2,1,0:T(8,128)}), f32[16,128,256]{2,1,0:T(8,128)S(1)}, u32[]{:S(2)}, u32[]{:S(2)}) async-start(f32[16,128,256]{2,1,0:T(8,128)} %shard_map.52), calls=%async_computation.5 | async-start | bytes 4194304 | tf_op jit(solution)/shard_map/all_to_all | solution.py:244
  97.2 1.3 copy-start.6
  98.5 48.3 %copy-start = (bf16[4096,256]{1,0:T(8,128)(2,1)S(1)}, bf16[4096,256]{1,0:T(8,128)(2,1)}, u32[]{:S(2)}) copy-start(bf16[4096,256]{1,0:T(8,128)(2,1)} %get-tuple-element.92.high) | copy-start | bytes 6291460
  98.5 48.3 %copy-start.7 = (f32[128,256]{1,0:T(8,128)S(1)}, f32[128,256]{1,0:T(8,128)}, u32[]{:S(2)}) copy-start(f32[128,256]{1,0:T(8,128)} %value.1) | copy-start | bytes 393220
  102.9 9.6 %collective-permute-start.1 = (f32[16,8,128]{2,1,0:T(8,128)S(1)}, f32[16,8,128]{2,1,0:T(8,128)S(1)}, u32[]{:S(2)}, u32[]{:S(2)}) collective-permute-start(f32[16,8,128]{2,1,0:T(8,128)S(1)} %get-tuple-element.95), channel_id=1, source_target_pairs={{0,16},{16,0},{32,48},{48,32},{64,80},{80,64},{96,112},{112,96},{1... | collective-permute-start | bytes 196616 | tf_op jit(solution)/shard_map/ppermute | solution.py:340
  124.5 22.2 %all-to-all-start.7 = ((f32[16,2,8,128]{3,2,1,0:T(8,128)}), f32[16,2,8,128]{3,2,1,0:T(8,128)S(1)}, u32[]{:S(2)}, u32[]{:S(2)}) async-start(f32[16,2,8,128]{3,2,1,0:T(8,128)} %all_to_all.40), calls=%async_computation.7 | async-start | bytes 262144 | tf_op jit(solution)/shard_map/all_to_all | solution.py:343
  146.8 23.5 %copy-start.2 = (bf16[4096,256]{1,0:T(8,128)(2,1)S(1)}, bf16[4096,256]{1,0:T(8,128)(2,1)}, u32[]{:S(2)}) copy-start(bf16[4096,256]{1,0:T(8,128)(2,1)} %get-tuple-element.63.low) | copy-start | bytes 6291460 | tf_op jit(solution)/shard_map/cond
  172.3 0.7 copy-start.9
Sparse Core Ops, SparseCore 0:
  10.1 79.6 all-gather.2

commit v12 on v11

--- a/solution.py
+++ b/solution.py
@@ -277,9 +277,6 @@
 
 def stages(records, pattern, iterate):
     place = jnp.stack([lax.axis_index("row"), lax.axis_index("col")]).astype(jnp.int32)
-    fullest = jnp.max(jnp.sum((pattern != 0).astype(jnp.int32), axis=1))
-    choice = sum((fullest > room).astype(jnp.int32) for room in ROOMS[:-1])
-    place, choice = lax.optimization_barrier((place, choice))
     tile = jax.ShapeDtypeStruct((BLOCK, 2 * BLOCK), jnp.float32)
     stored = HBM((NB * BLOCK, 2 * BLOCK), jnp.bfloat16)
     tiles = HBM((16, BLOCK, 2 * BLOCK), jnp.float32)
@@ -307,6 +304,9 @@
         outs=(HBM,),
     )
     margin = call(margin_kernel, tile, [left, square], place, pattern, fields, on_chip=(2,))
+    product_one, late = lax.optimization_barrier((product_one, pattern))
+    fullest = jnp.max(jnp.sum((late != 0).astype(jnp.int32), axis=1))
+    choice = sum((fullest > room).astype(jnp.int32) for room in ROOMS[:-1])
     one_row = exchange(product_one, "col")
     window = (PANEL, 2 * BLOCK)
     high, low = call(
@@ -321,6 +321,7 @@
         blocks={2: window},
         stay=(2,),
     )
+    high, choice = lax.optimization_barrier((high, choice))
     half = VMEM((16, 8, BLOCK), jnp.float32)
     turned = VMEM((2, BLOCK, BLOCK), jnp.float32)
     window = (PART, 2 * BLOCK)
@@ -350,7 +351,7 @@
             copies = call(compact_kernel, copies, [order, line], place, pattern, slices, on_chip=(2,))
             two_row = exchange(copies, "col")
             return call(
-                third_kernel, tile, [order], place, pattern, two_row, high, low, iterate, on_chip=(2, 3, 4)
+                third_kernel, HBM((BLOCK, 2 * BLOCK), jnp.float32), [order], place, pattern, two_row, high, low, iterate, on_chip=(2, 3, 4)
             )
 
         return branch

time: 183 us -> 181 us (0.989)
  waiting for transfers between devices: 28.8 us -> 26.6 us
    all_to_all x2, waiting for transfers between devices: 2.33 us -> 0.28 us  [exchange(): return lax.all_to_all(pieces, axis, 0, 0, tiled=True)]
  transfers between devices with their start and end apart: 6 -> 6, of which waited for: 4 -> 5; matrix products, arithmetic and copies ran while one was open for 0% -> 0% of each run, Pallas kernels for 13% -> 13%
where the time goes in v12:
time: 181 us; the launch traced here: 178 us
  blocking collectives  64.8 us (36%)
  starting transfers between devices  36.5 us (20%)
  Pallas kernels  31.1 us (17%)
  waiting for transfers between devices  26.6 us (15%)
  between operations  16.1 us (9%)
  local copies, waits for them, and re-layouts  2.04 us (1%)
    all_to_all x2, blocking collectives, exchange(): return lax.all_to_all(pieces, axis, 0, 0, tiled=True)  34.2 us
    pallas_call x7, Pallas kernels, call(): pl.pallas_call(kernel, out_shape=out_shapes, grid=grid, in_specs=in_specs...  31.1 us
    all_gather x1, blocking collectives, stages(): fields = lax.all_gather(both, 'row', axis=0, axis_index_groups=cores)  30.6 us
    all_gather x1, waiting for transfers between devices, stages(): iterate_col = lax.all_gather(iterate, 'row', axis=0, tiled=True)  14.6 us
    all_to_all x2, starting transfers between devices, exchange(): return lax.all_to_all(pieces, axis, 0, 0, tiled=True)  12.5 us
    all_to_all x1, starting transfers between devices, stages(): lax.all_to_all(slices, 'row', 0, 0, tiled=True, axis_index_groups=cores)  10.5 us
    all_to_all x1, waiting for transfers between devices, stages(): lax.all_to_all(slices, 'row', 0, 0, tiled=True, axis_index_groups=cores)  9.41 us
    ppermute x1, starting transfers between devices, stages(): given = lax.ppermute(given, 'row', partner)  8.65 us
  transfers between devices with their start and end apart: 6, of which 5 were waited for; matrix products, arithmetic and copies ran while one was open for 0% of the time, Pallas kernels for 13%

profile of v12, /device:TPU:1, one launch (start us, length us, event | category | flops | bytes accessed | tf_op | source)
XLA Modules:
  0.0 178.0 jit_solution(15320786586161809660)
XLA Ops:
  7.2 0.0 all-gather.3.cloned.1.call-start
  7.2 0.7 all-gather.3.cloned.1.call-update
  7.9 0.0 copy-start.5
  7.9 0.7 copy-done.5
  8.6 2.4 %shard_map.50 = (f32[9,128]{1,0:T(8,128)S(1)}, f32[16,128,256]{2,1,0:T(8,128)}) custom-call(f32[9,128]{1,0:T(8,128)S(1)} %copy-done.5, f32[128,256]{1,0:T(8,128)} %value.1), custom_call_target="tpu_custom_call" | custom-call | tf_op jit(solution)/shard_map/pallas_call | solution.py:267
  11.0 0.0 copy-start.8
  11.0 7.6 %all-to-all-start.4 = ((f32[16,128,256]{2,1,0:T(8,128)}), f32[16,128,256]{2,1,0:T(8,128)S(1)}, u32[]{:S(2)}, u32[]{:S(2)}) async-start(f32[16,128,256]{2,1,0:T(8,128)} %get-tuple-element.92), calls=%async_computation.4 | async-start | bytes 4194304 | tf_op jit(solution)/shard_map/all_to_all | solution.py:244
  18.6 4.9 %collective-permute-start = (f32[9,128]{1,0:T(8,128)S(1)}, f32[9,128]{1,0:T(8,128)S(1)}, u32[]{:S(2)}, u32[]{:S(2)}) collective-permute-start(f32[9,128]{1,0:T(8,128)S(1)} %get-tuple-element.91), channel_id=1, source_target_pairs={{0,16},{16,0},{32,48},{48,32},{64,80},{80,64},{96,112},{112,96},{1... | collective-permute-start | bytes 13832 | tf_op jit(solution)/shard_map/ppermute | solution.py:292
  23.5 0.1 pad_add_fusion.place
  23.6 0.7 collective-permute-done
  24.3 30.6 %all-gather = f32[32,9,128]{2,1,0:T(8,128)S(1)} all-gather(f32[2,9,128]{2,1,0:T(8,128)S(1)} %pad_maximum_fusion.1), channel_id=2, replica_groups={{0,32,64,96,128,160,192,224,256,288,320,352,384,416,448,480},{16,48,80,..., dimensions={0}, use_global_device_ids=true | all-gather | bytes 156672 | tf_op jit(solution)/shard_map/all_gather | solution.py:293
  54.9 0.0 all-to-all-done.4.iterate_row
  54.9 0.0 copy-done.8
  54.9 12.6 %shard_map.52 = f32[16,128,256]{2,1,0:T(8,128)} custom-call(s32[2]{0:T(128)S(1)} %pad_add_fusion.place, s32[32,32]{1,0:T(8,128)S(1)} %copy-done.8, f32[16,2,9,128]{3,2,1,0:T(8,128)S(1)} %bitcast.7, f32[16,128,256]{2,1,0:T(8,128)S(1)} %all-to-all-done.4.iterate_row), custom_call_target="tpu_custom_call" | custom-call | tf_op jit(solution)/shard_map/pallas_call | solution.py:267
  67.5 4.9 %all-to-all-start.5 = ((f32[16,128,256]{2,1,0:T(8,128)}), f32[16,128,256]{2,1,0:T(8,128)S(1)}, u32[]{:S(2)}, u32[]{:S(2)}) async-start(f32[16,128,256]{2,1,0:T(8,128)} %shard_map.52), calls=%async_computation.5 | async-start | bytes 4194304 | tf_op jit(solution)/shard_map/all_to_all | solution.py:244
  72.4 0.1 convert_reduce_fusion
  72.5 0.6 reduce_max.9
  75.1 14.6 %all-gather.3.cloned.1.call-done.iterate_col = f32[4096,256]{1,0:T(8,128)} async-done(((f32[128,256]{1,0:T(8,128)}), f32[4096,256]{1,0:T(8,128)}) %all-gather.3.cloned.1.call-update) | async-done | bytes 4194320 | tf_op jit(solution)/shard_map/all_gather | solution.py:283
  89.7 5.1 %shard_map.53 = (bf16[4096,256]{1,0:T(8,128)(2,1)}, bf16[4096,256]{1,0:T(8,128)(2,1)}) custom-call(s32[2]{0:T(128)S(1)} %pad_add_fusion.place, s32[32,32]{1,0:T(8,128)S(1)} %copy-done.8, f32[4096,256]{1,0:T(8,128)} %all-gather.3.cloned.1.call-done.iterate_col), custom_call_target="tpu_custom_call" | custom-call | tf_op jit(solution)/shard_map/pallas_call | solution.py:267
  94.8 0.3 all-to-all-done.5.one_row
  95.1 0.0 copy-start.6
  95.1 1.3 copy-done.6
  96.4 0.0 copy-start
  96.4 0.0 copy-start.7
  96.4 4.4 %shard_map.54 = (f32[16,8,128]{2,1,0:T(8,128)S(1)}, f32[16,8,128]{2,1,0:T(8,128)S(1)}) custom-call(s32[2]{0:T(128)S(1)} %pad_add_fusion.place, s32[32,32]{1,0:T(8,128)S(1)} %copy-done.8, f32[16,128,256]{2,1,0:T(8,128)} %copy-done.6, bf16[4096,256]{1,0:T(8,128)(2,1)} %get-tuple-element.96.high, bf16[4096,256]{1,0:T(8,128)(2,1)} %get-tuple-element.97.low), custom_call_target="tpu_custom_call" | custom-call | tf_op jit(solution)/shard_map/pallas_call | solution.py:267
  100.8 8.7 %collective-permute-start.1 = (f32[16,8,128]{2,1,0:T(8,128)S(1)}, f32[16,8,128]{2,1,0:T(8,128)S(1)}, u32[]{:S(2)}, u32[]{:S(2)}) collective-permute-start(f32[16,8,128]{2,1,0:T(8,128)S(1)} %get-tuple-element.99), channel_id=1, source_target_pairs={{0,16},{16,0},{32,48},{48,32},{64,80},{80,64},{96,112},{112,96},{1... | collective-permute-start | bytes 196616 | tf_op jit(solution)/shard_map/ppermute | solution.py:341
  109.5 0.9 collective-permute-done.1
  110.4 12.1 %all_to_all.40 = f32[16,2,8,128]{3,2,1,0:T(8,128)} all-to-all(f32[16,2,8,128]{3,2,1,0:T(8,128)S(1)} %copy.9), channel_id=1, replica_groups=mesh['row'=32,'col'=16] {'col'}, dimensions={0} | all-to-all | bytes 262144 | tf_op jit(solution)/shard_map/all_to_all | solution.py:244
  122.5 10.5 %all-to-all-start.7 = ((f32[16,2,8,128]{3,2,1,0:T(8,128)}), f32[16,2,8,128]{3,2,1,0:T(8,128)S(1)}, u32[]{:S(2)}, u32[]{:S(2)}) async-start(f32[16,2,8,128]{3,2,1,0:T(8,128)} %all_to_all.40), calls=%async_computation.7 | async-start | bytes 262144 | tf_op jit(solution)/shard_map/all_to_all | solution.py:344
  133.0 2.6 %shard_map.51 = f32[128,256]{1,0:T(8,128)} custom-call(s32[2]{0:T(128)S(1)} %pad_add_fusion.place, s32[32,32]{1,0:T(8,128)S(1)} %copy-done.8, f32[16,2,9,128]{3,2,1,0:T(8,128)S(1)} %bitcast.8), custom_call_target="tpu_custom_call" | custom-call | tf_op jit(solution)/shard_map/pallas_call | solution.py:267
  135.6 9.4 %all-to-all-done.7 = f32[16,2,8,128]{3,2,1,0:T(8,128)S(1)} async-done(((f32[16,2,8,128]{3,2,1,0:T(8,128)}), f32[16,2,8,128]{3,2,1,0:T(8,128)S(1)}, u32[]{:S(2)}, u32[]{:S(2)}) %all-to-all-start.7) | async-done | bytes 131104 | tf_op jit(solution)/shard_map/all_to_all | solution.py:344
  145.0 0.0 copy-done
  145.0 0.0 copy-done.7
  145.0 26.2 %conditional.1 = (f32[128,256]{1,0:T(8,128)}) conditional(s32[]{:T(128)} %clamp.3, (s32[2]{0:T(128)S(1)}, s32[32,32]{1,0:T(8,128)S(1)}, f32[16,2,8,128]{3,2,1,0:T(8,128)S(1)}, bf16[4096,256]{1,0:T(8,128)(2,1)S(1)}, bf16[4096,256]{1,0:T(8,128)(2,1)}, /*index=5*/f32[128,256]{1,0:T(8,128)S(1)}) %tuple.46, ...), branch_computations={%region_2.0_spmd, %region_3.0_spmd, %region_4.0_spmd, %region_5.0_... | conditional | bytes 12582948 | solution.py:361
  145.0 0.0 copy-start.2
  145.0 1.4 branch_1_fun.2
  146.4 22.1 %all_to_all.37.two_row = f32[16,24,8,128]{3,2,1,0:T(8,128)S(1)} all-to-all(f32[16,24,8,128]{3,2,1,0:T(8,128)S(1)} %branch_1_fun.2), channel_id=1, replica_groups=mesh['row'=32,'col'=16] {'col'}, dimensions={0} | all-to-all | bytes 3145728 | tf_op jit(solution)/shard_map/cond/branch_1_fun/all_to_all | solution.py:244
  168.5 0.0 copy-done.2
  168.5 2.7 %branch_1_fun.3 = f32[128,256]{1,0:T(8,128)} custom-call(s32[2]{0:T(128)S(1)} %get-tuple-element.59.place, s32[32,32]{1,0:T(8,128)S(1)} %get-tuple-element.60.pattern, f32[16,24,8,128]{3,2,1,0:T(8,128)S(1)} %all_to_all.37.two_row, bf16[4096,256]{1,0:T(8,128)(2,1)S(1)} %get-tuple-element.62.high, bf16[4096,256]{1,0:T(8,128)(2,1)S(1)} %copy-done.2, ...), custom_call_target="tpu_custom_call" | custom-call | tf_op jit(solution)/shard_map/cond/branch_1_fun/pallas_call | solution.py:267
  (3 shorter events, 0.0 us)
Async XLA Ops:
  7.2 82.5 %all-gather.3.cloned.1.call-start = ((), (), s32[]{:S(2)}) async-start(), calls=%async_computation.8 | async-start | bytes 4325376 | tf_op jit(solution)/shard_map/all_gather | solution.py:283
  7.9 0.7 copy-start.5
  11.0 43.9 %copy-start.8 = (s32[32,32]{1,0:T(8,128)S(1)}, s32[32,32]{1,0:T(8,128)}, u32[]{:S(2)}) copy-start(s32[32,32]{1,0:T(8,128)} %pattern.7) | copy-start | bytes 12292
  11.0 43.9 %all-to-all-start.4 = ((f32[16,128,256]{2,1,0:T(8,128)}), f32[16,128,256]{2,1,0:T(8,128)S(1)}, u32[]{:S(2)}, u32[]{:S(2)}) async-start(f32[16,128,256]{2,1,0:T(8,128)} %get-tuple-element.92), calls=%async_computation.4 | async-start | bytes 4194304 | tf_op jit(solution)/shard_map/all_to_all | solution.py:244
  18.6 5.7 %collective-permute-start = (f32[9,128]{1,0:T(8,128)S(1)}, f32[9,128]{1,0:T(8,128)S(1)}, u32[]{:S(2)}, u32[]{:S(2)}) collective-permute-start(f32[9,128]{1,0:T(8,128)S(1)} %get-tuple-element.91), channel_id=1, source_target_pairs={{0,16},{16,0},{32,48},{48,32},{64,80},{80,64},{96,112},{112,96},{1... | collective-permute-start | bytes 13832 | tf_op jit(solution)/shard_map/ppermute | solution.py:292
  67.5 27.6 %all-to-all-start.5 = ((f32[16,128,256]{2,1,0:T(8,128)}), f32[16,128,256]{2,1,0:T(8,128)S(1)}, u32[]{:S(2)}, u32[]{:S(2)}) async-start(f32[16,128,256]{2,1,0:T(8,128)} %shard_map.52), calls=%async_computation.5 | async-start | bytes 4194304 | tf_op jit(solution)/shard_map/all_to_all | solution.py:244
  95.1 1.3 copy-start.6
  96.4 48.6 %copy-start = (bf16[4096,256]{1,0:T(8,128)(2,1)S(1)}, bf16[4096,256]{1,0:T(8,128)(2,1)}, u32[]{:S(2)}) copy-start(bf16[4096,256]{1,0:T(8,128)(2,1)} %get-tuple-element.96.high) | copy-start | bytes 6291460
  96.4 48.6 %copy-start.7 = (f32[128,256]{1,0:T(8,128)S(1)}, f32[128,256]{1,0:T(8,128)}, u32[]{:S(2)}) copy-start(f32[128,256]{1,0:T(8,128)} %value.1) | copy-start | bytes 393220
  100.8 9.5 %collective-permute-start.1 = (f32[16,8,128]{2,1,0:T(8,128)S(1)}, f32[16,8,128]{2,1,0:T(8,128)S(1)}, u32[]{:S(2)}, u32[]{:S(2)}) collective-permute-start(f32[16,8,128]{2,1,0:T(8,128)S(1)} %get-tuple-element.99), channel_id=1, source_target_pairs={{0,16},{16,0},{32,48},{48,32},{64,80},{80,64},{96,112},{112,96},{1... | collective-permute-start | bytes 196616 | tf_op jit(solution)/shard_map/ppermute | solution.py:341
  122.5 22.5 %all-to-all-start.7 = ((f32[16,2,8,128]{3,2,1,0:T(8,128)}), f32[16,2,8,128]{3,2,1,0:T(8,128)S(1)}, u32[]{:S(2)}, u32[]{:S(2)}) async-start(f32[16,2,8,128]{3,2,1,0:T(8,128)} %all_to_all.40), calls=%async_computation.7 | async-start | bytes 262144 | tf_op jit(solution)/shard_map/all_to_all | solution.py:344
  145.0 23.5 %copy-start.2 = (bf16[4096,256]{1,0:T(8,128)(2,1)S(1)}, bf16[4096,256]{1,0:T(8,128)(2,1)}, u32[]{:S(2)}) copy-start(bf16[4096,256]{1,0:T(8,128)(2,1)} %get-tuple-element.63.low) | copy-start | bytes 6291460 | tf_op jit(solution)/shard_map/cond
Sparse Core Ops, SparseCore 0:
  10.1 79.5 all-gather.2
